TPU v7x, 32 devices: a whole 2x2x4 slice. The times are simulated.
32 devices in a mesh: groups: 2 (over y), ctx: 4 (over z), tp: 2 (over x), fsdp: 2 (over core).
Axes of the slice: x: 2, y: 2, z: 4, core: 2. Of those that a mesh axis runs over, the one named last changes fastest.
Arguments:
- x_in: bfloat16 [3072, 16384], P(('groups', 'ctx'), ('tp', 'fsdp')), parts along dimension 0, may hold values from -6 to 6
- bc_in: bfloat16 [3072, 8, 512], P(('groups', 'ctx'), ('tp', 'fsdp')), parts along dimension 0, may hold values from -4 to 4
- z_in: bfloat16 [3072, 16384], P(('groups', 'ctx'), ('tp', 'fsdp')), parts along dimension 0, may hold values from -6 to 6
- dt_in: bfloat16 [3072, 256], P(('groups', 'ctx'), ('tp', 'fsdp')), parts along dimension 0, may hold values from -6 to 6
- conv_x: float32 [4, 16384], P(None, ('tp', 'fsdp')), may hold values from -3 to 3
- conv_bc: float32 [4, 8, 512], P(None, ('tp', 'fsdp')), may hold values from -3 to 3
- dt_bias: float32 [256], P(('tp', 'fsdp')), may hold values from -0.3 to 0.3
- a_log: float32 [256], P(('tp', 'fsdp')), as said below
- d_skip: float32 [256], P(('tp', 'fsdp')), may hold values from 0.5 to 2
- norm_gain: float32 [16384], P(('tp', 'fsdp')), may hold values from 0.5 to 1.5
Outputs:
- mixed: bfloat16 [3072, 16384], P(('groups', 'ctx'), ('tp', 'fsdp')), parts along dimension 0
There are 2 independent parts, one for each index of `groups`. A program takes and returns all parts, laid end to end along the dimension named above; an argument that names none is the same for every part. Nothing has to cross between parts.
Inputs may be any that keep to these rules, and one draw needn't show every extreme that they name: a_log lies between log(1.6 / 1536) and -2.8.
All inputs are finite; a program needn't handle non-finite values.
Results may differ from a plain program's by a relative error of at most 0.0062.
Values may be sent and summed in bfloat16 or wider, within the bound.
No kernel may reach another device: no remote copies, remote signals or barrier semaphores. Data moves between devices by JAX's collectives and lax.ppermute only.
A program may use at most 128 MiB of HBM per device.

v0:
```python
import math

import jax
import jax.numpy as jnp
from jax import lax
from jax.sharding import PartitionSpec as P

HEADS = 256
HEAD_DIM = 64
STATE = 256
GROUPS = 8
KERNEL = 4


def from_behind(block, axis, distance):
    devices = range(lax.axis_size(axis))
    route = [(i - distance, i) for i in devices if i - distance in devices]
    return lax.ppermute(block, axis, route)


def causal_conv(current, earlier, kernel_taps):
    length = current.shape[0]
    joined = jnp.concatenate([earlier, current], axis=0)
    summed = jnp.zeros(current.shape, jnp.float32)
    for offset in range(kernel_taps.shape[0]):
        summed = summed + kernel_taps[offset] * joined[offset : offset + length]
    return jax.nn.silu(summed).astype(jnp.bfloat16)


def span_terms(inputs_x, b_rows, c_rows, steps_dt, rates, skip_gain):
    length, heads, width = inputs_x.shape
    groups = b_rows.shape[1]
    per_group = heads // groups
    block = math.gcd(per_group, 8)
    cumulative = jnp.cumsum(-rates * steps_dt, axis=0)
    scores = jnp.einsum("tgn,sgn->gts", c_rows, b_rows, preferred_element_type=jnp.float32)
    causal = lax.broadcasted_iota(jnp.int32, (length, length), 0) >= lax.broadcasted_iota(
        jnp.int32, (length, length), 1
    )

    def diagonal_block(start):
        grid = lax.dynamic_index_in_dim(scores, start // per_group, 0, keepdims=False)
        cum_block = lax.dynamic_slice_in_dim(cumulative, start, block, 1).T
        dt_block = lax.dynamic_slice_in_dim(steps_dt, start, block, 1).T
        x_block = lax.dynamic_slice_in_dim(inputs_x, start, block, 1)
        spread = cum_block[:, :, None] - cum_block[:, None, :]
        decay = jnp.where(causal, jnp.exp(jnp.minimum(spread, 0.0)), 0.0)
        mixing = (grid[None] * decay * dt_block[:, None, :]).astype(jnp.bfloat16)
        return jnp.einsum("hts,shp->thp", mixing, x_block, preferred_element_type=jnp.float32)

    starts = jnp.arange(0, heads, block, dtype=jnp.int32)
    blocks = lax.map(diagonal_block, starts)
    diag_part = jnp.moveaxis(blocks, 0, 1).reshape(length, heads, width)
    final_log = cumulative[-1]
    to_end = jnp.exp(final_log[None, :] - cumulative) * steps_dt
    weighted = (
        (inputs_x * to_end[:, :, None])
        .astype(jnp.bfloat16)
        .reshape(length, groups, per_group, width)
    )
    state = jnp.einsum("sghp,sgn->ghpn", weighted, b_rows, preferred_element_type=jnp.float32)
    state = state.reshape(heads, width, b_rows.shape[2])
    local_out = diag_part + skip_gain[None, :, None] * inputs_x
    return (local_out, state, final_log, cumulative)


def carried_term(c_rows, cumulative, incoming):
    length, groups, depth = c_rows.shape
    heads = incoming.shape[0]
    width = incoming.shape[1]
    rounded = incoming.astype(jnp.bfloat16).reshape(groups, heads // groups, width, depth)
    term = jnp.einsum(
        "tgn,ghpn->tghp", c_rows, rounded, preferred_element_type=jnp.float32
    ).reshape(length, heads, width)
    return term * jnp.exp(cumulative)[:, :, None]


def gated_norm(ssm_out, gate_in, gain_row, groups):
    length = ssm_out.shape[0]
    gated = ssm_out.astype(jnp.float32) * jax.nn.silu(gate_in.astype(jnp.float32))
    shaped = gated.reshape(length, groups, -1)
    scale = lax.rsqrt(jnp.mean(shaped * shaped, axis=-1, keepdims=True) + 1e-05)
    return ((shaped * scale).reshape(length, -1) * gain_row).astype(jnp.bfloat16)


def join_states(early, late):
    return (early[0] * late[0], late[0][..., None, None] * early[1] + late[1])


def shards(x_in, bc_in, z_in, dt_in, conv_x, conv_bc, dt_bias, a_log, d_skip, norm_gain):
    margin = KERNEL - 1
    earlier_x, earlier_bc = from_behind((x_in[-margin:], bc_in[-margin:]), "ctx", 1)
    conv_out = causal_conv(x_in, earlier_x, conv_x)
    bc_out = causal_conv(bc_in, earlier_bc, conv_bc)
    length = x_in.shape[0]
    heads = x_in.shape[1] // HEAD_DIM
    rates = jnp.exp(a_log)
    contexts = lax.axis_size("ctx")
    owned = heads // contexts
    first_head = lax.axis_index("ctx") * owned
    moved_x, moved_dt = (
        lax.all_to_all(conv_out, "ctx", split_axis=1, concat_axis=0, tiled=True),
        lax.all_to_all(dt_in, "ctx", split_axis=1, concat_axis=0, tiled=True),
    )
    every_bc = lax.all_gather(bc_out, "ctx", axis=0, tiled=True)
    group_now = first_head // (HEADS // GROUPS)
    own_bc = lax.dynamic_index_in_dim(every_bc, group_now, 1, keepdims=True)
    steps_dt = jax.nn.softplus(
        moved_dt.astype(jnp.float32) + lax.dynamic_slice_in_dim(dt_bias, first_head, owned)
    )
    own_rates = lax.dynamic_slice_in_dim(rates, first_head, owned)
    own_skip = lax.dynamic_slice_in_dim(d_skip, first_head, owned)
    batch = math.gcd(contexts, 8)
    outer = contexts // batch
    span_x = moved_x.reshape(outer, batch, length, owned, HEAD_DIM)
    span_b = own_bc[:, :, :STATE].reshape(outer, batch, length, 1, STATE)
    span_c = own_bc[:, :, STATE:].reshape(outer, batch, length, 1, STATE)
    span_dt = steps_dt.reshape(outer, batch, length, owned)

    def one_span(inputs_x, b_rows, c_rows, dt_rows):
        return span_terms(inputs_x, b_rows, c_rows, dt_rows, own_rates, own_skip)

    def span_batch(pieces):
        return jax.vmap(one_span)(pieces[0], pieces[1], pieces[2], pieces[3])

    local_out, states, final_log, cumulative = lax.map(
        span_batch, (span_x, span_b, span_c, span_dt)
    )
    local_out = local_out.reshape(contexts, length, owned, HEAD_DIM)
    states = states.reshape(contexts, owned, HEAD_DIM, STATE)
    final_log = final_log.reshape(contexts, owned)
    cumulative = cumulative.reshape(contexts, length, owned)
    running_decay, running_state = lax.associative_scan(join_states, (jnp.exp(final_log), states))
    incoming = jnp.concatenate([jnp.zeros_like(states[:1]), running_state[:-1]], axis=0)
    carried = jax.vmap(carried_term)(
        span_c.reshape(contexts, length, 1, STATE), cumulative, incoming
    )
    ssm_part = (
        (local_out + carried).astype(jnp.bfloat16).reshape(contexts * length, owned * HEAD_DIM)
    )
    ssm_out = lax.all_to_all(ssm_part, "ctx", split_axis=0, concat_axis=1, tiled=True)
    return gated_norm(ssm_out, z_in, norm_gain, bc_in.shape[1])


def solution(mesh):
    placed = (
        P(("groups", "ctx"), ("tp", "fsdp")),
        P(("groups", "ctx"), ("tp", "fsdp"), None),
        P(("groups", "ctx"), ("tp", "fsdp")),
        P(("groups", "ctx"), ("tp", "fsdp")),
        P(None, ("tp", "fsdp")),
        P(None, ("tp", "fsdp"), None),
        P(("tp", "fsdp")),
        P(("tp", "fsdp")),
        P(("tp", "fsdp")),
        P(("tp", "fsdp")),
    )
    return jax.shard_map(
        shards,
        mesh=mesh,
        in_specs=placed,
        out_specs=P(("groups", "ctx"), ("tp", "fsdp")),
        check_vma=False,
    )
```

profile of v0, /device:TPU:28, one launch (start us, length us, event | category | flops | bytes accessed | tf_op | source)
XLA Modules:
  0.0 350.6 jit_solution(12222126531260875397)
XLA Ops:
  7.8 1.3 collective-permute-start.1
  9.1 6.3 %all-to-all-start.1 = ((bf16[384,4,16]{0,2,1:T(8,128)(2,1)}), bf16[384,4,16]{0,2,1:T(8,128)(2,1)S(1)}, u32[]{:S(2)}, u32[]{:S(2)}) async-start(bf16[384,4,16]{0,2,1:T(8,128)(2,1)} %bitcast.177), calls=%async_computation.1 | async-start | bytes 98304 | tf_op jit(solution)/shard_map/all_to_all | solution.py:103
  19.3 1.9 multiply_convert_fusion.8
  22.0 10.0 %multiply_convert_fusion.6 = bf16[384,4096]{1,0:T(8,128)(2,1)S(1)} fusion(bf16[384,4096]{1,0:T(8,128)(2,1)} %param.12, bf16[3,4096]{1,0:T(4,128)(2,1)S(1)} %collective-permute-done, f32[4096]{0:T(1024)S(1)} %bitcast.175, f32[4096]{0:T(1024)S(1)} %bitcast.176, f32[4096]{0:T(1024)S(1)} %bitcast.174, f32[4096]{0:T(1024)S(1)} %bitcast.173), kind=kLoop, calls=%fused_computation.25 | loop fusion | flops 39321600 | bytes 6381568 | tf_op jit(solution)/shard_map/convert_element_type | solution.py:27
  32.1 2.8 copy.35
  34.9 5.7 %all-to-all-start = ((bf16[384,4,1024]{0,2,1:T(8,128)(2,1)}), bf16[384,4,1024]{0,2,1:T(8,128)(2,1)S(1)}, u32[]{:S(2)}, u32[]{:S(2)}) async-start(bf16[384,4,1024]{0,2,1:T(8,128)(2,1)} %bitcast.165), calls=%async_computation | async-start | bytes 6291456 | tf_op jit(solution)/shard_map/all_to_all | solution.py:102
  41.7 3.4 reduce-window.6
  46.8 1.5 fusion.35
  48.3 91.1 %all-gather.2.cloned.1.call-done = bf16[1536,2,512]{2,0,1:T(8,128)(2,1)} async-done(((bf16[384,2,512]{2,0,1:T(8,128)(2,1)}), bf16[1536,2,512]{2,0,1:T(8,128)(2,1)}) %all-gather.2.cloned.1.call-update) | async-done | bytes 3145744 | tf_op jit(solution)/shard_map/all_gather | solution.py:105
  139.4 1.5 constant_dynamic-slice_fusion.1
  142.0 2.0 convolution_bitcast_fusion
  144.0 7.2 %all-to-all-done = bf16[384,4,1024]{0,2,1:T(8,128)(2,1)S(1)} async-done(((bf16[384,4,1024]{0,2,1:T(8,128)(2,1)}), bf16[384,4,1024]{0,2,1:T(8,128)(2,1)S(1)}, u32[]{:S(2)}, u32[]{:S(2)}) %all-to-all-start) | async-done | bytes 3145760 | tf_op jit(solution)/shard_map/all_to_all | solution.py:102
  151.2 3.0 fusion.15
  156.3 1.5 pad_add_fusion
  157.8 18.5 %pad.96 = f32[4,16,64,256]{3,2,1,0:T(8,128)} pad(f32[2,16,64,256]{3,2,1,0:T(8,128)} %pad_add_fusion, f32[]{:T(128)} %constant.128.clone.1), padding=1_0_1x0_0_0x0_0_0x0_0_0 | pad | bytes 6291460
  176.3 1.8 fusion.37
  178.1 1.6 pad_maximum_fusion.1
  179.7 13.8 %pad.45 = f32[3,16,64,256]{3,2,1,0:T(8,128)S(1)} pad(f32[2,16,64,256]{3,2,1,0:T(8,128)} %pad_maximum_fusion.1, f32[]{:T(128)} %constant.128.clone.1), padding=0_0_1x0_0_0x0_0_0x0_0_0 | pad | bytes 5242884 | tf_op jit(solution)/shard_map/slice | solution.py:134
  193.6 28.1 %while.26 = (s32[]{:T(128)}, f32[2,4,384,8,64]{2,4,3,0,1:T(8,128)}, s32[2]{0:T(128)S(1)}, bf16[4,384,16,64]{1,3,2,0:T(8,128)(2,1)}, f32[4,1,384,384]{3,2,0,1:T(8...) while((s32[]{:T(128)}, f32[2,4,384,8,64]{2,4,3,0,1:T(8,128)}, ...), condition=%wide.region_3.4_spmd.clone, body=%wide.region_2.3_spmd.clone.sunk | while | flops 632438784 | bytes 7718099 | solution.py:52
  198.2 9.4 %bitcast_dynamic-update-slice_fusion.2 = f32[2,4,384,8,64]{2,4,3,0,1:T(8,128)} fusion(f32[2,4,384,8,64]{2,4,3,0,1:T(8,128)} %get-tuple-element.282, s32[]{:T(128)} %get-tuple-element.281, f32[4,8,384]{2,1,0:T(8,128)S(1)} %get-tuple-element.268, f32[4,8,384]{2,1,0:T(8,128)S(1)} %get-tuple-element.269, f32[4,384,384]{2,1,0:T(8,128)} %bitcast.172, ...), kind=kOutput, calls=%fused_computation.4.clone.1 | convolution fusion | flops 632291328 | bytes 7373824 | tf_op jit(solution)/shard_map/while/body/eval_jaxpr/vmap()/while/body/eval_jaxpr/hts,shp->thp/dot_general | solution.py:49
  212.3 9.4 %bitcast_dynamic-update-slice_fusion.2 = f32[2,4,384,8,64]{2,4,3,0,1:T(8,128)} fusion(f32[2,4,384,8,64]{2,4,3,0,1:T(8,128)} %get-tuple-element.282, s32[]{:T(128)} %get-tuple-element.281, f32[4,8,384]{2,1,0:T(8,128)S(1)} %get-tuple-element.268, f32[4,8,384]{2,1,0:T(8,128)S(1)} %get-tuple-element.269, f32[4,384,384]{2,1,0:T(8,128)} %bitcast.172, ...), kind=kOutput, calls=%fused_computation.4.clone.1 | convolution fusion | flops 632291328 | bytes 7373824 | tf_op jit(solution)/shard_map/while/body/eval_jaxpr/vmap()/while/body/eval_jaxpr/hts,shp->thp/dot_general | solution.py:49
  221.7 3.5 fusion.17
  226.7 2.8 fusion.12
  229.5 73.9 %all_to_all.39 = bf16[4,384,1024]{1,2,0:T(8,128)(2,1)S(1)} all-to-all(bf16[4,384,1024]{1,2,0:T(8,128)(2,1)S(1)} %fusion.12), channel_id=1, replica_groups=mesh['groups'=2,'ctx'=4,'tp'=2,'fsdp'=2] {'ctx'}, dimensions={0} | all-to-all | bytes 6291456 | tf_op jit(solution)/shard_map/all_to_all | solution.py:141
  303.3 3.0 convert_element_type.101
  306.4 6.7 %copy.44 = f32[384,4096]{1,0:T(8,128)} copy(f32[384,4096]{0,1:T(8,128)} %bitcast.162) | data formatting | bytes 12582912 | tf_op jit(solution)/shard_map/convert_element_type | solution.py:80
  313.1 5.4 %fusion.36 = f32[384,4096]{1,0:T(8,128)} fusion(f32[384,4096]{1,0:T(8,128)} %copy.44, bf16[384,4096]{1,0:T(8,128)(2,1)S(1)} %copy-done.3), kind=kLoop, calls=%fused_computation.87 | loop fusion | flops 11010048 | bytes 15728640 | tf_op jit(solution)/shard_map/mul | solution.py:82
  318.4 9.1 %mul.303 = f32[384,2,2048]{2,1,0:T(2,128)} reshape(f32[384,4096]{1,0:T(8,128)} %fusion.36) | data formatting | bytes 12582912 | tf_op jit(solution)/shard_map/mul | solution.py:82
  327.6 4.5 %reduce_sum.9 = f32[384,2]{1,0:T(8,128)S(1)} reduce(f32[384,2,2048]{2,1,0:T(2,128)} %mul.303, f32[]{:T(128)} %constant.128.clone.1), dimensions={2}, to_apply=%region_4.5 | reduce | flops 1572096 | bytes 6294532 | tf_op jit(solution)/shard_map/reduce_sum | solution.py:82
  332.1 1.7 mul.304
  333.8 6.0 %copy.60 = f32[48,8,2,2048]{3,1,2,0:T(8,128)S(1)} copy(f32[48,8,2,2048]{3,2,1,0:T(2,128)S(1)} %bitcast.163) | data formatting | bytes 12582912
  339.9 3.8 %multiply_convert_fusion.4 = bf16[384,4096]{1,0:T(8,128)(2,1)} fusion(f32[384,4096]{1,0:T(8,128)S(1)} %bitcast.164, f32[4096]{0:T(1024)S(1)} %copy-done.8, f32[384,4096]{1,0:T(8,128)S(1)} %bitcast.158, bf16[384,4096]{1,0:T(8,128)(2,1)S(1)} %copy-done.3), kind=kLoop, calls=%fused_computation.23 | loop fusion | flops 14155776 | bytes 18890752 | tf_op jit(solution)/shard_map/convert_element_type | solution.py:83
  (96 shorter events, 18.7 us)
Async XLA Ops:
  7.8 11.6 %collective-permute-start.1 = (bf16[3,2,512]{2,0,1:T(4,128)(2,1)S(1)}, bf16[3,2,512]{2,0,1:T(4,128)(2,1)S(1)}, u32[]{:S(2)}, u32[]{:S(2)}) collective-permute-start(bf16[3,2,512]{2,0,1:T(4,128)(2,1)S(1)} %slice.193), channel_id=1, source_target_pairs={{0,4},{4,8},{8,12},{1,5},{5,9},{9,13},{2,6},{6,10},{10,14},{3,7},{... | collective-permute-start | bytes 18440 | tf_op jit(solution)/shard_map/ppermute | solution.py:18
  9.1 25.8 %all-to-all-start.1 = ((bf16[384,4,16]{0,2,1:T(8,128)(2,1)}), bf16[384,4,16]{0,2,1:T(8,128)(2,1)S(1)}, u32[]{:S(2)}, u32[]{:S(2)}) async-start(bf16[384,4,16]{0,2,1:T(8,128)(2,1)} %bitcast.177), calls=%async_computation.1 | async-start | bytes 98304 | tf_op jit(solution)/shard_map/all_to_all | solution.py:103
  15.3 124.1 %all-gather.2.cloned.1.call-start = ((), (), s32[]{:S(2)}) async-start(), calls=%async_computation.3 | async-start | bytes 3932160 | tf_op jit(solution)/shard_map/all_gather | solution.py:105
  16.2 5.8 %collective-permute-start = (bf16[3,4096]{1,0:T(4,128)(2,1)S(1)}, bf16[3,4096]{1,0:T(4,128)(2,1)S(1)}, u32[]{:S(2)}, u32[]{:S(2)}) collective-permute-start(bf16[3,4096]{1,0:T(4,128)(2,1)S(1)} %slice.109), channel_id=1, source_target_pairs={{0,4},{4,8},{8,12},{1,5},{5,9},{9,13},{2,6},{6,10},{10,14},{3,7},{... | collective-permute-start | bytes 73736 | tf_op jit(solution)/shard_map/ppermute | solution.py:18
  34.8 5.7 %copy-start.14 = (f32[64]{0:T(128)S(1)}, f32[64]{0:T(128)}, u32[]{:S(2)}) copy-start(f32[64]{0:T(128)} %param.19) | copy-start | bytes 772
  34.9 5.7 %copy-start.15 = (f32[64]{0:T(128)S(1)}, f32[64]{0:T(128)}, u32[]{:S(2)}) copy-start(f32[64]{0:T(128)} %param.18) | copy-start | bytes 772
  34.9 5.8 %copy-start.16 = (f32[64]{0:T(128)S(1)}, f32[64]{0:T(128)}, u32[]{:S(2)}) copy-start(f32[64]{0:T(128)} %param.20) | copy-start | bytes 772
  34.9 6.7 %copy-start.6 = (bf16[384,4,16]{0,2,1:T(8,128)(2,1)}, bf16[384,4,16]{0,2,1:T(8,128)(2,1)S(1)}, u32[]{:S(2)}) copy-start(bf16[384,4,16]{0,2,1:T(8,128)(2,1)S(1)} %all-to-all-done.1) | copy-start | bytes 147460
  34.9 116.4 %all-to-all-start = ((bf16[384,4,1024]{0,2,1:T(8,128)(2,1)}), bf16[384,4,1024]{0,2,1:T(8,128)(2,1)S(1)}, u32[]{:S(2)}, u32[]{:S(2)}) async-start(bf16[384,4,1024]{0,2,1:T(8,128)(2,1)} %bitcast.165), calls=%async_computation | async-start | bytes 6291456 | tf_op jit(solution)/shard_map/all_to_all | solution.py:102
  40.7 0.8 copy-start.11
  45.6 0.6 copy-start.9
  140.9 0.9 copy-start.4
  140.9 1.1 copy-start.5
  151.2 3.0 copy-start
  151.2 3.0 copy-start.10
  154.2 2.0 copy-start.2
  154.2 0.7 copy-start.13
  157.8 18.5 %copy-start.12 = (f32[16]{0:T(128)S(1)}, f32[16]{0:T(128)}, u32[]{:S(2)}) copy-start(f32[16]{0:T(128)} %slice_bitcast_fusion.5) | copy-start | bytes 196
  178.1 15.4 %copy-start.17 = (s32[2]{0:T(128)S(1)}, s32[2]{0:T(128)}, u32[]{:S(2)}) copy-start(s32[2]{0:T(128)} %iota_multiply_fusion) | copy-start | bytes 28
  221.7 3.5 %slice-start.2 = ((s8[6291456]{0:T(1024)(128)(4,1)}), s8[4194304]{0:T(1024)(128)(4,1)S(1)}, s32[]{:S(2)}) async-start(s8[6291456]{0:T(1024)(128)(4,1)} %bitcast.170), calls=%async_computation.6 | async-start | bytes 8388608
  221.7 4.3 %copy-start.1 = (bf16[4,384,16,64]{1,3,2,0:T(8,128)(2,1)S(1)}, bf16[4,384,16,64]{1,3,2,0:T(8,128)(2,1)}, u32[]{:S(2)}) copy-start(bf16[4,384,16,64]{1,3,2,0:T(8,128)(2,1)} %get-tuple-element.305) | copy-start | bytes 9437188
  221.7 4.9 %slice-start.3 = ((s8[6291456]{0:T(1024)(128)(4,1)}), s8[2097152]{0:T(1024)(128)(4,1)S(1)}, s32[]{:S(2)}) async-start(s8[6291456]{0:T(1024)(128)(4,1)} %bitcast.170), calls=%async_computation.7 | async-start | bytes 4194304
  221.7 4.9 %copy-start.7 = (f32[4,384,16]{1,2,0:T(8,128)S(1)}, f32[4,384,16]{1,2,0:T(8,128)}, u32[]{:S(2)}) copy-start(f32[4,384,16]{1,2,0:T(8,128)} %get-tuple-element.212) | copy-start | bytes 294916
  306.4 6.7 %copy-start.3 = (bf16[384,4096]{1,0:T(8,128)(2,1)S(1)}, bf16[384,4096]{1,0:T(8,128)(2,1)}, u32[]{:S(2)}) copy-start(bf16[384,4096]{1,0:T(8,128)(2,1)} %param.14) | copy-start | bytes 9437188
  333.8 6.1 %slice-start = ((s8[6291456]{0:T(1024)(128)(4,1)}), s8[4194304]{0:T(1024)(128)(4,1)S(1)}, s32[]{:S(2)}) async-start(s8[6291456]{0:T(1024)(128)(4,1)} %bitcast.157), calls=%async_computation.4 | async-start | bytes 8388608
  333.8 6.1 %slice-start.1 = ((s8[6291456]{0:T(1024)(128)(4,1)}), s8[2097152]{0:T(1024)(128)(4,1)S(1)}, s32[]{:S(2)}) async-start(s8[6291456]{0:T(1024)(128)(4,1)} %bitcast.157), calls=%async_computation.5 | async-start | bytes 4194304
  333.8 6.1 %copy-start.8 = (f32[4096]{0:T(1024)S(1)}, f32[4096]{0:T(1024)}, u32[]{:S(2)}) copy-start(f32[4096]{0:T(1024)} %param.21) | copy-start | bytes 49156
Sparse Core Ops, SparseCore 0:
  21.4 118.0 all-gather.1
where the time goes:
time: 357 us; the launch traced here: 351 us
  waiting for transfers between devices  99.1 us (28%)
  local copies, waits for them, and re-layouts  75.1 us (21%)
  blocking collectives  73.9 us (21%)
  other arithmetic  43.1 us (12%)
  matrix products  27.3 us (8%)
  starting transfers between devices  14.6 us (4%)
  between operations  13.7 us (4%)
  loops' own time  3.85 us (1%)
    all_gather x1, waiting for transfers between devices, shards(): every_bc = lax.all_gather(bc_out, 'ctx', axis=0, tiled=True)  91.1 us
    all_to_all x1, blocking collectives, shards(): lax.all_to_all(ssm_part, 'ctx', split_axis=0, concat_axis=1, tiled=True)  73.9 us
    unnamed x47, local copies, waits for them, and re-layouts  29.9 us
    dot_general x2, matrix products, diagonal_block(): jnp.einsum('hts,shp->thp', mixing, x_block, preferred_element_type=jnp.fl...  18.9 us
    slice x1, local copies, waits for them, and re-layouts, shards(): running_state[:-1]  13.8 us
    convert_element_type x2, other arithmetic, causal_conv(): return jax.nn.silu(summed).astype(jnp.bfloat16)  12 us
    mul x1, local copies, waits for them, and re-layouts, gated_norm(): scale = lax.rsqrt(jnp.mean(shaped * shaped, axis=-1, keepdims=True) + 1e-05)  9.14 us
    all_to_all x1, waiting for transfers between devices, shards(): lax.all_to_all(conv_out, 'ctx', split_axis=1, concat_axis=0, tiled=True)  7.24 us
  transfers between devices with their start and end apart: 5, of which 3 were waited for; matrix products, arithmetic and copies ran while one was open for 8% of the time, Pallas kernels for 0%

commit v1 on v0

v1 whole, which is shorter than its diff:
```python
import functools

import jax
import jax.numpy as jnp
from jax import lax
from jax.experimental import pallas as pl
from jax.experimental.pallas import tpu as pltpu
from jax.sharding import PartitionSpec as P

HEAD_DIM = 64
STATE = 256
KERNEL = 4
SUB = 128
CHUNK = 512
F32 = jnp.float32
BF16 = jnp.bfloat16


def dot(left, right):
    return jnp.dot(left, right, preferred_element_type=F32)


def silu(value):
    half = 0.5 * value
    return half + half * jnp.tanh(half)


def two_terms(value):
    high = value.astype(BF16)
    low = (value - high.astype(F32)).astype(BF16)
    return high, low


def causal_conv(current, earlier, taps):
    length, width = current.shape
    wide = current.astype(F32)
    head = jnp.concatenate([jnp.zeros((8 - KERNEL + 1, width), F32), earlier.astype(F32)], axis=0)
    joined = jnp.concatenate([head, wide], axis=0)
    total = taps[KERNEL - 1 : KERNEL] * wide
    for back in range(1, KERNEL):
        row = KERNEL - 1 - back
        total = total + taps[row : row + 1] * joined[8 - back : 8 - back + length]
    return silu(total).astype(BF16)


def prepare_kernel(
    groups, bc_ref, early_ref, taps_ref, dt_ref, bias_ref, rate_ref, skip_ref,
    left_ref, bt_ref, u_ref, v_ref, rows_ref,
):
    length, heads = dt_ref.shape
    shifted = dt_ref[...].astype(F32) + bias_ref[...]
    steps = jnp.maximum(shifted, 0.0) + jnp.log1p(jnp.exp(-jnp.abs(shifted)))
    log_decay = -jnp.exp(rate_ref[...]) * steps
    at = lax.broadcasted_iota(jnp.int32, (length, length), 0)
    of = lax.broadcasted_iota(jnp.int32, (length, length), 1)
    lower = jnp.where(at >= of, 1.0, 0.0).astype(BF16)
    first = log_decay.astype(BF16)
    rest = log_decay - first.astype(F32)
    second = rest.astype(BF16)
    third = (rest - second.astype(F32)).astype(BF16)
    cumulative = dot(lower, first) + dot(lower, second) + dot(lower, third)
    subs = length // SUB
    decays, scales = [], []
    start = jnp.zeros((1, heads), F32)
    for sub in range(subs):
        rows = slice(sub * SUB, (sub + 1) * SUB)
        inside = cumulative[rows] - start
        for ref, value in ((u_ref, jnp.exp(inside)), (v_ref, jnp.exp(-inside) * steps[rows])):
            high, low = two_terms(value)
            ref[rows, :] = jnp.concatenate([high, low], axis=1)
        end = cumulative[(sub + 1) * SUB - 1 : (sub + 1) * SUB]
        decays.append(jnp.exp(end - start))
        scales.append(jnp.exp(start))
        start = end
    lines = decays + scales + [skip_ref[...], jnp.exp(start)]
    lines = lines + [jnp.zeros((1, heads), F32)] * (rows_ref.shape[0] - len(lines))
    high, low = two_terms(jnp.concatenate(lines, axis=0))
    rows_ref[...] = jnp.concatenate([high, low], axis=1)
    causal = at[:SUB, :SUB] >= of[:SUB, :SUB]
    for group in range(groups):
        lanes = slice(group * 2 * STATE, (group + 1) * 2 * STATE)
        conv = causal_conv(bc_ref[:, lanes], early_ref[:, lanes], taps_ref[:, lanes])
        b_turned = conv[:, :STATE].astype(F32).T.astype(BF16)
        c_rows = conv[:, STATE:]
        bt_ref[group] = b_turned
        for sub in range(subs):
            rows = slice(sub * SUB, (sub + 1) * SUB)
            scores = jnp.where(causal, dot(c_rows[rows], b_turned[:, rows]), 0.0)
            left_ref[group, rows, :SUB] = scores.astype(BF16)
            left_ref[group, rows, SUB:] = c_rows[rows]


def local_kernel(
    first_head, x_ref, early_ref, taps_ref, z_ref, left_ref, bt_ref, u_ref, v_ref, rows_ref,
    part_ref, reach_ref, state_ref, send_ref, lanes_ref,
):
    length, width = x_ref.shape
    terms = u_ref.shape[1]
    row = lax.broadcasted_iota(jnp.int32, (terms, width), 0)
    lane = lax.broadcasted_iota(jnp.int32, (terms, width), 1)
    heads = terms // 2
    owner = jnp.where(row >= heads, row - heads, row) - first_head
    spread = jnp.where(
        (lane >= owner * HEAD_DIM) & (lane < (owner + 1) * HEAD_DIM), 1.0, 0.0
    ).astype(BF16)
    lanes = dot(rows_ref[...], spread)
    lanes_ref[...] = lanes
    conv = causal_conv(x_ref[...], early_ref[...], taps_ref[...])
    subs = length // SUB
    skip = lanes[2 * subs : 2 * subs + 1]
    state = None
    for sub in range(subs):
        rows = slice(sub * SUB, (sub + 1) * SUB)
        inputs = conv[rows].astype(F32)
        scaled = (inputs * dot(v_ref[rows], spread)).astype(BF16)
        decay = lanes[sub : sub + 1]
        added = dot(bt_ref[0, :, rows], scaled)
        if sub == 0:
            inner = dot(left_ref[0, rows, :SUB], scaled)
            state = decay * added
        else:
            inner = dot(left_ref[0, rows, :SUB], scaled) + dot(
                left_ref[0, rows, SUB:], state.astype(BF16)
            )
            state = decay * (state + added)
        grown = dot(u_ref[rows], spread)
        gate = silu(z_ref[rows].astype(F32))
        part_ref[rows, :] = gate * (grown * inner + skip * inputs)
        reach_ref[rows, :] = gate * grown * lanes[subs + sub : subs + sub + 1]
    state_ref[...] = state
    send_ref[...] = state.astype(send_ref.dtype)


def finish_kernel(chunks, *refs):
    left_ref, gain_ref = refs[0], refs[1]
    parts = refs[2 : 2 + chunks]
    reaches = refs[2 + chunks : 2 + 2 * chunks]
    carried = refs[2 + 2 * chunks : 2 + 3 * chunks]
    latest = refs[2 + 3 * chunks : 2 + 4 * chunks]
    out_ref = refs[-1]
    c_rows = left_ref[0, :, SUB:]
    gated, square = [], None
    for index in range(chunks):
        incoming = (carried[index][...].astype(F32) + latest[index][...].astype(F32)).astype(BF16)
        value = parts[index][...] + reaches[index][...] * dot(c_rows, incoming)
        gated.append(value)
        term = jnp.sum(value * value, axis=1, keepdims=True)
        square = term if square is None else square + term
    width = gated[0].shape[1]
    scale = lax.rsqrt(square * (1.0 / (width * chunks)) + 1e-05)
    for index in range(chunks):
        lanes = slice(index * width, (index + 1) * width)
        out_ref[:, lanes] = (gated[index] * scale * gain_ref[:, lanes]).astype(BF16)


def whole(shape):
    return pl.BlockSpec(shape, lambda *_: (0,) * len(shape))


def shards(x_in, bc_in, z_in, dt_in, conv_x, conv_bc, dt_bias, a_log, d_skip, norm_gain):
    length, channels = x_in.shape
    groups = bc_in.shape[1]
    heads = channels // HEAD_DIM
    contexts = lax.axis_size("ctx")
    wire = BF16 if contexts <= 8 else F32
    margin = KERNEL - 1
    subs = length // SUB
    ahead = [(i, i + 1) for i in range(contexts - 1)]
    bc_flat = bc_in.reshape(length, groups * 2 * STATE)
    early_x, early_bc = lax.ppermute((x_in[-margin:], bc_flat[-margin:]), "ctx", ahead)
    line_rows = -(-(2 * subs + 2) // 8) * 8
    sub_width = SUB + STATE
    left, b_turned, grow, shrink, lines = pl.pallas_call(
        functools.partial(prepare_kernel, groups),
        out_shape=(
            jax.ShapeDtypeStruct((groups, length, sub_width), BF16),
            jax.ShapeDtypeStruct((groups, STATE, length), BF16),
            jax.ShapeDtypeStruct((length, 2 * heads), BF16),
            jax.ShapeDtypeStruct((length, 2 * heads), BF16),
            jax.ShapeDtypeStruct((line_rows, 2 * heads), BF16),
        ),
        name="prepare",
    )(
        bc_flat, early_bc, conv_bc.reshape(KERNEL, groups * 2 * STATE), dt_in,
        dt_bias.reshape(1, heads), a_log.reshape(1, heads), d_skip.reshape(1, heads),
    )

    per_group = channels // groups
    in_group = per_group // CHUNK
    count = channels // CHUNK
    local = []
    for chunk in range(count):
        group = chunk // in_group

        def column(rows, chunk=chunk):
            return pl.BlockSpec((rows, CHUNK), lambda i: (0, chunk))

        def grouped(rows, width, group=group):
            return pl.BlockSpec((1, rows, width), lambda i: (group, 0, 0))

        local.append(
            pl.pallas_call(
                functools.partial(local_kernel, chunk * (CHUNK // HEAD_DIM)),
                grid=(1,),
                in_specs=[
                    column(length), column(margin), column(KERNEL), column(length),
                    grouped(length, sub_width), grouped(STATE, length),
                    whole((length, 2 * heads)), whole((length, 2 * heads)),
                    whole((line_rows, 2 * heads)),
                ],
                out_specs=[
                    whole((length, CHUNK)), whole((length, CHUNK)), whole((STATE, CHUNK)),
                    whole((STATE, CHUNK)), whole((line_rows, CHUNK)),
                ],
                out_shape=(
                    jax.ShapeDtypeStruct((length, CHUNK), F32),
                    jax.ShapeDtypeStruct((length, CHUNK), F32),
                    jax.ShapeDtypeStruct((STATE, CHUNK), F32),
                    jax.ShapeDtypeStruct((STATE, CHUNK), wire),
                    jax.ShapeDtypeStruct((line_rows, CHUNK), F32),
                ),
                compiler_params=pltpu.CompilerParams(vmem_limit_bytes=24 << 20),
                cost_estimate=pl.CostEstimate(
                    flops=2 * length * CHUNK * 800, bytes_accessed=4 << 20,
                    transcendentals=2 * length * CHUNK,
                ),
                name="local",
            )(x_in, early_x, conv_x, z_in, left, b_turned, grow, shrink, lines)
        )

    carried, latest = [], []
    for chunk in range(count):
        state, sent, lanes = local[chunk][2:]
        total = lanes[2 * subs + 1 : 2 * subs + 2]
        received = []
        for hop in range(contexts - 1):
            arrived = lax.ppermute(sent, "ctx", [(hop, hop + 1)])
            received.append(arrived)
            sent = (total * arrived.astype(F32) + state).astype(wire)
        before = received[0]
        for arrived in received[1:-1]:
            before = before + arrived
        carried.append(before)
        latest.append(received[-1] if contexts > 2 else jnp.zeros_like(before))

    rows = 128
    gain = norm_gain.reshape(1, channels)
    out = None
    for group in range(groups):
        picked = range(group * in_group, (group + 1) * in_group)
        tall = pl.BlockSpec((rows, CHUNK), lambda i: (i, 0))
        operands = [left, gain]
        operands += [local[c][0] for c in picked] + [local[c][1] for c in picked]
        operands += [carried[c] for c in picked] + [latest[c] for c in picked]
        specs = [
            pl.BlockSpec((1, rows, sub_width), lambda i, group=group: (group, i, 0)),
            pl.BlockSpec((1, per_group), lambda i, group=group: (0, group)),
        ]
        specs += [tall] * (2 * in_group) + [whole((STATE, CHUNK))] * (2 * in_group)
        aliases = {}
        if out is not None:
            aliases = {len(operands): 0}
            operands.append(out)
            specs.append(pl.BlockSpec(memory_space=pl.ANY))
        out = pl.pallas_call(
            functools.partial(finish_kernel, in_group),
            grid=(length // rows,),
            in_specs=specs,
            out_specs=pl.BlockSpec((rows, per_group), lambda i, group=group: (i, group)),
            out_shape=jax.ShapeDtypeStruct((length, channels), BF16),
            input_output_aliases=aliases,
            compiler_params=pltpu.CompilerParams(vmem_limit_bytes=32 << 20),
            cost_estimate=pl.CostEstimate(
                flops=2 * length * per_group * STATE, bytes_accessed=8 << 20, transcendentals=length
            ),
            name="finish",
        )(*operands)
    return out


def solution(mesh):
    placed = (
        P(("groups", "ctx"), ("tp", "fsdp")),
        P(("groups", "ctx"), ("tp", "fsdp"), None),
        P(("groups", "ctx"), ("tp", "fsdp")),
        P(("groups", "ctx"), ("tp", "fsdp")),
        P(None, ("tp", "fsdp")),
        P(None, ("tp", "fsdp"), None),
        P(("tp", "fsdp")),
        P(("tp", "fsdp")),
        P(("tp", "fsdp")),
        P(("tp", "fsdp")),
    )
    return jax.shard_map(
        shards,
        mesh=mesh,
        in_specs=placed,
        out_specs=P(("groups", "ctx"), ("tp", "fsdp")),
        check_vma=False,
    )
```

time: 357 us -> 130 us (0.36); the launches traced: 351 us -> 129 us
  blocking collectives: 73.9 us -> 0 us
  local copies, waits for them, and re-layouts: 75.1 us -> 16.3 us
  other arithmetic: 43.1 us -> 1.83 us
  waiting for transfers between devices: 99.1 us -> 65.3 us
  matrix products: 27.3 us -> 0 us
  Pallas kernels: 0 us -> 20.8 us
  between operations: 13.7 us -> 0.6 us
  starting transfers between devices: 14.6 us -> 23.9 us
  loops' own time: 3.85 us -> 0 us
    all_gather x1 -> x0, waiting for transfers between devices: 91.1 us -> none  [shards(): every_bc = lax.all_gather(bc_out, 'ctx', axis=0, tiled=True)]
    all_to_all x1 -> x0, blocking collectives: 73.9 us -> none  [shards(): lax.all_to_all(ssm_part, 'ctx', split_axis=0, concat_axis=1, tiled=True)]
    ppermute x2 -> x26, waiting for transfers between devices: 0.77 us -> 65.3 us  [the longest x24 65.3 us: shards(): arrived = lax.ppermute(sent, 'ctx', [(hop, hop + 1)])]
    dot_general x5 -> x0, matrix products: 27.3 us -> none  [the longest x2 18.9 us: diagonal_block(): jnp.einsum('hts,shp->thp', mixing, x_block, preferred_element_type=jnp.fl...]
    ppermute x2 -> x26, starting transfers between devices: 2.58 us -> 23.9 us  [the longest x24 21.3 us: shards(): arrived = lax.ppermute(sent, 'ctx', [(hop, hop + 1)])]
    pallas_call x0 -> x11, Pallas kernels: none -> 20.8 us  [the longest x8 11.4 us: shards(): pl.pallas_call(functools.partial(local_kernel, chunk * (CHUNK // HEAD_DIM...]
    convert_element_type x5 -> x16, other arithmetic: 21.6 us -> 1.29 us  [shards(): sent = (total * arrived.astype(F32) + state).astype(wire)]
    slice x7 -> x8, local copies, waits for them, and re-layouts: 16.6 us -> 0.04 us  [shards(): total = lanes[2 * subs + 1:2 * subs + 2]]
  transfers between devices with their start and end apart: 5 -> 26, of which waited for: 3 -> 8; matrix products, arithmetic and copies ran while one was open for 8% -> 6% of each run, Pallas kernels for 0% -> 13%
where the time goes in v1:
time: 130 us; the launch traced here: 129 us
  waiting for transfers between devices  65.3 us (50%)
  starting transfers between devices  23.9 us (18%)
  Pallas kernels  20.8 us (16%)
  local copies, waits for them, and re-layouts  16.3 us (13%)
  other arithmetic  1.83 us (1%)
    ppermute x24, waiting for transfers between devices, shards(): arrived = lax.ppermute(sent, 'ctx', [(hop, hop + 1)])  65.3 us
    ppermute x24, starting transfers between devices, shards(): arrived = lax.ppermute(sent, 'ctx', [(hop, hop + 1)])  21.3 us
    unnamed x27, local copies, waits for them, and re-layouts  15.5 us
    pallas_call x8, Pallas kernels, shards(): pl.pallas_call(functools.partial(local_kernel, chunk * (CHUNK // HEAD_DIM...  11.4 us
    pallas_call x2, Pallas kernels, shards(): pl.pallas_call(functools.partial(finish_kernel, in_group), grid=(length /...  5.62 us
    pallas_call x1, Pallas kernels, shards(): pl.pallas_call(functools.partial(prepare_kernel, groups), out_shape=(jax....  3.73 us
  transfers between devices with their start and end apart: 26, of which 8 were waited for; matrix products, arithmetic and copies ran while one was open for 6% of the time, Pallas kernels for 13%

profile of v1, /device:TPU:28, one launch (start us, length us, event | category | flops | bytes accessed | tf_op | source)
XLA Modules:
  0.0 128.8 jit_solution(14367365293028339665)
XLA Ops:
  0.9 1.3 %collective-permute-start.1 = (bf16[3,4096]{1,0:T(4,128)(2,1)S(1)}, bf16[3,4096]{1,0:T(4,128)(2,1)S(1)}, u32[]{:S(2)}, u32[]{:S(2)}) collective-permute-start(bf16[3,4096]{1,0:T(4,128)(2,1)S(1)} %slice.35), channel_id=1, source_target_pairs={{0,4},{4,8},{8,12},{1,5},{5,9},{9,13},{2,6},{6,10},{10,14},{3,7},{... | collective-permute-start | bytes 73736 | tf_op jit(solution)/shard_map/ppermute | solution.py:170
  2.9 1.3 %collective-permute-start = (bf16[3,1024]{1,0:T(4,128)(2,1)S(1)}, bf16[3,1024]{1,0:T(4,128)(2,1)S(1)}, u32[]{:S(2)}, u32[]{:S(2)}) collective-permute-start(bf16[3,1024]{1,0:T(4,128)(2,1)S(1)} %bitcast.41), channel_id=1, source_target_pairs={{0,4},{4,8},{8,12},{1,5},{5,9},{9,13},{2,6},{6,10},{10,14},{3,7},{... | collective-permute-start | bytes 18440 | tf_op jit(solution)/shard_map/ppermute | solution.py:170
  4.2 1.3 %copy.15 = f32[1,4,2,512]{3,1,2,0:T(4,128)} copy(f32[1,4,2,512]{3,2,1,0:T(2,128)} %bitcast.40) | data formatting | bytes 32768
  5.5 1.5 %copy.12.dt_ref = bf16[384,64]{1,0:T(8,128)(2,1)} copy(bf16[384,64]{0,1:T(8,128)(2,1)} %param.13) | data formatting | bytes 98304 | tf_op args[3]
  7.0 2.1 %copy.13 = bf16[48,8,2,512]{3,1,2,0:T(8,128)(2,1)} copy(bf16[48,8,2,512]{3,2,1,0:T(2,128)(2,1)} %bitcast.22) | data formatting | bytes 1572864
  9.8 3.7 %prepare.1 = (bf16[2,384,384]{2,1,0:T(8,128)(2,1)}, bf16[2,256,384]{2,1,0:T(8,128)(2,1)}, bf16[384,128]{1,0:T(8,128)(2,1)}, bf16[384,128]{1,0:T(8,128)(2,1)}, bf16[8,128]{1,0:T(8,128)(2,1)}) custom-call(bf16[384,1024]{1,0:T(8,128)(2,1)} %bitcast.21, bf16[3,1024]{1,0:T(4,128)(2,1)} %copy-done.10, f32[4,1024]{1,0:T(4,128)} %bitcast.23, ...), custom_call_target="tpu_custom_call" | custom-call | tf_op jit(solution)/shard_map/prepare/pallas_call | solution.py:173
  13.5 1.9 %copy-done = bf16[384,4096]{1,0:T(8,128)(2,1)S(1)} copy-done((bf16[384,4096]{1,0:T(8,128)(2,1)S(1)}, bf16[384,4096]{1,0:T(8,128)(2,1)}, u32[]{:S(2)}) %copy-start) | copy-done | bytes 3145752
  15.4 1.9 %copy-done.1 = bf16[384,4096]{1,0:T(8,128)(2,1)S(1)} copy-done((bf16[384,4096]{1,0:T(8,128)(2,1)S(1)}, bf16[384,4096]{1,0:T(8,128)(2,1)}, u32[]{:S(2)}) %copy-start.1) | copy-done | bytes 3145752
  22.7 1.4 %local.15 = (f32[384,512]{1,0:T(8,128)S(1)}, f32[384,512]{1,0:T(8,128)S(1)}, f32[256,512]{1,0:T(8,128)S(1)}, bf16[256,512]{1,0:T(8,128)(2,1)S(1)}, f32[8,512]{1,0:T(8,128)S(1)}) custom-call(bf16[384,4096]{1,0:T(8,128)(2,1)S(1)} %copy-done, bf16[3,4096]{1,0:T(4,128)(2,1)S(1)} %collective-permute-done.1.early_ref, f32[4,4096]{1,0:T(4,128)S(1)} %copy-done.7, ...), custom_call_target="tpu_custom_call" | custom-call | flops 314572800 | bytes 4194304 | tf_op jit(solution)/shard_map/local/pallas_call | solution.py:202
  24.8 1.4 %local.14 = (f32[384,512]{1,0:T(8,128)S(1)}, f32[384,512]{1,0:T(8,128)S(1)}, f32[256,512]{1,0:T(8,128)S(1)}, bf16[256,512]{1,0:T(8,128)(2,1)S(1)}, f32[8,512]{1,0:T(8,128)S(1)}) custom-call(bf16[384,4096]{1,0:T(8,128)(2,1)S(1)} %copy-done, bf16[3,4096]{1,0:T(4,128)(2,1)S(1)} %collective-permute-done.1.early_ref, f32[4,4096]{1,0:T(4,128)S(1)} %copy-done.7, ...), custom_call_target="tpu_custom_call" | custom-call | flops 314572800 | bytes 4194304 | tf_op jit(solution)/shard_map/local/pallas_call | solution.py:202
  26.9 1.4 %local.13 = (f32[384,512]{1,0:T(8,128)S(1)}, f32[384,512]{1,0:T(8,128)S(1)}, f32[256,512]{1,0:T(8,128)S(1)}, bf16[256,512]{1,0:T(8,128)(2,1)S(1)}, f32[8,512]{1,0:T(8,128)S(1)}) custom-call(bf16[384,4096]{1,0:T(8,128)(2,1)S(1)} %copy-done, bf16[3,4096]{1,0:T(4,128)(2,1)S(1)} %collective-permute-done.1.early_ref, f32[4,4096]{1,0:T(4,128)S(1)} %copy-done.7, ...), custom_call_target="tpu_custom_call" | custom-call | flops 314572800 | bytes 4194304 | tf_op jit(solution)/shard_map/local/pallas_call | solution.py:202
  29.1 1.4 %local.12 = (f32[384,512]{1,0:T(8,128)S(1)}, f32[384,512]{1,0:T(8,128)S(1)}, f32[256,512]{1,0:T(8,128)S(1)}, bf16[256,512]{1,0:T(8,128)(2,1)S(1)}, f32[8,512]{1,0:T(8,128)S(1)}) custom-call(bf16[384,4096]{1,0:T(8,128)(2,1)S(1)} %copy-done, bf16[3,4096]{1,0:T(4,128)(2,1)S(1)} %collective-permute-done.1.early_ref, f32[4,4096]{1,0:T(4,128)S(1)} %copy-done.7, ...), custom_call_target="tpu_custom_call" | custom-call | flops 314572800 | bytes 4194304 | tf_op jit(solution)/shard_map/local/pallas_call | solution.py:202
  31.2 1.4 %local.11 = (f32[384,512]{1,0:T(8,128)S(1)}, f32[384,512]{1,0:T(8,128)S(1)}, f32[256,512]{1,0:T(8,128)S(1)}, bf16[256,512]{1,0:T(8,128)(2,1)S(1)}, f32[8,512]{1,0:T(8,128)S(1)}) custom-call(bf16[384,4096]{1,0:T(8,128)(2,1)S(1)} %copy-done, bf16[3,4096]{1,0:T(4,128)(2,1)S(1)} %collective-permute-done.1.early_ref, f32[4,4096]{1,0:T(4,128)S(1)} %copy-done.7, ...), custom_call_target="tpu_custom_call" | custom-call | flops 314572800 | bytes 4194304 | tf_op jit(solution)/shard_map/local/pallas_call | solution.py:202
  33.5 1.4 %local.9 = (f32[384,512]{1,0:T(8,128)S(1)}, f32[384,512]{1,0:T(8,128)S(1)}, f32[256,512]{1,0:T(8,128)S(1)}, bf16[256,512]{1,0:T(8,128)(2,1)S(1)}, f32[8,512]{1,0:T(8,128)S(1)}) custom-call(bf16[384,4096]{1,0:T(8,128)(2,1)S(1)} %copy-done, bf16[3,4096]{1,0:T(4,128)(2,1)S(1)} %collective-permute-done.1.early_ref, f32[4,4096]{1,0:T(4,128)S(1)} %copy-done.7, ...), custom_call_target="tpu_custom_call" | custom-call | flops 314572800 | bytes 4194304 | tf_op jit(solution)/shard_map/local/pallas_call | solution.py:202
  34.9 1.4 %local.8 = (f32[384,512]{1,0:T(8,128)S(1)}, f32[384,512]{1,0:T(8,128)S(1)}, f32[256,512]{1,0:T(8,128)S(1)}, bf16[256,512]{1,0:T(8,128)(2,1)S(1)}, f32[8,512]{1,0:T(8,128)S(1)}) custom-call(bf16[384,4096]{1,0:T(8,128)(2,1)S(1)} %copy-done, bf16[3,4096]{1,0:T(4,128)(2,1)S(1)} %collective-permute-done.1.early_ref, f32[4,4096]{1,0:T(4,128)S(1)} %copy-done.7, ...), custom_call_target="tpu_custom_call" | custom-call | flops 314572800 | bytes 4194304 | tf_op jit(solution)/shard_map/local/pallas_call | solution.py:202
  36.4 1.4 %local.10 = (f32[384,512]{1,0:T(8,128)S(1)}, f32[384,512]{1,0:T(8,128)S(1)}, f32[256,512]{1,0:T(8,128)S(1)}, bf16[256,512]{1,0:T(8,128)(2,1)S(1)}, f32[8,512]{1,0:T(8,128)S(1)}) custom-call(bf16[384,4096]{1,0:T(8,128)(2,1)S(1)} %copy-done, bf16[3,4096]{1,0:T(4,128)(2,1)S(1)} %collective-permute-done.1.early_ref, f32[4,4096]{1,0:T(4,128)S(1)} %copy-done.7, ...), custom_call_target="tpu_custom_call" | custom-call | flops 314572800 | bytes 4194304 | tf_op jit(solution)/shard_map/local/pallas_call | solution.py:202
  46.4 1.3 %collective-permute-start.25 = (bf16[256,512]{1,0:T(8,128)(2,1)S(1)}, bf16[256,512]{1,0:T(8,128)(2,1)S(1)}, u32[]{:S(2)}, u32[]{:S(2)}) collective-permute-start(bf16[256,512]{1,0:T(8,128)(2,1)S(1)} %add_convert_fusion), channel_id=1, source_target_pairs={{8,12},{9,13},{10,14},{11,15},{24,28},{25,29},{26,30},{27,31}} | collective-permute-start | bytes 786440 | tf_op jit(solution)/shard_map/ppermute | solution.py:237
  47.8 1.3 %collective-permute-start.24 = (bf16[256,512]{1,0:T(8,128)(2,1)S(1)}, bf16[256,512]{1,0:T(8,128)(2,1)S(1)}, u32[]{:S(2)}, u32[]{:S(2)}) collective-permute-start(bf16[256,512]{1,0:T(8,128)(2,1)S(1)} %add_convert_fusion.1), channel_id=1, source_target_pairs={{8,12},{9,13},{10,14},{11,15},{24,28},{25,29},{26,30},{27,31}} | collective-permute-start | bytes 786440 | tf_op jit(solution)/shard_map/ppermute | solution.py:237
  49.2 1.3 %collective-permute-start.23 = (bf16[256,512]{1,0:T(8,128)(2,1)S(1)}, bf16[256,512]{1,0:T(8,128)(2,1)S(1)}, u32[]{:S(2)}, u32[]{:S(2)}) collective-permute-start(bf16[256,512]{1,0:T(8,128)(2,1)S(1)} %add_convert_fusion.2), channel_id=1, source_target_pairs={{8,12},{9,13},{10,14},{11,15},{24,28},{25,29},{26,30},{27,31}} | collective-permute-start | bytes 786440 | tf_op jit(solution)/shard_map/ppermute | solution.py:237
  50.6 1.3 %collective-permute-start.22 = (bf16[256,512]{1,0:T(8,128)(2,1)S(1)}, bf16[256,512]{1,0:T(8,128)(2,1)S(1)}, u32[]{:S(2)}, u32[]{:S(2)}) collective-permute-start(bf16[256,512]{1,0:T(8,128)(2,1)S(1)} %add_convert_fusion.3), channel_id=1, source_target_pairs={{8,12},{9,13},{10,14},{11,15},{24,28},{25,29},{26,30},{27,31}} | collective-permute-start | bytes 786440 | tf_op jit(solution)/shard_map/ppermute | solution.py:237
  52.0 1.3 %collective-permute-start.13 = (bf16[256,512]{1,0:T(8,128)(2,1)S(1)}, bf16[256,512]{1,0:T(8,128)(2,1)S(1)}, u32[]{:S(2)}, u32[]{:S(2)}) collective-permute-start(bf16[256,512]{1,0:T(8,128)(2,1)S(1)} %add_convert_fusion.8), channel_id=1, source_target_pairs={{8,12},{9,13},{10,14},{11,15},{24,28},{25,29},{26,30},{27,31}} | collective-permute-start | bytes 786440 | tf_op jit(solution)/shard_map/ppermute | solution.py:237
  53.4 33.3 %collective-permute-done.25.refs_17_ = bf16[256,512]{1,0:T(8,128)(2,1)S(1)} collective-permute-done((bf16[256,512]{1,0:T(8,128)(2,1)S(1)}, bf16[256,512]{1,0:T(8,128)(2,1)S(1)}, u32[]{:S(2)}, u32[]{:S(2)}) %collective-permute-start.25) | collective-permute-done | bytes 262176 | tf_op jit(solution)/shard_map/ppermute | solution.py:237
  88.0 4.3 %collective-permute-done.24.refs_16_ = bf16[256,512]{1,0:T(8,128)(2,1)S(1)} collective-permute-done((bf16[256,512]{1,0:T(8,128)(2,1)S(1)}, bf16[256,512]{1,0:T(8,128)(2,1)S(1)}, u32[]{:S(2)}, u32[]{:S(2)}) %collective-permute-start.24) | collective-permute-done | bytes 262176 | tf_op jit(solution)/shard_map/ppermute | solution.py:237
  93.6 4.3 %collective-permute-done.23.refs_15_ = bf16[256,512]{1,0:T(8,128)(2,1)S(1)} collective-permute-done((bf16[256,512]{1,0:T(8,128)(2,1)S(1)}, bf16[256,512]{1,0:T(8,128)(2,1)S(1)}, u32[]{:S(2)}, u32[]{:S(2)}) %collective-permute-start.23) | collective-permute-done | bytes 262176 | tf_op jit(solution)/shard_map/ppermute | solution.py:237
  98.0 1.3 collective-permute-start.10
  99.8 3.8 %collective-permute-done.22.refs_14_ = bf16[256,512]{1,0:T(8,128)(2,1)S(1)} collective-permute-done((bf16[256,512]{1,0:T(8,128)(2,1)S(1)}, bf16[256,512]{1,0:T(8,128)(2,1)S(1)}, u32[]{:S(2)}, u32[]{:S(2)}) %collective-permute-start.22) | collective-permute-done | bytes 262176 | tf_op jit(solution)/shard_map/ppermute | solution.py:237
  103.6 2.8 %finish.2.refs_18_ = bf16[384,4096]{1,0:T(8,128)(2,1)} custom-call(bf16[2,384,384]{2,1,0:T(8,128)(2,1)S(1)} %copy-done.3, f32[1,4096]{1,0:T(1,128)S(1)} %bitcast.19, f32[384,512]{1,0:T(8,128)S(1)} %get-tuple-element.75.refs_2_, f32[384,512]{1,0:T(8,128)S(1)} %get-tuple-element.76.refs_3_, f32[384,512]{1,0:T(8,128)S(1)} %get-tuple-element.77.refs_4_, ...), custom_call_target="tpu_custom_call" | custom-call | flops 402653184 | bytes 8388608 | tf_op jit(solution)/shard_map/finish/pallas_call | solution.py:265
  106.4 4.4 %collective-permute-done.13.refs_17_ = bf16[256,512]{1,0:T(8,128)(2,1)S(1)} collective-permute-done((bf16[256,512]{1,0:T(8,128)(2,1)S(1)}, bf16[256,512]{1,0:T(8,128)(2,1)S(1)}, u32[]{:S(2)}, u32[]{:S(2)}) %collective-permute-start.13) | collective-permute-done | bytes 262176 | tf_op jit(solution)/shard_map/ppermute | solution.py:237
  110.8 5.6 %collective-permute-done.12.refs_16_ = bf16[256,512]{1,0:T(8,128)(2,1)S(1)} collective-permute-done((bf16[256,512]{1,0:T(8,128)(2,1)S(1)}, bf16[256,512]{1,0:T(8,128)(2,1)S(1)}, u32[]{:S(2)}, u32[]{:S(2)}) %collective-permute-start.12) | collective-permute-done | bytes 262176 | tf_op jit(solution)/shard_map/ppermute | solution.py:237
  116.4 5.6 %collective-permute-done.11.refs_15_ = bf16[256,512]{1,0:T(8,128)(2,1)S(1)} collective-permute-done((bf16[256,512]{1,0:T(8,128)(2,1)S(1)}, bf16[256,512]{1,0:T(8,128)(2,1)S(1)}, u32[]{:S(2)}, u32[]{:S(2)}) %collective-permute-start.11) | collective-permute-done | bytes 262176 | tf_op jit(solution)/shard_map/ppermute | solution.py:237
  122.0 3.9 %collective-permute-done.10.refs_14_ = bf16[256,512]{1,0:T(8,128)(2,1)S(1)} collective-permute-done((bf16[256,512]{1,0:T(8,128)(2,1)S(1)}, bf16[256,512]{1,0:T(8,128)(2,1)S(1)}, u32[]{:S(2)}, u32[]{:S(2)}) %collective-permute-start.10) | collective-permute-done | bytes 262176 | tf_op jit(solution)/shard_map/ppermute | solution.py:237
  126.0 2.8 %finish.3 = bf16[384,4096]{1,0:T(8,128)(2,1)} custom-call(bf16[2,384,384]{2,1,0:T(8,128)(2,1)S(1)} %copy-done.3, f32[1,4096]{1,0:T(1,128)S(1)} %bitcast.20, f32[384,512]{1,0:T(8,128)S(1)} %get-tuple-element.55.refs_2_, f32[384,512]{1,0:T(8,128)S(1)} %get-tuple-element.56.refs_3_, ...), custom_call_target="tpu_custom_call", output_to_operand_aliasing={{}: (18, {})} | custom-call | flops 402653184 | bytes 8388608 | tf_op jit(solution)/shard_map/finish/pallas_call | solution.py:265
  (91 shorter events, 23.0 us)
Async XLA Ops:
  0.9 12.7 %collective-permute-start.1 = (bf16[3,4096]{1,0:T(4,128)(2,1)S(1)}, bf16[3,4096]{1,0:T(4,128)(2,1)S(1)}, u32[]{:S(2)}, u32[]{:S(2)}) collective-permute-start(bf16[3,4096]{1,0:T(4,128)(2,1)S(1)} %slice.35), channel_id=1, source_target_pairs={{0,4},{4,8},{8,12},{1,5},{5,9},{9,13},{2,6},{6,10},{10,14},{3,7},{... | collective-permute-start | bytes 73736 | tf_op jit(solution)/shard_map/ppermute | solution.py:170
  2.9 6.3 %collective-permute-start = (bf16[3,1024]{1,0:T(4,128)(2,1)S(1)}, bf16[3,1024]{1,0:T(4,128)(2,1)S(1)}, u32[]{:S(2)}, u32[]{:S(2)}) collective-permute-start(bf16[3,1024]{1,0:T(4,128)(2,1)S(1)} %bitcast.41), channel_id=1, source_target_pairs={{0,4},{4,8},{8,12},{1,5},{5,9},{9,13},{2,6},{6,10},{10,14},{3,7},{... | collective-permute-start | bytes 18440 | tf_op jit(solution)/shard_map/ppermute | solution.py:170
  13.5 1.9 %copy-start = (bf16[384,4096]{1,0:T(8,128)(2,1)S(1)}, bf16[384,4096]{1,0:T(8,128)(2,1)}, u32[]{:S(2)}) copy-start(bf16[384,4096]{1,0:T(8,128)(2,1)} %x_ref.15) | copy-start | bytes 9437188
  15.4 1.9 %copy-start.1 = (bf16[384,4096]{1,0:T(8,128)(2,1)S(1)}, bf16[384,4096]{1,0:T(8,128)(2,1)}, u32[]{:S(2)}) copy-start(bf16[384,4096]{1,0:T(8,128)(2,1)} %z_ref.15) | copy-start | bytes 9437188
  17.3 1.1 copy-start.2
  18.4 1.0 copy-start.4
  24.1 13.7 %collective-permute-start.20 = (bf16[256,512]{1,0:T(8,128)(2,1)S(1)}, bf16[256,512]{1,0:T(8,128)(2,1)S(1)}, u32[]{:S(2)}, u32[]{:S(2)}) collective-permute-start(bf16[256,512]{1,0:T(8,128)(2,1)S(1)} %get-tuple-element.92), channel_id=1, source_target_pairs={{0,4},{1,5},{2,6},{3,7},{16,20},{17,21},{18,22},{19,23}} | collective-permute-start | bytes 786440 | tf_op jit(solution)/shard_map/ppermute | solution.py:237
  26.2 12.4 %collective-permute-start.18 = (bf16[256,512]{1,0:T(8,128)(2,1)S(1)}, bf16[256,512]{1,0:T(8,128)(2,1)S(1)}, u32[]{:S(2)}, u32[]{:S(2)}) collective-permute-start(bf16[256,512]{1,0:T(8,128)(2,1)S(1)} %get-tuple-element.89), channel_id=1, source_target_pairs={{0,4},{1,5},{2,6},{3,7},{16,20},{17,21},{18,22},{19,23}} | collective-permute-start | bytes 786440 | tf_op jit(solution)/shard_map/ppermute | solution.py:237
  28.4 11.0 %collective-permute-start.16 = (bf16[256,512]{1,0:T(8,128)(2,1)S(1)}, bf16[256,512]{1,0:T(8,128)(2,1)S(1)}, u32[]{:S(2)}, u32[]{:S(2)}) collective-permute-start(bf16[256,512]{1,0:T(8,128)(2,1)S(1)} %get-tuple-element.86), channel_id=1, source_target_pairs={{0,4},{1,5},{2,6},{3,7},{16,20},{17,21},{18,22},{19,23}} | collective-permute-start | bytes 786440 | tf_op jit(solution)/shard_map/ppermute | solution.py:237
  30.5 9.7 %collective-permute-start.14 = (bf16[256,512]{1,0:T(8,128)(2,1)S(1)}, bf16[256,512]{1,0:T(8,128)(2,1)S(1)}, u32[]{:S(2)}, u32[]{:S(2)}) collective-permute-start(bf16[256,512]{1,0:T(8,128)(2,1)S(1)} %get-tuple-element.83), channel_id=1, source_target_pairs={{0,4},{1,5},{2,6},{3,7},{16,20},{17,21},{18,22},{19,23}} | collective-permute-start | bytes 786440 | tf_op jit(solution)/shard_map/ppermute | solution.py:237
  32.6 8.3 %collective-permute-start.8 = (bf16[256,512]{1,0:T(8,128)(2,1)S(1)}, bf16[256,512]{1,0:T(8,128)(2,1)S(1)}, u32[]{:S(2)}, u32[]{:S(2)}) collective-permute-start(bf16[256,512]{1,0:T(8,128)(2,1)S(1)} %get-tuple-element.72), channel_id=1, source_target_pairs={{0,4},{1,5},{2,6},{3,7},{16,20},{17,21},{18,22},{19,23}} | collective-permute-start | bytes 786440 | tf_op jit(solution)/shard_map/ppermute | solution.py:237
  37.8 3.9 %collective-permute-start.6 = (bf16[256,512]{1,0:T(8,128)(2,1)S(1)}, bf16[256,512]{1,0:T(8,128)(2,1)S(1)}, u32[]{:S(2)}, u32[]{:S(2)}) collective-permute-start(bf16[256,512]{1,0:T(8,128)(2,1)S(1)} %get-tuple-element.69), channel_id=1, source_target_pairs={{0,4},{1,5},{2,6},{3,7},{16,20},{17,21},{18,22},{19,23}} | collective-permute-start | bytes 786440 | tf_op jit(solution)/shard_map/ppermute | solution.py:237
  38.6 3.9 %collective-permute-start.4 = (bf16[256,512]{1,0:T(8,128)(2,1)S(1)}, bf16[256,512]{1,0:T(8,128)(2,1)S(1)}, u32[]{:S(2)}, u32[]{:S(2)}) collective-permute-start(bf16[256,512]{1,0:T(8,128)(2,1)S(1)} %get-tuple-element.66), channel_id=1, source_target_pairs={{0,4},{1,5},{2,6},{3,7},{16,20},{17,21},{18,22},{19,23}} | collective-permute-start | bytes 786440 | tf_op jit(solution)/shard_map/ppermute | solution.py:237
  39.4 3.9 %collective-permute-start.2 = (bf16[256,512]{1,0:T(8,128)(2,1)S(1)}, bf16[256,512]{1,0:T(8,128)(2,1)S(1)}, u32[]{:S(2)}, u32[]{:S(2)}) collective-permute-start(bf16[256,512]{1,0:T(8,128)(2,1)S(1)} %get-tuple-element.63), channel_id=1, source_target_pairs={{0,4},{1,5},{2,6},{3,7},{16,20},{17,21},{18,22},{19,23}} | collective-permute-start | bytes 786440 | tf_op jit(solution)/shard_map/ppermute | solution.py:237
  40.2 3.9 %collective-permute-start.21 = (bf16[256,512]{1,0:T(8,128)(2,1)S(1)}, bf16[256,512]{1,0:T(8,128)(2,1)S(1)}, u32[]{:S(2)}, u32[]{:S(2)}) collective-permute-start(bf16[256,512]{1,0:T(8,128)(2,1)S(1)} %add_convert_fusion.4), channel_id=1, source_target_pairs={{4,8},{5,9},{6,10},{7,11},{20,24},{21,25},{22,26},{23,27}} | collective-permute-start | bytes 786440 | tf_op jit(solution)/shard_map/ppermute | solution.py:237
  41.0 3.9 %collective-permute-start.19 = (bf16[256,512]{1,0:T(8,128)(2,1)S(1)}, bf16[256,512]{1,0:T(8,128)(2,1)S(1)}, u32[]{:S(2)}, u32[]{:S(2)}) collective-permute-start(bf16[256,512]{1,0:T(8,128)(2,1)S(1)} %add_convert_fusion.5), channel_id=1, source_target_pairs={{4,8},{5,9},{6,10},{7,11},{20,24},{21,25},{22,26},{23,27}} | collective-permute-start | bytes 786440 | tf_op jit(solution)/shard_map/ppermute | solution.py:237
  41.8 3.9 %collective-permute-start.17 = (bf16[256,512]{1,0:T(8,128)(2,1)S(1)}, bf16[256,512]{1,0:T(8,128)(2,1)S(1)}, u32[]{:S(2)}, u32[]{:S(2)}) collective-permute-start(bf16[256,512]{1,0:T(8,128)(2,1)S(1)} %add_convert_fusion.6), channel_id=1, source_target_pairs={{4,8},{5,9},{6,10},{7,11},{20,24},{21,25},{22,26},{23,27}} | collective-permute-start | bytes 786440 | tf_op jit(solution)/shard_map/ppermute | solution.py:237
  42.5 3.9 %collective-permute-start.15 = (bf16[256,512]{1,0:T(8,128)(2,1)S(1)}, bf16[256,512]{1,0:T(8,128)(2,1)S(1)}, u32[]{:S(2)}, u32[]{:S(2)}) collective-permute-start(bf16[256,512]{1,0:T(8,128)(2,1)S(1)} %add_convert_fusion.7), channel_id=1, source_target_pairs={{4,8},{5,9},{6,10},{7,11},{20,24},{21,25},{22,26},{23,27}} | collective-permute-start | bytes 786440 | tf_op jit(solution)/shard_map/ppermute | solution.py:237
  43.3 4.5 %collective-permute-start.9 = (bf16[256,512]{1,0:T(8,128)(2,1)S(1)}, bf16[256,512]{1,0:T(8,128)(2,1)S(1)}, u32[]{:S(2)}, u32[]{:S(2)}) collective-permute-start(bf16[256,512]{1,0:T(8,128)(2,1)S(1)} %add_convert_fusion.12), channel_id=1, source_target_pairs={{4,8},{5,9},{6,10},{7,11},{20,24},{21,25},{22,26},{23,27}} | collective-permute-start | bytes 786440 | tf_op jit(solution)/shard_map/ppermute | solution.py:237
  44.1 5.1 %collective-permute-start.7 = (bf16[256,512]{1,0:T(8,128)(2,1)S(1)}, bf16[256,512]{1,0:T(8,128)(2,1)S(1)}, u32[]{:S(2)}, u32[]{:S(2)}) collective-permute-start(bf16[256,512]{1,0:T(8,128)(2,1)S(1)} %add_convert_fusion.13), channel_id=1, source_target_pairs={{4,8},{5,9},{6,10},{7,11},{20,24},{21,25},{22,26},{23,27}} | collective-permute-start | bytes 786440 | tf_op jit(solution)/shard_map/ppermute | solution.py:237
  44.9 5.7 %collective-permute-start.5 = (bf16[256,512]{1,0:T(8,128)(2,1)S(1)}, bf16[256,512]{1,0:T(8,128)(2,1)S(1)}, u32[]{:S(2)}, u32[]{:S(2)}) collective-permute-start(bf16[256,512]{1,0:T(8,128)(2,1)S(1)} %add_convert_fusion.14), channel_id=1, source_target_pairs={{4,8},{5,9},{6,10},{7,11},{20,24},{21,25},{22,26},{23,27}} | collective-permute-start | bytes 786440 | tf_op jit(solution)/shard_map/ppermute | solution.py:237
  45.7 6.3 %collective-permute-start.3 = (bf16[256,512]{1,0:T(8,128)(2,1)S(1)}, bf16[256,512]{1,0:T(8,128)(2,1)S(1)}, u32[]{:S(2)}, u32[]{:S(2)}) collective-permute-start(bf16[256,512]{1,0:T(8,128)(2,1)S(1)} %add_convert_fusion.15), channel_id=1, source_target_pairs={{4,8},{5,9},{6,10},{7,11},{20,24},{21,25},{22,26},{23,27}} | collective-permute-start | bytes 786440 | tf_op jit(solution)/shard_map/ppermute | solution.py:237
  46.4 40.3 %collective-permute-start.25 = (bf16[256,512]{1,0:T(8,128)(2,1)S(1)}, bf16[256,512]{1,0:T(8,128)(2,1)S(1)}, u32[]{:S(2)}, u32[]{:S(2)}) collective-permute-start(bf16[256,512]{1,0:T(8,128)(2,1)S(1)} %add_convert_fusion), channel_id=1, source_target_pairs={{8,12},{9,13},{10,14},{11,15},{24,28},{25,29},{26,30},{27,31}} | collective-permute-start | bytes 786440 | tf_op jit(solution)/shard_map/ppermute | solution.py:237
  47.8 44.5 %collective-permute-start.24 = (bf16[256,512]{1,0:T(8,128)(2,1)S(1)}, bf16[256,512]{1,0:T(8,128)(2,1)S(1)}, u32[]{:S(2)}, u32[]{:S(2)}) collective-permute-start(bf16[256,512]{1,0:T(8,128)(2,1)S(1)} %add_convert_fusion.1), channel_id=1, source_target_pairs={{8,12},{9,13},{10,14},{11,15},{24,28},{25,29},{26,30},{27,31}} | collective-permute-start | bytes 786440 | tf_op jit(solution)/shard_map/ppermute | solution.py:237
  49.2 48.7 %collective-permute-start.23 = (bf16[256,512]{1,0:T(8,128)(2,1)S(1)}, bf16[256,512]{1,0:T(8,128)(2,1)S(1)}, u32[]{:S(2)}, u32[]{:S(2)}) collective-permute-start(bf16[256,512]{1,0:T(8,128)(2,1)S(1)} %add_convert_fusion.2), channel_id=1, source_target_pairs={{8,12},{9,13},{10,14},{11,15},{24,28},{25,29},{26,30},{27,31}} | collective-permute-start | bytes 786440 | tf_op jit(solution)/shard_map/ppermute | solution.py:237
  50.6 53.0 %collective-permute-start.22 = (bf16[256,512]{1,0:T(8,128)(2,1)S(1)}, bf16[256,512]{1,0:T(8,128)(2,1)S(1)}, u32[]{:S(2)}, u32[]{:S(2)}) collective-permute-start(bf16[256,512]{1,0:T(8,128)(2,1)S(1)} %add_convert_fusion.3), channel_id=1, source_target_pairs={{8,12},{9,13},{10,14},{11,15},{24,28},{25,29},{26,30},{27,31}} | collective-permute-start | bytes 786440 | tf_op jit(solution)/shard_map/ppermute | solution.py:237
  52.0 58.8 %collective-permute-start.13 = (bf16[256,512]{1,0:T(8,128)(2,1)S(1)}, bf16[256,512]{1,0:T(8,128)(2,1)S(1)}, u32[]{:S(2)}, u32[]{:S(2)}) collective-permute-start(bf16[256,512]{1,0:T(8,128)(2,1)S(1)} %add_convert_fusion.8), channel_id=1, source_target_pairs={{8,12},{9,13},{10,14},{11,15},{24,28},{25,29},{26,30},{27,31}} | collective-permute-start | bytes 786440 | tf_op jit(solution)/shard_map/ppermute | solution.py:237
  53.4 50.2 %copy-start.3 = (bf16[2,384,384]{2,1,0:T(8,128)(2,1)S(1)}, bf16[2,384,384]{2,1,0:T(8,128)(2,1)}, u32[]{:S(2)}) copy-start(bf16[2,384,384]{2,1,0:T(8,128)(2,1)} %get-tuple-element.50.left_ref.refs_0_) | copy-start | bytes 1769476
  53.4 50.2 %copy-start.9 = (f32[4096]{0:T(1024)S(1)}, f32[4096]{0:T(1024)}, u32[]{:S(2)}) copy-start(f32[4096]{0:T(1024)} %param.19) | copy-start | bytes 49156
  86.7 29.7 %collective-permute-start.12 = (bf16[256,512]{1,0:T(8,128)(2,1)S(1)}, bf16[256,512]{1,0:T(8,128)(2,1)S(1)}, u32[]{:S(2)}, u32[]{:S(2)}) collective-permute-start(bf16[256,512]{1,0:T(8,128)(2,1)S(1)} %add_convert_fusion.9), channel_id=1, source_target_pairs={{8,12},{9,13},{10,14},{11,15},{24,28},{25,29},{26,30},{27,31}} | collective-permute-start | bytes 786440 | tf_op jit(solution)/shard_map/ppermute | solution.py:237
  92.3 29.7 %collective-permute-start.11 = (bf16[256,512]{1,0:T(8,128)(2,1)S(1)}, bf16[256,512]{1,0:T(8,128)(2,1)S(1)}, u32[]{:S(2)}, u32[]{:S(2)}) collective-permute-start(bf16[256,512]{1,0:T(8,128)(2,1)S(1)} %add_convert_fusion.10), channel_id=1, source_target_pairs={{8,12},{9,13},{10,14},{11,15},{24,28},{25,29},{26,30},{27,31}} | collective-permute-start | bytes 786440 | tf_op jit(solution)/shard_map/ppermute | solution.py:237
  98.0 28.0 %collective-permute-start.10 = (bf16[256,512]{1,0:T(8,128)(2,1)S(1)}, bf16[256,512]{1,0:T(8,128)(2,1)S(1)}, u32[]{:S(2)}, u32[]{:S(2)}) collective-permute-start(bf16[256,512]{1,0:T(8,128)(2,1)S(1)} %add_convert_fusion.11), channel_id=1, source_target_pairs={{8,12},{9,13},{10,14},{11,15},{24,28},{25,29},{26,30},{27,31}} | collective-permute-start | bytes 786440 | tf_op jit(solution)/shard_map/ppermute | solution.py:237
  (5 other events, 3.9 us)

commit v2 on v1

v2 whole, which is shorter than its diff:
```python
import functools

import jax
import jax.numpy as jnp
from jax import lax
from jax.experimental import pallas as pl
from jax.experimental.pallas import tpu as pltpu
from jax.sharding import PartitionSpec as P

HEAD_DIM = 64
STATE = 256
KERNEL = 4
SUB = 128
CHUNK = 512
LOCAL_VMEM = 16 << 20
LAG = 1
F32 = jnp.float32
BF16 = jnp.bfloat16


def dot(left, right):
    return jnp.dot(left, right, preferred_element_type=F32)


def silu(value):
    half = 0.5 * value
    return half + half * jnp.tanh(half)


def two_terms(value):
    high = value.astype(BF16)
    low = (value - high.astype(F32)).astype(BF16)
    return high, low


def causal_conv(current, earlier, taps):
    length, width = current.shape
    wide = current.astype(F32)
    head = jnp.concatenate([jnp.zeros((8 - KERNEL + 1, width), F32), earlier.astype(F32)], axis=0)
    joined = jnp.concatenate([head, wide], axis=0)
    total = taps[KERNEL - 1 : KERNEL] * wide
    for back in range(1, KERNEL):
        row = KERNEL - 1 - back
        total = total + taps[row : row + 1] * joined[8 - back : 8 - back + length]
    return silu(total).astype(BF16)


def column_of(row):
    size = row.shape[1]
    at = lax.broadcasted_iota(jnp.int32, (size, size), 0)
    of = lax.broadcasted_iota(jnp.int32, (size, size), 1)
    return jnp.sum(jnp.where(at == of, row, 0.0), axis=1, keepdims=True)


def terms_by_row(value):
    high = value.astype(BF16).astype(F32)
    low = value - high
    return jnp.concatenate([high, low], axis=0).T.astype(BF16)


def steps_kernel(staged, *refs):
    whole_refs = refs[:staged]
    small_refs = refs[staged : staged + 4]
    copies_out = refs[staged + 4 : 2 * staged + 4]
    u_ref, v_ref, rows_ref = refs[2 * staged + 4 : 2 * staged + 7]
    small = refs[2 * staged + 7 : 2 * staged + 11]
    small_sems, whole_sems = refs[2 * staged + 11 :]
    small_copies = [
        pltpu.make_async_copy(source, target, small_sems.at[index])
        for index, (source, target) in enumerate(zip(small_refs, small))
    ]
    whole_copies = [
        pltpu.make_async_copy(source, target, whole_sems.at[index])
        for index, (source, target) in enumerate(zip(whole_refs, copies_out))
    ]
    for copy in small_copies + whole_copies:
        copy.start()
    for copy in small_copies:
        copy.wait()
    dt_ref, bias_ref, rate_ref, skip_ref = small
    heads, length = dt_ref.shape
    shifted = dt_ref[...].astype(F32) + column_of(bias_ref[...])
    steps = jnp.maximum(shifted, 0.0) + jnp.log1p(jnp.exp(-jnp.abs(shifted)))
    log_decay = -jnp.exp(column_of(rate_ref[...])) * steps
    of = lax.broadcasted_iota(jnp.int32, (length, length), 0)
    at = lax.broadcasted_iota(jnp.int32, (length, length), 1)
    upper = jnp.where(at >= of, 1.0, 0.0).astype(BF16)
    first = log_decay.astype(BF16)
    rest = log_decay - first.astype(F32)
    second = rest.astype(BF16)
    third = (rest - second.astype(F32)).astype(BF16)
    cumulative = dot(first, upper) + dot(second, upper) + dot(third, upper)
    subs = length // SUB
    decays, scales = [], []
    start = jnp.zeros((heads, 1), F32)
    for sub in range(subs):
        rows = slice(sub * SUB, (sub + 1) * SUB)
        inside = cumulative[:, rows] - start
        u_ref[rows, :] = terms_by_row(jnp.exp(inside))
        v_ref[rows, :] = terms_by_row(jnp.exp(-inside) * steps[:, rows])
        end = cumulative[:, (sub + 1) * SUB - 1 : (sub + 1) * SUB]
        decays.append(jnp.exp(end - start))
        scales.append(jnp.exp(start))
        start = end
    lines = decays + scales + [column_of(skip_ref[...]), jnp.exp(start)]
    lane = lax.broadcasted_iota(jnp.int32, (heads, SUB), 1)
    table = jnp.zeros((heads, SUB), F32)
    for index, line in enumerate(lines):
        table = jnp.where(lane == index, line, table)
    rows_ref[...] = terms_by_row(table)[: rows_ref.shape[0]]
    for copy in whole_copies:
        copy.wait()


def groups_kernel(groups, bc_ref, early_ref, taps_ref, gate_ref, left_ref, bt_ref):
    length = bc_ref.shape[0]
    subs = length // SUB
    of = lax.broadcasted_iota(jnp.int32, (SUB, SUB), 1)
    at = lax.broadcasted_iota(jnp.int32, (SUB, SUB), 0)
    causal = at >= of
    for group in range(groups):
        lanes = slice(group * 2 * STATE, (group + 1) * 2 * STATE)
        conv = causal_conv(bc_ref[:, lanes], early_ref[:, lanes], taps_ref[:, group, :])
        b_turned = conv[:, :STATE].astype(F32).T.astype(BF16)
        c_rows = conv[:, STATE:]
        bt_ref[group] = b_turned
        for sub in range(subs):
            rows = slice(sub * SUB, (sub + 1) * SUB)
            scores = jnp.where(causal, dot(c_rows[rows], b_turned[:, rows]), 0.0)
            left_ref[group, rows, :SUB] = scores.astype(BF16)
            left_ref[group, rows, SUB:] = c_rows[rows]


def local_kernel(
    first_head, x_ref, early_ref, taps_ref, z_ref, left_ref, bt_ref, u_ref, v_ref, rows_ref, *refs
):
    part_ref, reach_ref, state_ref, send_ref, lanes_ref = refs[-5:]
    length, width = x_ref.shape
    terms = u_ref.shape[1]
    row = lax.broadcasted_iota(jnp.int32, (terms, width), 0)
    lane = lax.broadcasted_iota(jnp.int32, (terms, width), 1)
    heads = terms // 2
    owner = jnp.where(row >= heads, row - heads, row) - first_head
    spread = jnp.where(
        (lane >= owner * HEAD_DIM) & (lane < (owner + 1) * HEAD_DIM), 1.0, 0.0
    ).astype(BF16)
    lanes = dot(rows_ref[...], spread)
    lanes_ref[...] = lanes
    conv = causal_conv(x_ref[...], early_ref[...], taps_ref[...])
    subs = length // SUB
    skip = lanes[2 * subs : 2 * subs + 1]
    state = None
    for sub in range(subs):
        rows = slice(sub * SUB, (sub + 1) * SUB)
        inputs = conv[rows].astype(F32)
        scaled = (inputs * dot(v_ref[rows], spread)).astype(BF16)
        decay = lanes[sub : sub + 1]
        added = dot(bt_ref[0, :, rows], scaled)
        if sub == 0:
            inner = dot(left_ref[0, rows, :SUB], scaled)
            state = decay * added
        else:
            inner = dot(left_ref[0, rows, :SUB], scaled) + dot(
                left_ref[0, rows, SUB:], state.astype(BF16)
            )
            state = decay * (state + added)
        grown = dot(u_ref[rows], spread)
        gate = silu(z_ref[rows].astype(F32))
        part_ref[rows, :] = gate * (grown * inner + skip * inputs)
        reach_ref[rows, :] = gate * grown * lanes[subs + sub : subs + sub + 1]
    state_ref[...] = state
    send_ref[...] = state.astype(send_ref.dtype)


def combine_kernel(line, lanes_ref, state_ref, arrived_ref, gate_ref, sent_ref):
    total = lanes_ref[line : line + 1]
    joined = total * arrived_ref[...].astype(F32) + state_ref[...]
    sent_ref[...] = joined.astype(sent_ref.dtype)


def absorb_kernel(left_ref, part_ref, reach_ref, before_ref, latest_ref, gate_ref, gated_ref, square_ref):
    length, width = part_ref.shape
    incoming = (before_ref[...].astype(F32) + latest_ref[...].astype(F32)).astype(BF16)
    for start in range(0, length, SUB):
        rows = slice(start, start + SUB)
        value = part_ref[rows] + reach_ref[rows] * dot(left_ref[0, rows, SUB:], incoming)
        gated_ref[rows, :] = value
        power = value * value
        total = power[:, :128]
        for lane in range(128, width, 128):
            total = total + power[:, lane : lane + 128]
        square_ref[rows, :] = total


def finish_kernel(chunks, *refs):
    gain_ref = refs[0]
    gated = refs[1 : 1 + chunks]
    squares = refs[1 + chunks : 1 + 2 * chunks]
    out_ref = refs[-1]
    width = gated[0].shape[1]
    total = squares[0][...]
    for square in squares[1:]:
        total = total + square[...]
    mean = jnp.sum(total, axis=1, keepdims=True) * (1.0 / (width * chunks))
    scale = lax.rsqrt(mean + 1e-05)
    for index in range(chunks):
        lanes = slice(index * width, (index + 1) * width)
        out_ref[:, lanes] = (gated[index][...] * scale * gain_ref[:, lanes]).astype(BF16)


def whole(shape):
    return pl.BlockSpec(shape, lambda *_: (0,) * len(shape))


def shards(x_in, bc_in, z_in, dt_in, conv_x, conv_bc, dt_bias, a_log, d_skip, norm_gain):
    length, channels = x_in.shape
    groups = bc_in.shape[1]
    heads = channels // HEAD_DIM
    contexts = lax.axis_size("ctx")
    wire = BF16 if contexts <= 8 else F32
    margin = KERNEL - 1
    subs = length // SUB
    ahead = [(i, i + 1) for i in range(contexts - 1)]
    bc_width = groups * 2 * STATE
    bc_flat = lax.optimization_barrier(bc_in.reshape(length, bc_width))
    early = jnp.concatenate([x_in[-margin:], bc_flat[-margin:]], axis=1)
    early = lax.ppermute(early, "ctx", ahead)
    line_rows = -(-(2 * subs + 2) // 8) * 8
    sub_width = SUB + STATE
    staged = (x_in, z_in, conv_x, conv_bc, norm_gain.reshape(1, channels))
    small = (dt_in.T, dt_bias.reshape(1, heads), a_log.reshape(1, heads), d_skip.reshape(1, heads))
    x_in, z_in, taps_x, taps_bc, gain, grow, shrink, lines = pl.pallas_call(
        functools.partial(steps_kernel, len(staged)),
        in_specs=[pl.BlockSpec(memory_space=pltpu.HBM)] * (len(staged) + len(small)),
        out_specs=tuple(pl.BlockSpec(memory_space=pltpu.VMEM) for _ in range(len(staged) + 3)),
        out_shape=tuple(jax.ShapeDtypeStruct(array.shape, array.dtype) for array in staged) + (
            jax.ShapeDtypeStruct((length, 2 * heads), BF16),
            jax.ShapeDtypeStruct((length, 2 * heads), BF16),
            jax.ShapeDtypeStruct((line_rows, 2 * heads), BF16),
        ),
        scratch_shapes=[pltpu.VMEM(array.shape, array.dtype) for array in small] + [
            pltpu.SemaphoreType.DMA((len(small),)), pltpu.SemaphoreType.DMA((len(staged),)),
        ],
        compiler_params=pltpu.CompilerParams(vmem_limit_bytes=12 << 20),
        cost_estimate=pl.CostEstimate(
            flops=6 * heads * length * length, bytes_accessed=8 << 20, transcendentals=1 << 18
        ),
        name="steps",
    )(*[pltpu.with_memory_space_constraint(array, pltpu.HBM) for array in staged + small])
    left, b_turned = pl.pallas_call(
        functools.partial(groups_kernel, groups),
        out_shape=(
            jax.ShapeDtypeStruct((groups, length, sub_width), BF16),
            jax.ShapeDtypeStruct((groups, STATE, length), BF16),
        ),
        grid=(1,),
        in_specs=[
            whole((length, bc_width)),
            pl.BlockSpec((margin, bc_width), lambda i: (0, channels // bc_width)),
            whole((KERNEL, groups, 2 * STATE)), whole((line_rows, 2 * heads)),
        ],
        out_specs=(whole((groups, length, sub_width)), whole((groups, STATE, length))),
        compiler_params=pltpu.CompilerParams(vmem_limit_bytes=12 << 20),
        cost_estimate=pl.CostEstimate(
            flops=4 * groups * length * SUB * STATE, bytes_accessed=4 << 20,
            transcendentals=length * bc_width,
        ),
        name="groups",
    )(bc_flat, early, taps_bc, lines)

    per_group = channels // groups
    in_group = per_group // CHUNK
    count = channels // CHUNK
    token = pl.BlockSpec((8, 128), lambda i: (0, 0))

    def local(chunk, gates):
        group = chunk // in_group

        def column(rows):
            return pl.BlockSpec((rows, CHUNK), lambda i: (0, chunk))

        def grouped(rows, width):
            return pl.BlockSpec((1, rows, width), lambda i: (group, 0, 0))

        return pl.pallas_call(
            functools.partial(local_kernel, chunk * (CHUNK // HEAD_DIM)),
            grid=(1,),
            in_specs=[
                column(length), column(margin), column(KERNEL), column(length),
                grouped(length, sub_width), grouped(STATE, length),
                whole((length, 2 * heads)), whole((length, 2 * heads)),
                whole((line_rows, 2 * heads)),
            ] + [token] * len(gates),
            out_specs=[
                whole((length, CHUNK)), whole((length, CHUNK)), whole((STATE, CHUNK)),
                whole((STATE, CHUNK)), whole((line_rows, CHUNK)),
            ],
            out_shape=(
                jax.ShapeDtypeStruct((length, CHUNK), F32),
                jax.ShapeDtypeStruct((length, CHUNK), F32),
                jax.ShapeDtypeStruct((STATE, CHUNK), F32),
                jax.ShapeDtypeStruct((STATE, CHUNK), wire),
                jax.ShapeDtypeStruct((line_rows, CHUNK), F32),
            ),
            compiler_params=pltpu.CompilerParams(vmem_limit_bytes=LOCAL_VMEM),
            cost_estimate=pl.CostEstimate(
                flops=2 * length * CHUNK * 800, bytes_accessed=4 << 20,
                transcendentals=2 * length * CHUNK,
            ),
            name="local",
        )(x_in, early, taps_x, z_in, left, b_turned, grow, shrink, lines, *gates)

    def combine(lanes, state, came, gate):
        return pl.pallas_call(
            functools.partial(combine_kernel, 2 * subs + 1),
            grid=(1,),
            in_specs=[whole((line_rows, CHUNK)), whole((STATE, CHUNK)), whole((STATE, CHUNK)), token],
            out_specs=whole((STATE, CHUNK)),
            out_shape=jax.ShapeDtypeStruct((STATE, CHUNK), wire),
            compiler_params=pltpu.CompilerParams(vmem_limit_bytes=4 << 20),
            cost_estimate=pl.CostEstimate(
                flops=2 * STATE * CHUNK, bytes_accessed=1 << 20, transcendentals=0
            ),
            name="combine",
        )(lanes, state, came, gate)

    def absorb(chunk, before, latest, gate):
        group = chunk // in_group
        part, reach = pieces[chunk][:2]
        return pl.pallas_call(
            absorb_kernel,
            grid=(1,),
            in_specs=[
                pl.BlockSpec((1, length, sub_width), lambda i: (group, 0, 0)),
                whole((length, CHUNK)), whole((length, CHUNK)),
                whole((STATE, CHUNK)), whole((STATE, CHUNK)), token,
            ],
            out_specs=(whole((length, CHUNK)), whole((length, 128))),
            out_shape=(
                jax.ShapeDtypeStruct((length, CHUNK), F32),
                jax.ShapeDtypeStruct((length, 128), F32),
            ),
            compiler_params=pltpu.CompilerParams(vmem_limit_bytes=8 << 20),
            cost_estimate=pl.CostEstimate(
                flops=2 * length * CHUNK * STATE, bytes_accessed=3 << 20, transcendentals=0
            ),
            name="absorb",
        )(left, part, reach, before, latest, gate)

    def finish(group, done, out, gate):
        rows = SUB
        tall = pl.BlockSpec((rows, CHUNK), lambda i: (i, 0))
        thin = pl.BlockSpec((rows, 128), lambda i: (i, 0))
        operands = [gain] + [pair[0] for pair in done] + [pair[1] for pair in done] + [gate]
        specs = [pl.BlockSpec((1, per_group), lambda i: (0, group))]
        specs += [tall] * in_group + [thin] * in_group + [token]
        aliases = {}
        if out is not None:
            aliases = {len(operands): 0}
            operands.append(out)
            specs.append(pl.BlockSpec(memory_space=pl.ANY))
        return pl.pallas_call(
            functools.partial(finish_kernel, in_group),
            grid=(length // rows,),
            in_specs=specs,
            out_specs=pl.BlockSpec((rows, per_group), lambda i: (i, group)),
            out_shape=jax.ShapeDtypeStruct((length, channels), BF16),
            input_output_aliases=aliases,
            compiler_params=pltpu.CompilerParams(vmem_limit_bytes=12 << 20),
            cost_estimate=pl.CostEstimate(
                flops=4 * length * per_group, bytes_accessed=4 << 20, transcendentals=length
            ),
            name="finish",
        )(*operands)

    hops = contexts - 1
    pieces, done = [], []
    arrived = [[] for _ in range(hops)]
    gate, out = None, None
    for step in range(count + LAG * hops):
        if step < count:
            piece = local(step, [] if gate is None else [gate])
            pieces.append(piece)
            gate = piece[4]
            arrived[0].append(lax.ppermute(piece[3], "ctx", [(0, 1)]))
        for hop in range(1, hops):
            chunk = step - LAG * hop
            if 0 <= chunk < count:
                state, lanes = pieces[chunk][2], pieces[chunk][4]
                gate = combine(lanes, state, arrived[hop - 1][chunk], gate)
                arrived[hop].append(lax.ppermute(gate, "ctx", [(hop, hop + 1)]))
        chunk = step - LAG * hops
        if 0 <= chunk < count:
            before = arrived[0][chunk]
            for hop in range(1, hops - 1):
                before = before + arrived[hop][chunk]
            latest = arrived[-1][chunk] if hops > 1 else jnp.zeros_like(before)
            done.append(absorb(chunk, before, latest, gate))
            gate = done[-1][1]
            if (chunk + 1) % in_group == 0:
                group = chunk // in_group
                out = finish(group, done[group * in_group :], out, gate)
    return out


def solution(mesh):
    placed = (
        P(("groups", "ctx"), ("tp", "fsdp")),
        P(("groups", "ctx"), ("tp", "fsdp"), None),
        P(("groups", "ctx"), ("tp", "fsdp")),
        P(("groups", "ctx"), ("tp", "fsdp")),
        P(None, ("tp", "fsdp")),
        P(None, ("tp", "fsdp"), None),
        P(("tp", "fsdp")),
        P(("tp", "fsdp")),
        P(("tp", "fsdp")),
        P(("tp", "fsdp")),
    )
    return jax.shard_map(
        shards,
        mesh=mesh,
        in_specs=placed,
        out_specs=P(("groups", "ctx"), ("tp", "fsdp")),
        check_vma=False,
    )
```

time: 130 us -> 85.8 us (0.66)
  waiting for transfers between devices: 65.3 us -> 35.7 us
  local copies, waits for them, and re-layouts: 16.3 us -> 2.13 us
  Pallas kernels: 20.8 us -> 23.6 us
    ppermute x26 -> x25, waiting for transfers between devices: 65.3 us -> 35.7 us  [the longest x16 34.4 us: shards(): arrived[hop].append(lax.ppermute(gate, 'ctx', [(hop, hop + 1)]))]
    unnamed x27 -> x1, local copies, waits for them, and re-layouts: 15.5 us -> 1.26 us
    pallas_call x11 -> x36, Pallas kernels: 20.8 us -> 23.6 us  [the longest x8 11.4 us: local(): pl.pallas_call(functools.partial(local_kernel, chunk * (CHUNK // HEAD_DIM...]
    ppermute x26 -> x25, starting transfers between devices: 23.9 us -> 22.6 us  [the longest x16 15.9 us: shards(): arrived[hop].append(lax.ppermute(gate, 'ctx', [(hop, hop + 1)]))]
  transfers between devices with their start and end apart: 26 -> 25, of which waited for: 8 -> 9; matrix products, arithmetic and copies ran while one was open for 6% -> 1% of each run, Pallas kernels for 13% -> 22%
where the time goes in v2:
time: 85.8 us; the launch traced here: 85.2 us
  waiting for transfers between devices  35.7 us (42%)
  Pallas kernels  23.6 us (28%)
  starting transfers between devices  22.6 us (26%)
  local copies, waits for them, and re-layouts  2.13 us (2%)
    ppermute x16, waiting for transfers between devices, shards(): arrived[hop].append(lax.ppermute(gate, 'ctx', [(hop, hop + 1)]))  34.4 us
    ppermute x16, starting transfers between devices, shards(): arrived[hop].append(lax.ppermute(gate, 'ctx', [(hop, hop + 1)]))  15.9 us
    pallas_call x8, Pallas kernels, local(): pl.pallas_call(functools.partial(local_kernel, chunk * (CHUNK // HEAD_DIM...  11.4 us
    ppermute x8, starting transfers between devices, shards(): arrived[0].append(lax.ppermute(piece[3], 'ctx', [(0, 1)]))  5.42 us
    pallas_call x2, Pallas kernels, finish(): pl.pallas_call(functools.partial(finish_kernel, in_group), grid=(length /...  3.96 us
    pallas_call x1, Pallas kernels, shards(): pl.pallas_call(functools.partial(steps_kernel, len(staged)), in_specs=[pl...  3.34 us
    pallas_call x8, Pallas kernels, absorb(): pl.pallas_call(absorb_kernel, grid=(1,), in_specs=[pl.BlockSpec((1, lengt...  2.48 us
  transfers between devices with their start and end apart: 25, of which 9 were waited for; matrix products, arithmetic and copies ran while one was open for 1% of the time, Pallas kernels for 22%

profile of v2, /device:TPU:28, one launch (start us, length us, event | category | flops | bytes accessed | tf_op | source)
XLA Modules:
  0.0 85.2 jit_solution(1731115457634229052)
XLA Ops:
  0.0 0.9 %slice.6 = bf16[3,4096]{1,0:T(4,128)(2,1)S(1)} slice(bf16[384,4096]{1,0:T(8,128)(2,1)} %refs_0_.1), slice={[381:384], [0:4096]} | slice | bytes 49152 | tf_op jit(solution)/shard_map/slice | solution.py:226
  0.9 1.3 %copy.12 = bf16[48,8,2,512]{3,1,2,0:T(8,128)(2,1)S(1)} copy(bf16[48,8,2,512]{3,2,1,0:T(2,128)(2,1)} %bitcast.9) | data formatting | bytes 1572864
  2.2 1.3 %collective-permute-start = (bf16[3,5120]{1,0:T(4,128)(2,1)S(1)}, bf16[3,5120]{1,0:T(4,128)(2,1)S(1)}, u32[]{:S(2)}, u32[]{:S(2)}) collective-permute-start(bf16[3,5120]{1,0:T(4,128)(2,1)S(1)} %pad_maximum_fusion), channel_id=1, source_target_pairs={{0,4},{4,8},{8,12},{1,5},{5,9},{9,13},{2,6},{6,10},{10,14},{3,7},{... | collective-permute-start | bytes 92168 | tf_op jit(solution)/shard_map/ppermute | solution.py:227
  3.5 3.3 %steps.1 = (bf16[384,4096]{1,0:T(8,128)(2,1)S(1)}, bf16[384,4096]{1,0:T(8,128)(2,1)S(1)}, f32[4,4096]{1,0:T(4,128)S(1)}, f32[4,2,512]{2,1,0:T(2,128)S(1)}, f32[1...) custom-call(bf16[384,4096]{1,0:T(8,128)(2,1)} %refs_0_.1, ...), custom_call_target="tpu_custom_call" | custom-call | flops 56623104 | bytes 8388608 | tf_op jit(solution)/shard_map/steps/pallas_call | solution.py:232
  6.8 1.2 %collective-permute-done.early_ref = bf16[3,5120]{1,0:T(4,128)(2,1)S(1)} collective-permute-done((bf16[3,5120]{1,0:T(4,128)(2,1)S(1)}, bf16[3,5120]{1,0:T(4,128)(2,1)S(1)}, u32[]{:S(2)}, u32[]{:S(2)}) %collective-permute-start) | collective-permute-done | bytes 30752 | tf_op jit(solution)/shard_map/ppermute | solution.py:227
  8.1 1.2 %groups.1 = (bf16[2,384,384]{2,1,0:T(8,128)(2,1)S(1)}, bf16[2,256,384]{2,1,0:T(8,128)(2,1)S(1)}) custom-call(bf16[384,1024]{1,0:T(8,128)(2,1)S(1)} %bitcast.8, bf16[3,5120]{1,0:T(4,128)(2,1)S(1)} %collective-permute-done.early_ref, f32[4,2,512]{2,1,0:T(2,128)S(1)} %get-tuple-element.72.taps_ref, bf16[8,128]{1,0:T(8,128)(2,1)S(1)} %get-tuple-element.73.gate_ref.rows_ref), custom_call_target="tpu_custom_call" | custom-call | flops 100663296 | bytes 4194304 | tf_op jit(solution)/shard_map/groups/pallas_call | solution.py:250
  9.3 1.4 %local.8 = (f32[384,512]{1,0:T(8,128)S(1)}, f32[384,512]{1,0:T(8,128)S(1)}, f32[256,512]{1,0:T(8,128)S(1)}, bf16[256,512]{1,0:T(8,128)(2,1)S(1)}, f32[8,512]{1,0:T(8,128)S(1)}) custom-call(bf16[384,4096]{1,0:T(8,128)(2,1)S(1)} %get-tuple-element.75.x_ref, bf16[3,5120]{1,0:T(4,128)(2,1)S(1)} %collective-permute-done.early_ref, ...), custom_call_target="tpu_custom_call" | custom-call | flops 314572800 | bytes 4194304 | tf_op jit(solution)/shard_map/local/pallas_call | solution.py:285
  11.4 1.4 %local.9 = (f32[384,512]{1,0:T(8,128)S(1)}, f32[384,512]{1,0:T(8,128)S(1)}, f32[256,512]{1,0:T(8,128)S(1)}, bf16[256,512]{1,0:T(8,128)(2,1)S(1)}, f32[8,512]{1,0:T(8,128)S(1)}) custom-call(bf16[384,4096]{1,0:T(8,128)(2,1)S(1)} %get-tuple-element.75.x_ref, bf16[3,5120]{1,0:T(4,128)(2,1)S(1)} %collective-permute-done.early_ref, ...), custom_call_target="tpu_custom_call" | custom-call | flops 314572800 | bytes 4194304 | tf_op jit(solution)/shard_map/local/pallas_call | solution.py:285
  14.3 1.4 %local.10 = (f32[384,512]{1,0:T(8,128)S(1)}, f32[384,512]{1,0:T(8,128)S(1)}, f32[256,512]{1,0:T(8,128)S(1)}, bf16[256,512]{1,0:T(8,128)(2,1)S(1)}, f32[8,512]{1,0:T(8,128)S(1)}) custom-call(bf16[384,4096]{1,0:T(8,128)(2,1)S(1)} %get-tuple-element.75.x_ref, bf16[3,5120]{1,0:T(4,128)(2,1)S(1)} %collective-permute-done.early_ref, ...), custom_call_target="tpu_custom_call" | custom-call | flops 314572800 | bytes 4194304 | tf_op jit(solution)/shard_map/local/pallas_call | solution.py:285
  17.3 1.3 %collective-permute-start.4 = (bf16[256,512]{1,0:T(8,128)(2,1)S(1)}, bf16[256,512]{1,0:T(8,128)(2,1)S(1)}, u32[]{:S(2)}, u32[]{:S(2)}) collective-permute-start(bf16[256,512]{1,0:T(8,128)(2,1)S(1)} %combine.18.refs_0_), channel_id=1, source_target_pairs={{8,12},{9,13},{10,14},{11,15},{24,28},{25,29},{26,30},{27,31}} | collective-permute-start | bytes 786440 | tf_op jit(solution)/shard_map/ppermute | solution.py:391
  18.6 1.4 %local.11 = (f32[384,512]{1,0:T(8,128)S(1)}, f32[384,512]{1,0:T(8,128)S(1)}, f32[256,512]{1,0:T(8,128)S(1)}, bf16[256,512]{1,0:T(8,128)(2,1)S(1)}, f32[8,512]{1,0:T(8,128)S(1)}) custom-call(bf16[384,4096]{1,0:T(8,128)(2,1)S(1)} %get-tuple-element.75.x_ref, bf16[3,5120]{1,0:T(4,128)(2,1)S(1)} %collective-permute-done.early_ref, ...), custom_call_target="tpu_custom_call" | custom-call | flops 314572800 | bytes 4194304 | tf_op jit(solution)/shard_map/local/pallas_call | solution.py:285
  21.6 1.3 %collective-permute-start.8 = (bf16[256,512]{1,0:T(8,128)(2,1)S(1)}, bf16[256,512]{1,0:T(8,128)(2,1)S(1)}, u32[]{:S(2)}, u32[]{:S(2)}) collective-permute-start(bf16[256,512]{1,0:T(8,128)(2,1)S(1)} %combine.20.gate_ref), channel_id=1, source_target_pairs={{8,12},{9,13},{10,14},{11,15},{24,28},{25,29},{26,30},{27,31}} | collective-permute-start | bytes 786440 | tf_op jit(solution)/shard_map/ppermute | solution.py:391
  23.0 12.7 %collective-permute-done.4.latest_ref = bf16[256,512]{1,0:T(8,128)(2,1)S(1)} collective-permute-done((bf16[256,512]{1,0:T(8,128)(2,1)S(1)}, bf16[256,512]{1,0:T(8,128)(2,1)S(1)}, u32[]{:S(2)}, u32[]{:S(2)}) %collective-permute-start.4) | collective-permute-done | bytes 262176 | tf_op jit(solution)/shard_map/ppermute | solution.py:391
  36.1 1.4 %local.12 = (f32[384,512]{1,0:T(8,128)S(1)}, f32[384,512]{1,0:T(8,128)S(1)}, f32[256,512]{1,0:T(8,128)S(1)}, bf16[256,512]{1,0:T(8,128)(2,1)S(1)}, f32[8,512]{1,0:T(8,128)S(1)}) custom-call(bf16[384,4096]{1,0:T(8,128)(2,1)S(1)} %get-tuple-element.75.x_ref, bf16[3,5120]{1,0:T(4,128)(2,1)S(1)} %collective-permute-done.early_ref, ...), custom_call_target="tpu_custom_call" | custom-call | flops 314572800 | bytes 4194304 | tf_op jit(solution)/shard_map/local/pallas_call | solution.py:285
  39.1 1.5 %collective-permute-start.13 = (bf16[256,512]{1,0:T(8,128)(2,1)S(1)}, bf16[256,512]{1,0:T(8,128)(2,1)S(1)}, u32[]{:S(2)}, u32[]{:S(2)}) collective-permute-start(bf16[256,512]{1,0:T(8,128)(2,1)S(1)} %combine.22.gate_ref), channel_id=1, source_target_pairs={{8,12},{9,13},{10,14},{11,15},{24,28},{25,29},{26,30},{27,31}} | collective-permute-start | bytes 786440 | tf_op jit(solution)/shard_map/ppermute | solution.py:391
  40.6 1.7 %collective-permute-done.8.latest_ref = bf16[256,512]{1,0:T(8,128)(2,1)S(1)} collective-permute-done((bf16[256,512]{1,0:T(8,128)(2,1)S(1)}, bf16[256,512]{1,0:T(8,128)(2,1)S(1)}, u32[]{:S(2)}, u32[]{:S(2)}) %collective-permute-start.8) | collective-permute-done | bytes 262176 | tf_op jit(solution)/shard_map/ppermute | solution.py:391
  42.6 1.4 %local.13 = (f32[384,512]{1,0:T(8,128)S(1)}, f32[384,512]{1,0:T(8,128)S(1)}, f32[256,512]{1,0:T(8,128)S(1)}, bf16[256,512]{1,0:T(8,128)(2,1)S(1)}, f32[8,512]{1,0:T(8,128)S(1)}) custom-call(bf16[384,4096]{1,0:T(8,128)(2,1)S(1)} %get-tuple-element.75.x_ref, bf16[3,5120]{1,0:T(4,128)(2,1)S(1)} %collective-permute-done.early_ref, ...), custom_call_target="tpu_custom_call" | custom-call | flops 314572800 | bytes 4194304 | tf_op jit(solution)/shard_map/local/pallas_call | solution.py:285
  45.6 1.3 %collective-permute-start.18 = (bf16[256,512]{1,0:T(8,128)(2,1)S(1)}, bf16[256,512]{1,0:T(8,128)(2,1)S(1)}, u32[]{:S(2)}, u32[]{:S(2)}) collective-permute-start(bf16[256,512]{1,0:T(8,128)(2,1)S(1)} %combine.24.gate_ref), channel_id=1, source_target_pairs={{8,12},{9,13},{10,14},{11,15},{24,28},{25,29},{26,30},{27,31}} | collective-permute-start | bytes 786440 | tf_op jit(solution)/shard_map/ppermute | solution.py:391
  47.0 1.2 %collective-permute-done.13.latest_ref = bf16[256,512]{1,0:T(8,128)(2,1)S(1)} collective-permute-done((bf16[256,512]{1,0:T(8,128)(2,1)S(1)}, bf16[256,512]{1,0:T(8,128)(2,1)S(1)}, u32[]{:S(2)}, u32[]{:S(2)}) %collective-permute-start.13) | collective-permute-done | bytes 262176 | tf_op jit(solution)/shard_map/ppermute | solution.py:391
  48.5 1.4 %local.14 = (f32[384,512]{1,0:T(8,128)S(1)}, f32[384,512]{1,0:T(8,128)S(1)}, f32[256,512]{1,0:T(8,128)S(1)}, bf16[256,512]{1,0:T(8,128)(2,1)S(1)}, f32[8,512]{1,0:T(8,128)S(1)}) custom-call(bf16[384,4096]{1,0:T(8,128)(2,1)S(1)} %get-tuple-element.75.x_ref, bf16[3,5120]{1,0:T(4,128)(2,1)S(1)} %collective-permute-done.early_ref, ...), custom_call_target="tpu_custom_call" | custom-call | flops 314572800 | bytes 4194304 | tf_op jit(solution)/shard_map/local/pallas_call | solution.py:285
  51.5 1.3 %collective-permute-start.15 = (bf16[256,512]{1,0:T(8,128)(2,1)S(1)}, bf16[256,512]{1,0:T(8,128)(2,1)S(1)}, u32[]{:S(2)}, u32[]{:S(2)}) collective-permute-start(bf16[256,512]{1,0:T(8,128)(2,1)S(1)} %combine.26.gate_ref), channel_id=1, source_target_pairs={{8,12},{9,13},{10,14},{11,15},{24,28},{25,29},{26,30},{27,31}} | collective-permute-start | bytes 786440 | tf_op jit(solution)/shard_map/ppermute | solution.py:391
  52.8 3.5 %collective-permute-done.18.latest_ref = bf16[256,512]{1,0:T(8,128)(2,1)S(1)} collective-permute-done((bf16[256,512]{1,0:T(8,128)(2,1)S(1)}, bf16[256,512]{1,0:T(8,128)(2,1)S(1)}, u32[]{:S(2)}, u32[]{:S(2)}) %collective-permute-start.18) | collective-permute-done | bytes 262176 | tf_op jit(solution)/shard_map/ppermute | solution.py:391
  56.6 1.4 %local.15 = (f32[384,512]{1,0:T(8,128)S(1)}, f32[384,512]{1,0:T(8,128)S(1)}, f32[256,512]{1,0:T(8,128)S(1)}, bf16[256,512]{1,0:T(8,128)(2,1)S(1)}, f32[8,512]{1,0:T(8,128)S(1)}) custom-call(bf16[384,4096]{1,0:T(8,128)(2,1)S(1)} %get-tuple-element.75.x_ref, bf16[3,5120]{1,0:T(4,128)(2,1)S(1)} %collective-permute-done.early_ref, ...), custom_call_target="tpu_custom_call" | custom-call | flops 314572800 | bytes 4194304 | tf_op jit(solution)/shard_map/local/pallas_call | solution.py:285
  59.6 1.3 %collective-permute-start.19 = (bf16[256,512]{1,0:T(8,128)(2,1)S(1)}, bf16[256,512]{1,0:T(8,128)(2,1)S(1)}, u32[]{:S(2)}, u32[]{:S(2)}) collective-permute-start(bf16[256,512]{1,0:T(8,128)(2,1)S(1)} %combine.28.gate_ref), channel_id=1, source_target_pairs={{8,12},{9,13},{10,14},{11,15},{24,28},{25,29},{26,30},{27,31}} | collective-permute-start | bytes 786440 | tf_op jit(solution)/shard_map/ppermute | solution.py:391
  61.0 1.3 %collective-permute-done.15.latest_ref = bf16[256,512]{1,0:T(8,128)(2,1)S(1)} collective-permute-done((bf16[256,512]{1,0:T(8,128)(2,1)S(1)}, bf16[256,512]{1,0:T(8,128)(2,1)S(1)}, u32[]{:S(2)}, u32[]{:S(2)}) %collective-permute-start.15) | collective-permute-done | bytes 262176 | tf_op jit(solution)/shard_map/ppermute | solution.py:391
  63.5 1.3 %collective-permute-start.22 = (bf16[256,512]{1,0:T(8,128)(2,1)S(1)}, bf16[256,512]{1,0:T(8,128)(2,1)S(1)}, u32[]{:S(2)}, u32[]{:S(2)}) collective-permute-start(bf16[256,512]{1,0:T(8,128)(2,1)S(1)} %combine.30.gate_ref), channel_id=1, source_target_pairs={{8,12},{9,13},{10,14},{11,15},{24,28},{25,29},{26,30},{27,31}} | collective-permute-start | bytes 786440 | tf_op jit(solution)/shard_map/ppermute | solution.py:391
  64.8 4.0 %collective-permute-done.19.latest_ref = bf16[256,512]{1,0:T(8,128)(2,1)S(1)} collective-permute-done((bf16[256,512]{1,0:T(8,128)(2,1)S(1)}, bf16[256,512]{1,0:T(8,128)(2,1)S(1)}, u32[]{:S(2)}, u32[]{:S(2)}) %collective-permute-start.19) | collective-permute-done | bytes 262176 | tf_op jit(solution)/shard_map/ppermute | solution.py:391
  69.2 1.3 %collective-permute-start.24 = (bf16[256,512]{1,0:T(8,128)(2,1)S(1)}, bf16[256,512]{1,0:T(8,128)(2,1)S(1)}, u32[]{:S(2)}, u32[]{:S(2)}) collective-permute-start(bf16[256,512]{1,0:T(8,128)(2,1)S(1)} %combine.31.gate_ref), channel_id=1, source_target_pairs={{8,12},{9,13},{10,14},{11,15},{24,28},{25,29},{26,30},{27,31}} | collective-permute-start | bytes 786440 | tf_op jit(solution)/shard_map/ppermute | solution.py:391
  70.5 2.0 %finish.2.refs_10_ = bf16[384,4096]{1,0:T(8,128)(2,1)} custom-call(f32[1,4096]{1,0:T(1,128)S(1)} %get-tuple-element.71.refs_0_, f32[384,512]{1,0:T(8,128)S(1)} %get-tuple-element.133.refs_1_, f32[384,512]{1,0:T(8,128)S(1)} %get-tuple-element.134.refs_2_, f32[384,512]{1,0:T(8,128)S(1)} %get-tuple-element.135.refs_3_, ...), custom_call_target="tpu_custom_call" | custom-call | flops 3145728 | bytes 4194304 | tf_op jit(solution)/shard_map/finish/pallas_call | solution.py:362
  72.7 7.5 %collective-permute-done.22.latest_ref = bf16[256,512]{1,0:T(8,128)(2,1)S(1)} collective-permute-done((bf16[256,512]{1,0:T(8,128)(2,1)S(1)}, bf16[256,512]{1,0:T(8,128)(2,1)S(1)}, u32[]{:S(2)}, u32[]{:S(2)}) %collective-permute-start.22) | collective-permute-done | bytes 262176 | tf_op jit(solution)/shard_map/ppermute | solution.py:391
  80.5 2.5 %collective-permute-done.24.latest_ref = bf16[256,512]{1,0:T(8,128)(2,1)S(1)} collective-permute-done((bf16[256,512]{1,0:T(8,128)(2,1)S(1)}, bf16[256,512]{1,0:T(8,128)(2,1)S(1)}, u32[]{:S(2)}, u32[]{:S(2)}) %collective-permute-start.24) | collective-permute-done | bytes 262176 | tf_op jit(solution)/shard_map/ppermute | solution.py:391
  83.3 2.0 %finish.3 = bf16[384,4096]{1,0:T(8,128)(2,1)} custom-call(f32[1,4096]{1,0:T(1,128)S(1)} %get-tuple-element.71.refs_0_, f32[384,512]{1,0:T(8,128)S(1)} %get-tuple-element.117.refs_1_, f32[384,512]{1,0:T(8,128)S(1)} %get-tuple-element.123.refs_2_, f32[384,512]{1,0:T(8,128)S(1)} %get-tuple-element.127.refs_3_, ...), custom_call_target="tpu_custom_call", output_to_operand_aliasing={{}: (10, {})} | custom-call | flops 3145728 | bytes 4194304 | tf_op jit(solution)/shard_map/finish/pallas_call | solution.py:362
  (66 shorter events, 15.1 us)
Async XLA Ops:
  2.2 5.9 %collective-permute-start = (bf16[3,5120]{1,0:T(4,128)(2,1)S(1)}, bf16[3,5120]{1,0:T(4,128)(2,1)S(1)}, u32[]{:S(2)}, u32[]{:S(2)}) collective-permute-start(bf16[3,5120]{1,0:T(4,128)(2,1)S(1)} %pad_maximum_fusion), channel_id=1, source_target_pairs={{0,4},{4,8},{8,12},{1,5},{5,9},{9,13},{2,6},{6,10},{10,14},{3,7},{... | collective-permute-start | bytes 92168 | tf_op jit(solution)/shard_map/ppermute | solution.py:227
  10.7 2.8 %collective-permute-start.1 = (bf16[256,512]{1,0:T(8,128)(2,1)S(1)}, bf16[256,512]{1,0:T(8,128)(2,1)S(1)}, u32[]{:S(2)}, u32[]{:S(2)}) collective-permute-start(bf16[256,512]{1,0:T(8,128)(2,1)S(1)} %get-tuple-element.83), channel_id=1, source_target_pairs={{0,4},{1,5},{2,6},{3,7},{16,20},{17,21},{18,22},{19,23}} | collective-permute-start | bytes 786440 | tf_op jit(solution)/shard_map/ppermute | solution.py:385
  12.9 3.6 %collective-permute-start.3 = (bf16[256,512]{1,0:T(8,128)(2,1)S(1)}, bf16[256,512]{1,0:T(8,128)(2,1)S(1)}, u32[]{:S(2)}, u32[]{:S(2)}) collective-permute-start(bf16[256,512]{1,0:T(8,128)(2,1)S(1)} %get-tuple-element.88), channel_id=1, source_target_pairs={{0,4},{1,5},{2,6},{3,7},{16,20},{17,21},{18,22},{19,23}} | collective-permute-start | bytes 786440 | tf_op jit(solution)/shard_map/ppermute | solution.py:385
  13.6 3.6 %collective-permute-start.2 = (bf16[256,512]{1,0:T(8,128)(2,1)S(1)}, bf16[256,512]{1,0:T(8,128)(2,1)S(1)}, u32[]{:S(2)}, u32[]{:S(2)}) collective-permute-start(bf16[256,512]{1,0:T(8,128)(2,1)S(1)} %combine.16.refs_0_), channel_id=1, source_target_pairs={{4,8},{5,9},{6,10},{7,11},{20,24},{21,25},{22,26},{23,27}} | collective-permute-start | bytes 786440 | tf_op jit(solution)/shard_map/ppermute | solution.py:391
  15.8 5.0 %collective-permute-start.6 = (bf16[256,512]{1,0:T(8,128)(2,1)S(1)}, bf16[256,512]{1,0:T(8,128)(2,1)S(1)}, u32[]{:S(2)}, u32[]{:S(2)}) collective-permute-start(bf16[256,512]{1,0:T(8,128)(2,1)S(1)} %get-tuple-element.91), channel_id=1, source_target_pairs={{0,4},{1,5},{2,6},{3,7},{16,20},{17,21},{18,22},{19,23}} | collective-permute-start | bytes 786440 | tf_op jit(solution)/shard_map/ppermute | solution.py:385
  16.6 5.0 %collective-permute-start.5 = (bf16[256,512]{1,0:T(8,128)(2,1)S(1)}, bf16[256,512]{1,0:T(8,128)(2,1)S(1)}, u32[]{:S(2)}, u32[]{:S(2)}) collective-permute-start(bf16[256,512]{1,0:T(8,128)(2,1)S(1)} %combine.17.gate_ref), channel_id=1, source_target_pairs={{4,8},{5,9},{6,10},{7,11},{20,24},{21,25},{22,26},{23,27}} | collective-permute-start | bytes 786440 | tf_op jit(solution)/shard_map/ppermute | solution.py:391
  17.3 18.4 %collective-permute-start.4 = (bf16[256,512]{1,0:T(8,128)(2,1)S(1)}, bf16[256,512]{1,0:T(8,128)(2,1)S(1)}, u32[]{:S(2)}, u32[]{:S(2)}) collective-permute-start(bf16[256,512]{1,0:T(8,128)(2,1)S(1)} %combine.18.refs_0_), channel_id=1, source_target_pairs={{8,12},{9,13},{10,14},{11,15},{24,28},{25,29},{26,30},{27,31}} | collective-permute-start | bytes 786440 | tf_op jit(solution)/shard_map/ppermute | solution.py:391
  20.1 18.1 %collective-permute-start.10 = (bf16[256,512]{1,0:T(8,128)(2,1)S(1)}, bf16[256,512]{1,0:T(8,128)(2,1)S(1)}, u32[]{:S(2)}, u32[]{:S(2)}) collective-permute-start(bf16[256,512]{1,0:T(8,128)(2,1)S(1)} %get-tuple-element.102), channel_id=1, source_target_pairs={{0,4},{1,5},{2,6},{3,7},{16,20},{17,21},{18,22},{19,23}} | collective-permute-start | bytes 786440 | tf_op jit(solution)/shard_map/ppermute | solution.py:385
  20.9 18.2 %collective-permute-start.9 = (bf16[256,512]{1,0:T(8,128)(2,1)S(1)}, bf16[256,512]{1,0:T(8,128)(2,1)S(1)}, u32[]{:S(2)}, u32[]{:S(2)}) collective-permute-start(bf16[256,512]{1,0:T(8,128)(2,1)S(1)} %combine.19.gate_ref), channel_id=1, source_target_pairs={{4,8},{5,9},{6,10},{7,11},{20,24},{21,25},{22,26},{23,27}} | collective-permute-start | bytes 786440 | tf_op jit(solution)/shard_map/ppermute | solution.py:391
  21.6 20.7 %collective-permute-start.8 = (bf16[256,512]{1,0:T(8,128)(2,1)S(1)}, bf16[256,512]{1,0:T(8,128)(2,1)S(1)}, u32[]{:S(2)}, u32[]{:S(2)}) collective-permute-start(bf16[256,512]{1,0:T(8,128)(2,1)S(1)} %combine.20.gate_ref), channel_id=1, source_target_pairs={{8,12},{9,13},{10,14},{11,15},{24,28},{25,29},{26,30},{27,31}} | collective-permute-start | bytes 786440 | tf_op jit(solution)/shard_map/ppermute | solution.py:391
  37.5 7.3 %collective-permute-start.7 = (bf16[256,512]{1,0:T(8,128)(2,1)S(1)}, bf16[256,512]{1,0:T(8,128)(2,1)S(1)}, u32[]{:S(2)}, u32[]{:S(2)}) collective-permute-start(bf16[256,512]{1,0:T(8,128)(2,1)S(1)} %get-tuple-element.96), channel_id=1, source_target_pairs={{0,4},{1,5},{2,6},{3,7},{16,20},{17,21},{18,22},{19,23}} | collective-permute-start | bytes 786440 | tf_op jit(solution)/shard_map/ppermute | solution.py:385
  38.3 7.2 %collective-permute-start.14 = (bf16[256,512]{1,0:T(8,128)(2,1)S(1)}, bf16[256,512]{1,0:T(8,128)(2,1)S(1)}, u32[]{:S(2)}, u32[]{:S(2)}) collective-permute-start(bf16[256,512]{1,0:T(8,128)(2,1)S(1)} %combine.21.gate_ref), channel_id=1, source_target_pairs={{4,8},{5,9},{6,10},{7,11},{20,24},{21,25},{22,26},{23,27}} | collective-permute-start | bytes 786440 | tf_op jit(solution)/shard_map/ppermute | solution.py:391
  39.1 9.0 %collective-permute-start.13 = (bf16[256,512]{1,0:T(8,128)(2,1)S(1)}, bf16[256,512]{1,0:T(8,128)(2,1)S(1)}, u32[]{:S(2)}, u32[]{:S(2)}) collective-permute-start(bf16[256,512]{1,0:T(8,128)(2,1)S(1)} %combine.22.gate_ref), channel_id=1, source_target_pairs={{8,12},{9,13},{10,14},{11,15},{24,28},{25,29},{26,30},{27,31}} | collective-permute-start | bytes 786440 | tf_op jit(solution)/shard_map/ppermute | solution.py:391
  44.1 5.8 %collective-permute-start.12 = (bf16[256,512]{1,0:T(8,128)(2,1)S(1)}, bf16[256,512]{1,0:T(8,128)(2,1)S(1)}, u32[]{:S(2)}, u32[]{:S(2)}) collective-permute-start(bf16[256,512]{1,0:T(8,128)(2,1)S(1)} %get-tuple-element.106), channel_id=1, source_target_pairs={{0,4},{1,5},{2,6},{3,7},{16,20},{17,21},{18,22},{19,23}} | collective-permute-start | bytes 786440 | tf_op jit(solution)/shard_map/ppermute | solution.py:385
  44.8 6.6 %collective-permute-start.11 = (bf16[256,512]{1,0:T(8,128)(2,1)S(1)}, bf16[256,512]{1,0:T(8,128)(2,1)S(1)}, u32[]{:S(2)}, u32[]{:S(2)}) collective-permute-start(bf16[256,512]{1,0:T(8,128)(2,1)S(1)} %combine.23.gate_ref), channel_id=1, source_target_pairs={{4,8},{5,9},{6,10},{7,11},{20,24},{21,25},{22,26},{23,27}} | collective-permute-start | bytes 786440 | tf_op jit(solution)/shard_map/ppermute | solution.py:391
  45.6 10.7 %collective-permute-start.18 = (bf16[256,512]{1,0:T(8,128)(2,1)S(1)}, bf16[256,512]{1,0:T(8,128)(2,1)S(1)}, u32[]{:S(2)}, u32[]{:S(2)}) collective-permute-start(bf16[256,512]{1,0:T(8,128)(2,1)S(1)} %combine.24.gate_ref), channel_id=1, source_target_pairs={{8,12},{9,13},{10,14},{11,15},{24,28},{25,29},{26,30},{27,31}} | collective-permute-start | bytes 786440 | tf_op jit(solution)/shard_map/ppermute | solution.py:391
  50.0 9.5 %collective-permute-start.16 = (bf16[256,512]{1,0:T(8,128)(2,1)S(1)}, bf16[256,512]{1,0:T(8,128)(2,1)S(1)}, u32[]{:S(2)}, u32[]{:S(2)}) collective-permute-start(bf16[256,512]{1,0:T(8,128)(2,1)S(1)} %combine.25.gate_ref), channel_id=1, source_target_pairs={{4,8},{5,9},{6,10},{7,11},{20,24},{21,25},{22,26},{23,27}} | collective-permute-start | bytes 786440 | tf_op jit(solution)/shard_map/ppermute | solution.py:391
  50.7 8.1 %collective-permute-start.17 = (bf16[256,512]{1,0:T(8,128)(2,1)S(1)}, bf16[256,512]{1,0:T(8,128)(2,1)S(1)}, u32[]{:S(2)}, u32[]{:S(2)}) collective-permute-start(bf16[256,512]{1,0:T(8,128)(2,1)S(1)} %get-tuple-element.112), channel_id=1, source_target_pairs={{0,4},{1,5},{2,6},{3,7},{16,20},{17,21},{18,22},{19,23}} | collective-permute-start | bytes 786440 | tf_op jit(solution)/shard_map/ppermute | solution.py:385
  51.5 10.7 %collective-permute-start.15 = (bf16[256,512]{1,0:T(8,128)(2,1)S(1)}, bf16[256,512]{1,0:T(8,128)(2,1)S(1)}, u32[]{:S(2)}, u32[]{:S(2)}) collective-permute-start(bf16[256,512]{1,0:T(8,128)(2,1)S(1)} %combine.26.gate_ref), channel_id=1, source_target_pairs={{8,12},{9,13},{10,14},{11,15},{24,28},{25,29},{26,30},{27,31}} | collective-permute-start | bytes 786440 | tf_op jit(solution)/shard_map/ppermute | solution.py:391
  58.1 4.5 %collective-permute-start.21 = (bf16[256,512]{1,0:T(8,128)(2,1)S(1)}, bf16[256,512]{1,0:T(8,128)(2,1)S(1)}, u32[]{:S(2)}, u32[]{:S(2)}) collective-permute-start(bf16[256,512]{1,0:T(8,128)(2,1)S(1)} %get-tuple-element.121), channel_id=1, source_target_pairs={{0,4},{1,5},{2,6},{3,7},{16,20},{17,21},{18,22},{19,23}} | collective-permute-start | bytes 786440 | tf_op jit(solution)/shard_map/ppermute | solution.py:385
  58.8 4.6 %collective-permute-start.20 = (bf16[256,512]{1,0:T(8,128)(2,1)S(1)}, bf16[256,512]{1,0:T(8,128)(2,1)S(1)}, u32[]{:S(2)}, u32[]{:S(2)}) collective-permute-start(bf16[256,512]{1,0:T(8,128)(2,1)S(1)} %combine.27.gate_ref), channel_id=1, source_target_pairs={{4,8},{5,9},{6,10},{7,11},{20,24},{21,25},{22,26},{23,27}} | collective-permute-start | bytes 786440 | tf_op jit(solution)/shard_map/ppermute | solution.py:391
  59.6 9.2 %collective-permute-start.19 = (bf16[256,512]{1,0:T(8,128)(2,1)S(1)}, bf16[256,512]{1,0:T(8,128)(2,1)S(1)}, u32[]{:S(2)}, u32[]{:S(2)}) collective-permute-start(bf16[256,512]{1,0:T(8,128)(2,1)S(1)} %combine.28.gate_ref), channel_id=1, source_target_pairs={{8,12},{9,13},{10,14},{11,15},{24,28},{25,29},{26,30},{27,31}} | collective-permute-start | bytes 786440 | tf_op jit(solution)/shard_map/ppermute | solution.py:391
  62.6 6.5 %collective-permute-start.23 = (bf16[256,512]{1,0:T(8,128)(2,1)S(1)}, bf16[256,512]{1,0:T(8,128)(2,1)S(1)}, u32[]{:S(2)}, u32[]{:S(2)}) collective-permute-start(bf16[256,512]{1,0:T(8,128)(2,1)S(1)} %combine.29.gate_ref), channel_id=1, source_target_pairs={{4,8},{5,9},{6,10},{7,11},{20,24},{21,25},{22,26},{23,27}} | collective-permute-start | bytes 786440 | tf_op jit(solution)/shard_map/ppermute | solution.py:391
  63.5 16.6 %collective-permute-start.22 = (bf16[256,512]{1,0:T(8,128)(2,1)S(1)}, bf16[256,512]{1,0:T(8,128)(2,1)S(1)}, u32[]{:S(2)}, u32[]{:S(2)}) collective-permute-start(bf16[256,512]{1,0:T(8,128)(2,1)S(1)} %combine.30.gate_ref), channel_id=1, source_target_pairs={{8,12},{9,13},{10,14},{11,15},{24,28},{25,29},{26,30},{27,31}} | collective-permute-start | bytes 786440 | tf_op jit(solution)/shard_map/ppermute | solution.py:391
  69.2 13.7 %collective-permute-start.24 = (bf16[256,512]{1,0:T(8,128)(2,1)S(1)}, bf16[256,512]{1,0:T(8,128)(2,1)S(1)}, u32[]{:S(2)}, u32[]{:S(2)}) collective-permute-start(bf16[256,512]{1,0:T(8,128)(2,1)S(1)} %combine.31.gate_ref), channel_id=1, source_target_pairs={{8,12},{9,13},{10,14},{11,15},{24,28},{25,29},{26,30},{27,31}} | collective-permute-start | bytes 786440 | tf_op jit(solution)/shard_map/ppermute | solution.py:391

commit v3 on v2

v3 whole, which is shorter than its diff:
```python
import functools

import jax
import jax.numpy as jnp
from jax import lax
from jax.experimental import pallas as pl
from jax.experimental.pallas import tpu as pltpu
from jax.sharding import PartitionSpec as P

HEAD_DIM = 64
STATE = 256
KERNEL = 4
SUB = 128
CHUNK = 512
PIECE = 2 * CHUNK
LOCAL_VMEM = 16 << 20
COST = pl.CostEstimate(flops=1 << 10, bytes_accessed=1 << 10, transcendentals=0)
F32 = jnp.float32
BF16 = jnp.bfloat16


def dot(left, right):
    return jnp.dot(left, right, preferred_element_type=F32)


def silu(value):
    half = 0.5 * value
    return half + half * jnp.tanh(half)


def two_terms(value):
    high = value.astype(BF16)
    low = (value - high.astype(F32)).astype(BF16)
    return high, low


def causal_conv(current, earlier, taps):
    length, width = current.shape
    wide = current.astype(F32)
    head = jnp.concatenate([jnp.zeros((8 - KERNEL + 1, width), F32), earlier.astype(F32)], axis=0)
    joined = jnp.concatenate([head, wide], axis=0)
    total = taps[KERNEL - 1 : KERNEL] * wide
    for back in range(1, KERNEL):
        row = KERNEL - 1 - back
        total = total + taps[row : row + 1] * joined[8 - back : 8 - back + length]
    return silu(total).astype(BF16)


def column_of(row):
    size = row.shape[1]
    at = lax.broadcasted_iota(jnp.int32, (size, size), 0)
    of = lax.broadcasted_iota(jnp.int32, (size, size), 1)
    return jnp.sum(jnp.where(at == of, row, 0.0), axis=1, keepdims=True)


def terms_by_row(value):
    high = value.astype(BF16).astype(F32)
    low = value - high
    return jnp.concatenate([high, low], axis=0).T.astype(BF16)


def started(pairs, sems):
    copies = [
        pltpu.make_async_copy(source, target, sems.at[index])
        for index, (source, target) in enumerate(pairs)
    ]
    for copy in copies:
        copy.start()
    return copies


def staging(stages, sources, targets, sems):
    return started(
        [
            (source.at[:, piece * PIECE : (piece + 1) * PIECE], target)
            for piece, source, target in zip(stages, sources, targets)
        ],
        sems,
    )


def steps_kernel(
    x_hbm, taps_x_hbm, taps_bc_hbm, bc_hbm, gain_hbm, dt_hbm, bias_hbm, rate_hbm, skip_hbm,
    x_ref, tail_ref, taps_x_ref, taps_bc_ref, bc_ref, gain_ref, u_ref, v_ref, rows_ref, *scratch
):
    small, (small_sems, whole_sems) = scratch[:4], scratch[4:]
    small_copies = started(zip((dt_hbm, bias_hbm, rate_hbm, skip_hbm), small), small_sems)
    tall, wide = x_ref.shape[0], x_ref.shape[1]
    whole_copies = started(
        (
            (x_hbm.at[tall - 8 : tall, :], tail_ref), (bc_hbm, bc_ref), (taps_bc_hbm, taps_bc_ref),
            (taps_x_hbm, taps_x_ref), (x_hbm.at[:, :wide], x_ref), (gain_hbm, gain_ref),
        ),
        whole_sems,
    )
    for copy in small_copies:
        copy.wait()
    dt_ref, bias_ref, rate_ref, skip_ref = small
    heads, length = dt_ref.shape
    shifted = dt_ref[...].astype(F32) + column_of(bias_ref[...])
    steps = jnp.maximum(shifted, 0.0) + jnp.log1p(jnp.exp(-jnp.abs(shifted)))
    log_decay = -jnp.exp(column_of(rate_ref[...])) * steps
    of = lax.broadcasted_iota(jnp.int32, (length, length), 0)
    at = lax.broadcasted_iota(jnp.int32, (length, length), 1)
    upper = jnp.where(at >= of, 1.0, 0.0).astype(BF16)
    first = log_decay.astype(BF16)
    rest = log_decay - first.astype(F32)
    second = rest.astype(BF16)
    third = (rest - second.astype(F32)).astype(BF16)
    cumulative = dot(first, upper) + dot(second, upper) + dot(third, upper)
    subs = length // SUB
    decays, scales = [], []
    start = jnp.zeros((heads, 1), F32)
    for sub in range(subs):
        rows = slice(sub * SUB, (sub + 1) * SUB)
        inside = cumulative[:, rows] - start
        u_ref[rows, :] = terms_by_row(jnp.exp(inside))
        v_ref[rows, :] = terms_by_row(jnp.exp(-inside) * steps[:, rows])
        end = cumulative[:, (sub + 1) * SUB - 1 : (sub + 1) * SUB]
        decays.append(jnp.exp(end - start))
        scales.append(jnp.exp(start))
        start = end
    lines = decays + scales + [column_of(skip_ref[...]), jnp.exp(start)]
    lane = lax.broadcasted_iota(jnp.int32, (heads, SUB), 1)
    table = jnp.zeros((heads, SUB), F32)
    for index, line in enumerate(lines):
        table = jnp.where(lane == index, line, table)
    rows_ref[...] = terms_by_row(table)[: rows_ref.shape[0]]
    for copy in whole_copies:
        copy.wait()


def stage_kernel(stages, gate_ref, *refs):
    for copy in staging(stages, refs[: len(stages)], refs[len(stages) : -1], refs[-1]):
        copy.wait()


def groups_kernel(groups, stages, bc_ref, early_ref, taps_ref, gate_ref, *refs):
    sources, (left_ref, bt_ref), targets = refs[: len(stages)], refs[len(stages) : len(stages) + 2], refs[len(stages) + 2 : -1]
    copies = staging(stages, sources, targets, refs[-1])
    length = bc_ref.shape[0]
    subs = length // SUB
    of = lax.broadcasted_iota(jnp.int32, (SUB, SUB), 1)
    at = lax.broadcasted_iota(jnp.int32, (SUB, SUB), 0)
    causal = at >= of
    for group in range(groups):
        lanes = slice(group * 2 * STATE, (group + 1) * 2 * STATE)
        base = early_ref.shape[1] - bc_ref.shape[1] + lanes.start
        earlier = early_ref[:, base : base + 2 * STATE]
        conv = causal_conv(bc_ref[:, lanes], earlier, taps_ref[:, group, :])
        b_turned = conv[:, :STATE].astype(F32).T.astype(BF16)
        c_rows = conv[:, STATE:]
        bt_ref[group] = b_turned
        for sub in range(subs):
            rows = slice(sub * SUB, (sub + 1) * SUB)
            scores = jnp.where(causal, dot(c_rows[rows], b_turned[:, rows]), 0.0)
            left_ref[group, rows, :SUB] = scores.astype(BF16)
            left_ref[group, rows, SUB:] = c_rows[rows]
    for copy in copies:
        copy.wait()


def spread_matrix(terms, width, first_head):
    row = lax.broadcasted_iota(jnp.int32, (terms, width), 0)
    lane = lax.broadcasted_iota(jnp.int32, (terms, width), 1)
    heads = terms // 2
    start = (jnp.where(row >= heads, row - heads, row) - first_head) * HEAD_DIM
    return jnp.where((lane >= start) & (lane < start + HEAD_DIM), 1.0, 0.0).astype(BF16)


def next_state(state, scaled, b_turned, decay):
    added = dot(b_turned, scaled)
    return decay * (added if state is None else state + added)


def first_kernel(
    group, chunk, stages, place_ref, x_ref, taps_ref, v_ref, rows_ref, bc_ref, bc_taps_ref, gate_ref, *refs
):
    send_ref = refs[len(stages)]
    copies = staging(stages, refs[: len(stages)], refs[len(stages) + 1 : -1], refs[-1]) if stages else []

    @pl.when(place_ref[0] == 0)
    def _():
        at = slice(chunk * CHUNK, (chunk + 1) * CHUNK)
        length, width = x_ref.shape[0], CHUNK
        spread = spread_matrix(v_ref.shape[1], width, chunk * (CHUNK // HEAD_DIM))
        lanes = dot(rows_ref[...], spread)
        start = group * 2 * STATE
        nothing = jnp.zeros((KERNEL - 1, STATE), BF16)
        b_rows = causal_conv(bc_ref[:, start : start + STATE], nothing, bc_taps_ref[:, group, :STATE])
        b_turned = b_rows.astype(F32).T.astype(BF16)
        nothing = jnp.zeros((KERNEL - 1, width), BF16)
        inner_at = slice(chunk * CHUNK % PIECE, chunk * CHUNK % PIECE + CHUNK)
        conv = causal_conv(x_ref[:, inner_at], nothing, taps_ref[:, at])
        state = None
        for sub in range(length // SUB):
            rows = slice(sub * SUB, (sub + 1) * SUB)
            scaled = (conv[rows].astype(F32) * dot(v_ref[rows], spread)).astype(BF16)
            state = next_state(state, scaled, b_turned[:, rows], lanes[sub : sub + 1])
        send_ref[...] = state.astype(send_ref.dtype)

    for copy in copies:
        copy.wait()


def local_kernel(
    group, chunk, stages, x_ref, early_ref, taps_ref, z_ref, left_ref, bt_ref, u_ref, v_ref, rows_ref,
    gate_ref, *refs
):
    outs = len(stages)
    part_ref, reach_ref, state_ref, lanes_ref = refs[outs : outs + 4]
    copies = staging(stages, refs[:outs], refs[outs + 4 : -1], refs[-1]) if stages else []
    lanes_at = slice(chunk * CHUNK, (chunk + 1) * CHUNK)
    inner_at = slice(chunk * CHUNK % PIECE, chunk * CHUNK % PIECE + CHUNK)
    length, width = x_ref.shape[0], CHUNK
    spread = spread_matrix(u_ref.shape[1], width, chunk * (CHUNK // HEAD_DIM))
    lanes = dot(rows_ref[...], spread)
    lanes_ref[...] = lanes
    conv = causal_conv(x_ref[:, inner_at], early_ref[:, lanes_at], taps_ref[:, lanes_at])
    subs = length // SUB
    skip = lanes[2 * subs : 2 * subs + 1]
    state = None
    for sub in range(subs):
        rows = slice(sub * SUB, (sub + 1) * SUB)
        inputs = conv[rows].astype(F32)
        scaled = (inputs * dot(v_ref[rows], spread)).astype(BF16)
        inner = dot(left_ref[group, rows, :SUB], scaled)
        if sub > 0:
            inner = inner + dot(left_ref[group, rows, SUB:], state.astype(BF16))
        state = next_state(state, scaled, bt_ref[group, :, rows], lanes[sub : sub + 1])
        grown = dot(u_ref[rows], spread)
        gate = silu(z_ref[rows, inner_at].astype(F32))
        part_ref[rows, :] = gate * (grown * inner + skip * inputs)
        reach_ref[rows, :] = gate * grown * lanes[subs + sub : subs + sub + 1]
    state_ref[...] = state
    for copy in copies:
        copy.wait()


def combine_kernel(line, owners, arrivals, place_ref, *refs):
    place = place_ref[0]
    lanes = refs[: len(owners)]
    states = refs[len(owners) : 2 * len(owners)]
    came = refs[2 * len(owners) : 2 * len(owners) + arrivals]
    sent_ref = refs[-1]
    total, state = lanes[0][line : line + 1], states[0][...]
    for owner, lane_ref, state_ref in zip(owners[1:], lanes[1:], states[1:]):
        total = jnp.where(place >= owner, lane_ref[line : line + 1], total)
        state = jnp.where(place >= owner, state_ref[...], state)
    value = came[0][...].astype(F32)
    for other in came[1:]:
        value = jnp.where(place >= 2, other[...].astype(F32), value)
    sent_ref[...] = (total * value + state).astype(sent_ref.dtype)


def absorb_kernel(group, owners, left_ref, part_ref, reach_ref, place_ref, *refs):
    length, width = part_ref.shape
    gated_ref, square_ref = refs[-2:]
    place = place_ref[0]
    incoming = refs[0][...].astype(F32)
    for owner, other in zip(owners[1:], refs[1:]):
        incoming = jnp.where(place >= owner, other[...].astype(F32), incoming)
    incoming = incoming.astype(BF16)
    for start in range(0, length, SUB):
        rows = slice(start, start + SUB)
        value = part_ref[rows] + reach_ref[rows] * dot(left_ref[group, rows, SUB:], incoming)
        gated_ref[rows, :] = value
        power = value * value
        total = power[:, :128]
        for lane in range(128, width, 128):
            total = total + power[:, lane : lane + 128]
        square_ref[rows, :] = total


def finish_kernel(group, chunks, gain_ref, *refs):
    gated = refs[:chunks]
    squares = refs[chunks : 2 * chunks]
    out_ref = refs[-1]
    height = out_ref.shape[0]
    rows = pl.ds(pl.multiple_of(pl.program_id(0) * height, height), height)
    total = squares[0][rows, :]
    for square in squares[1:]:
        total = total + square[rows, :]
    mean = jnp.sum(total, axis=1, keepdims=True) * (1.0 / (CHUNK * chunks))
    scale = lax.rsqrt(mean + 1e-05)
    for index in range(chunks):
        lanes = slice(index * CHUNK, (index + 1) * CHUNK)
        start = (group * chunks + index) * CHUNK
        out_ref[:, lanes] = (gated[index][rows, :] * scale * gain_ref[:, start : start + CHUNK]).astype(BF16)


def shards(x_in, bc_in, z_in, dt_in, conv_x, conv_bc, dt_bias, a_log, d_skip, norm_gain):
    length, channels = x_in.shape
    groups = bc_in.shape[1]
    heads = channels // HEAD_DIM
    contexts = lax.axis_size("ctx")
    wire = BF16 if contexts <= 8 else F32
    margin = KERNEL - 1
    subs = length // SUB
    ahead = [(i, i + 1) for i in range(contexts - 1)]
    bc_width = groups * 2 * STATE
    line_rows = -(-(2 * subs + 2) // 8) * 8
    sub_width = SUB + STATE
    place = lax.axis_index("ctx").astype(jnp.int32).reshape(1)
    small = (dt_in.T, dt_bias.reshape(1, heads), a_log.reshape(1, heads), d_skip.reshape(1, heads))
    far = lambda array: pltpu.with_memory_space_constraint(array, pltpu.HBM)
    large = tuple(far(array) for array in (x_in, conv_x, conv_bc, bc_in, norm_gain.reshape(1, channels)))
    begun = PIECE
    x_begun, tail, taps_x, taps_bc, bc_near, gain, grow, shrink, lines = pl.pallas_call(
        steps_kernel,
        in_specs=[pl.BlockSpec(memory_space=pltpu.HBM)] * (len(large) + len(small)),
        out_specs=[pl.BlockSpec(memory_space=pltpu.VMEM)] * 9,
        out_shape=(
            jax.ShapeDtypeStruct((length, begun), BF16),
            jax.ShapeDtypeStruct((8, channels), BF16),
            jax.ShapeDtypeStruct(conv_x.shape, F32),
            jax.ShapeDtypeStruct(conv_bc.shape, F32),
            jax.ShapeDtypeStruct(bc_in.shape, BF16),
            jax.ShapeDtypeStruct((1, channels), F32),
            jax.ShapeDtypeStruct((length, 2 * heads), BF16),
            jax.ShapeDtypeStruct((length, 2 * heads), BF16),
            jax.ShapeDtypeStruct((line_rows, 2 * heads), BF16),
        ),
        scratch_shapes=[pltpu.VMEM(array.shape, array.dtype) for array in small] + [
            pltpu.SemaphoreType.DMA((len(small),)), pltpu.SemaphoreType.DMA((6,)),
        ],
        compiler_params=pltpu.CompilerParams(vmem_limit_bytes=12 << 20),
        cost_estimate=COST,
        name="steps",
    )(*large, *[far(array) for array in small])
    bc_flat = bc_near.reshape(length, bc_width)
    per_group = channels // groups
    in_group = per_group // CHUNK
    count = channels // CHUNK
    hops = contexts - 1
    near = pl.BlockSpec(memory_space=pltpu.VMEM)
    scalar = pl.BlockSpec(memory_space=pltpu.SMEM)
    afar = pl.BlockSpec(memory_space=pltpu.HBM)
    last_piece = channels // PIECE - 1
    hold = jax.ShapeDtypeStruct((STATE, CHUNK), wire)
    from_first, from_later = [], []

    def send(value):
        from_first.append(lax.ppermute(value, "ctx", [(0, 1)]))

    pieces_x, pieces_z = {0: x_begun}, {}
    z_far = far(z_in)

    def staged_of(stages):
        inputs = [large[0] if name == "x" else z_far for name, _ in stages]
        shapes = [jax.ShapeDtypeStruct((length, PIECE), BF16) for _ in stages]
        scratch = [pltpu.SemaphoreType.DMA((len(stages),))] if stages else []
        return [piece for _, piece in stages], inputs, shapes, scratch

    def keep(stages, arrays):
        for (name, piece), array in zip(stages, arrays):
            (pieces_x if name == "x" else pieces_z)[piece] = array

    def first(chunk, gate, stages):
        which, inputs, shapes, scratch = staged_of(stages)
        result = pl.pallas_call(
            functools.partial(first_kernel, chunk // in_group, chunk, which),
            in_specs=[scalar] + [near] * 7 + [afar] * len(inputs),
            out_specs=[near] * (1 + len(shapes)),
            out_shape=[hold] + shapes,
            scratch_shapes=scratch,
            compiler_params=pltpu.CompilerParams(vmem_limit_bytes=12 << 20),
            cost_estimate=COST,
            name="first",
        )(place, pieces_x[chunk * CHUNK // PIECE], taps_x, shrink, lines, bc_flat, taps_bc, gate, *inputs)
        keep(stages, result[1:])
        return result[0]

    early = jnp.concatenate([tail[-margin:], bc_near[-margin:].reshape(margin, bc_width)], axis=1)
    ready = first(0, shrink, [])
    early, ready = lax.optimization_barrier((early, ready))
    early = lax.ppermute(early, "ctx", ahead)
    send(ready)
    stages = [("z", 0), ("x", 1)] if last_piece > 0 else [("z", 0)]
    which, inputs, shapes, scratch = staged_of(stages)
    arrays = pl.pallas_call(
        functools.partial(stage_kernel, which),
        out_shape=shapes,
        in_specs=[near] + [afar] * len(inputs),
        out_specs=[near] * len(shapes),
        scratch_shapes=scratch,
        compiler_params=pltpu.CompilerParams(vmem_limit_bytes=8 << 20),
        cost_estimate=COST,
        name="stage",
    )(ready, *inputs)
    keep(stages, arrays)
    stages = [("z", 1)] if last_piece > 0 else []
    which, inputs, shapes, scratch = staged_of(stages)
    left, b_turned, *arrays = pl.pallas_call(
        functools.partial(groups_kernel, groups, which),
        out_shape=[
            jax.ShapeDtypeStruct((groups, length, sub_width), BF16),
            jax.ShapeDtypeStruct((groups, STATE, length), BF16),
        ] + shapes,
        in_specs=[near] * 4 + [afar] * len(inputs),
        out_specs=[near] * (2 + len(shapes)),
        scratch_shapes=scratch or [pltpu.SemaphoreType.DMA((1,))],
        compiler_params=pltpu.CompilerParams(vmem_limit_bytes=12 << 20),
        cost_estimate=COST,
        name="groups",
    )(bc_flat, early, taps_bc, lines, *inputs)
    keep(stages, arrays)

    def local(chunk, gate, stages):
        group, piece = chunk // in_group, chunk * CHUNK // PIECE
        which, inputs, shapes, scratch = staged_of(stages)
        result = pl.pallas_call(
            functools.partial(local_kernel, group, chunk, which),
            in_specs=[near] * 10 + [afar] * len(inputs),
            out_specs=[near] * (4 + len(shapes)),
            out_shape=[
                jax.ShapeDtypeStruct((length, CHUNK), F32),
                jax.ShapeDtypeStruct((length, CHUNK), F32),
                jax.ShapeDtypeStruct((STATE, CHUNK), F32),
                jax.ShapeDtypeStruct((line_rows, CHUNK), F32),
            ] + shapes,
            scratch_shapes=scratch,
            compiler_params=pltpu.CompilerParams(vmem_limit_bytes=LOCAL_VMEM),
            cost_estimate=COST,
            name="local",
        )(
            pieces_x[piece], early, taps_x, pieces_z[piece], left, b_turned, grow, shrink, lines,
            gate, *inputs,
        )
        keep(stages, result[4:])
        return result[:4]

    def combine(owners, chunks, came, gate):
        lanes = [pieces[chunk][3] for chunk in chunks]
        states = [pieces[chunk][2] for chunk in chunks]
        return pl.pallas_call(
            functools.partial(combine_kernel, 2 * subs + 1, owners, len(came)),
            in_specs=[scalar] + [near] * (2 * len(owners) + len(came) + 1),
            out_specs=near,
            out_shape=hold,
            compiler_params=pltpu.CompilerParams(vmem_limit_bytes=8 << 20),
            cost_estimate=COST,
            name="combine",
        )(place, *lanes, *states, *came, gate)

    def absorb(chunk, owners, came, gate):
        group = chunk // in_group
        part, reach = pieces[chunk][:2]
        return pl.pallas_call(
            functools.partial(absorb_kernel, group, owners),
            in_specs=[near] * 3 + [scalar] + [near] * (1 + len(came)),
            out_specs=(near, near),
            out_shape=(
                jax.ShapeDtypeStruct((length, CHUNK), F32),
                jax.ShapeDtypeStruct((length, 128), F32),
            ),
            compiler_params=pltpu.CompilerParams(vmem_limit_bytes=8 << 20),
            cost_estimate=COST,
            name="absorb",
        )(left, part, reach, place, *came, gate)

    def finish(group, done, out, gate):
        rows = SUB
        operands = [gain] + [pair[0] for pair in done] + [pair[1] for pair in done] + [gate]
        specs = [near] * len(operands)
        aliases = {}
        if out is not None:
            aliases = {len(operands): 0}
            operands.append(out)
            specs.append(pl.BlockSpec(memory_space=pl.ANY))
        return pl.pallas_call(
            functools.partial(finish_kernel, group, in_group),
            grid=(length // rows,),
            in_specs=specs,
            out_specs=pl.BlockSpec((rows, per_group), lambda i: (i, group)),
            out_shape=jax.ShapeDtypeStruct((length, channels), BF16),
            input_output_aliases=aliases,
            compiler_params=pltpu.CompilerParams(vmem_limit_bytes=12 << 20),
            cost_estimate=COST,
            name="finish",
        )(*operands)

    pieces, done = {}, []
    gate, out = b_turned, None

    def work(chunk):
        stages = []
        if len(pieces) < last_piece - 1:
            stages = [("x", len(pieces) + 2), ("z", len(pieces) + 2)]
        pieces[chunk] = local(chunk, gate, stages)
        return pieces[chunk][3]

    gate = first(1, gate, [])
    send(gate)
    gate = work(0)
    if count > 2:
        gate = first(2, gate, [])
        send(gate)
    last_step = count - 1 + 2 * max(hops - 2, 0)
    for step in range(last_step + 2):
        senders = [
            owner for owner in range(1, hops) if 0 <= step - 2 * (owner - 1) < count
        ]
        if senders:
            came = [from_first[step]] if step < count else []
            came += [from_later[step - 2]] if step >= 2 else []
            gate = combine(senders, [step - 2 * (owner - 1) for owner in senders], came, gate)
            from_later.append(
                lax.ppermute(gate, "ctx", [(owner, owner + 1) for owner in senders])
            )
        if step + 3 < count:
            gate = first(step + 3, gate, [])
            send(gate)
        if step + 1 < count:
            gate = work(step + 1)
        chunk = step - 1 - 2 * max(hops - 2, 0)
        if 0 <= chunk < count:
            owners = [0] + list(range(2, contexts))
            came = [from_first[chunk]] + [from_later[chunk + 2 * (i - 2)] for i in owners[1:]]
            done.append(absorb(chunk, owners, came, gate))
            gate = done[-1][1]
            if (chunk + 1) % in_group == 0:
                group = chunk // in_group
                out = finish(group, done[group * in_group :], out, gate)
    return out


def solution(mesh):
    placed = (
        P(("groups", "ctx"), ("tp", "fsdp")),
        P(("groups", "ctx"), ("tp", "fsdp"), None),
        P(("groups", "ctx"), ("tp", "fsdp")),
        P(("groups", "ctx"), ("tp", "fsdp")),
        P(None, ("tp", "fsdp")),
        P(None, ("tp", "fsdp"), None),
        P(("tp", "fsdp")),
        P(("tp", "fsdp")),
        P(("tp", "fsdp")),
        P(("tp", "fsdp")),
    )
    return jax.shard_map(
        shards,
        mesh=mesh,
        in_specs=placed,
        out_specs=P(("groups", "ctx"), ("tp", "fsdp")),
        check_vma=False,
    )
```

time: 85.8 us -> 74.2 us (0.86)
  waiting for transfers between devices: 35.7 us -> 29.2 us
  starting transfers between devices: 22.6 us -> 18.6 us
  local copies, waits for them, and re-layouts: 2.13 us -> 0.16 us
  Pallas kernels: 23.6 us -> 25.3 us
    ppermute x24 -> x18, waiting for transfers between devices: 34.5 us -> 25.2 us  [the longest x10 25.2 us: shards(): lax.ppermute(gate, 'ctx', [(owner, owner + 1) for owner in senders])]
    ppermute x24 -> x18, starting transfers between devices: 21.4 us -> 17.3 us  [the longest x10 11.9 us: shards(): lax.ppermute(gate, 'ctx', [(owner, owner + 1) for owner in senders])]
    ppermute x1, waiting for transfers between devices: 1.25 us -> 3.91 us  [shards(): early = lax.ppermute(early, 'ctx', ahead)]
    pallas_call x36 -> x39, Pallas kernels: 23.6 us -> 25.3 us  [the longest x8 12 us: local(): pl.pallas_call(functools.partial(local_kernel, group, chunk, which), in_s...]
    unnamed x1 -> x3, local copies, waits for them, and re-layouts: 1.26 us -> 0.14 us
  transfers between devices with their start and end apart: 25 -> 19, of which waited for: 9 -> 9; matrix products, arithmetic and copies ran while one was open for 1% -> 0% of each run, Pallas kernels for 22% -> 28%
where the time goes in v3:
time: 74.2 us; the launch traced here: 73.7 us
  waiting for transfers between devices  29.2 us (39%)
  Pallas kernels  25.3 us (34%)
  starting transfers between devices  18.6 us (25%)
    ppermute x10, waiting for transfers between devices, shards(): lax.ppermute(gate, 'ctx', [(owner, owner + 1) for owner in senders])  25.2 us
    pallas_call x8, Pallas kernels, local(): pl.pallas_call(functools.partial(local_kernel, group, chunk, which), in_s...  12 us
    ppermute x10, starting transfers between devices, shards(): lax.ppermute(gate, 'ctx', [(owner, owner + 1) for owner in senders])  11.9 us
    ppermute x8, starting transfers between devices, send(): from_first.append(lax.ppermute(value, 'ctx', [(0, 1)]))  5.42 us
    pallas_call x2, Pallas kernels, finish(): pl.pallas_call(functools.partial(finish_kernel, group, in_group), grid=(l...  3.97 us
    ppermute x1, waiting for transfers between devices, shards(): early = lax.ppermute(early, 'ctx', ahead)  3.91 us
    pallas_call x8, Pallas kernels, absorb(): pl.pallas_call(functools.partial(absorb_kernel, group, owners), in_specs=...  2.77 us
    pallas_call x1, Pallas kernels, shards(): pl.pallas_call(steps_kernel, in_specs=[pl.BlockSpec(memory_space=pltpu.HB...  2 us
  transfers between devices with their start and end apart: 19, of which 9 were waited for; matrix products, arithmetic and copies ran while one was open for 0% of the time, Pallas kernels for 28%

profile of v3, /device:TPU:28, one launch (start us, length us, event | category | flops | bytes accessed | tf_op | source)
XLA Modules:
  0.0 73.7 jit_solution(16113840571562863073)
XLA Ops:
  0.0 2.0 %steps.1 = (bf16[384,1024]{1,0:T(8,128)(2,1)S(1)}, bf16[8,4096]{1,0:T(8,128)(2,1)S(1)}, f32[4,4096]{1,0:T(4,128)S(1)}, f32[4,2,512]{2,1,0:T(2,128)S(1)}, bf16[38...) custom-call(bf16[384,4096]{1,0:T(8,128)(2,1)} %refs_0_.7, ...), custom_call_target="tpu_custom_call" | custom-call | flops 1024 | bytes 1024 | tf_op jit(solution)/shard_map/steps/pallas_call | solution.py:309
  2.2 1.3 %collective-permute-start = (bf16[3,5120]{1,0:T(4,128)(2,1)S(1)}, bf16[3,5120]{1,0:T(4,128)(2,1)S(1)}, u32[]{:S(2)}, u32[]{:S(2)}) collective-permute-start(bf16[3,5120]{1,0:T(4,128)(2,1)S(1)} %pad_maximum_fusion), channel_id=1, source_target_pairs={{0,4},{4,8},{8,12},{1,5},{5,9},{9,13},{2,6},{6,10},{10,14},{3,7},{... | collective-permute-start | bytes 92168 | tf_op jit(solution)/shard_map/ppermute | solution.py:377
  3.5 0.7 collective-permute-start.1
  4.2 3.9 %collective-permute-done.early_ref = bf16[3,5120]{1,0:T(4,128)(2,1)S(1)} collective-permute-done((bf16[3,5120]{1,0:T(4,128)(2,1)S(1)}, bf16[3,5120]{1,0:T(4,128)(2,1)S(1)}, u32[]{:S(2)}, u32[]{:S(2)}) %collective-permute-start) | collective-permute-done | bytes 30752 | tf_op jit(solution)/shard_map/ppermute | solution.py:377
  8.1 1.9 %groups.1 = (bf16[2,384,384]{2,1,0:T(8,128)(2,1)S(1)}, bf16[2,256,384]{2,1,0:T(8,128)(2,1)S(1)}, bf16[384,1024]{1,0:T(8,128)(2,1)S(1)}) custom-call(bf16[384,1024]{1,0:T(8,128)(2,1)S(1)} %bitcast.12, bf16[3,5120]{1,0:T(4,128)(2,1)S(1)} %collective-permute-done.early_ref, f32[4,2,512]{2,1,0:T(2,128)S(1)} %get-tuple-element.80.bc_taps_ref.taps_ref, ...), custom_call_target="tpu_custom_call" | custom-call | flops 1024 | bytes 1024 | tf_op jit(solution)/shard_map/groups/pallas_call | solution.py:394
  10.7 1.4 %stage.1 = (bf16[384,1024]{1,0:T(8,128)(2,1)S(1)}, bf16[384,1024]{1,0:T(8,128)(2,1)S(1)}) custom-call(bf16[256,512]{1,0:T(8,128)(2,1)S(1)} %first.8.gate_ref, bf16[384,4096]{1,0:T(8,128)(2,1)} %refs_1_.5, bf16[384,4096]{1,0:T(8,128)(2,1)} %refs_0_.7), custom_call_target="tpu_custom_call" | custom-call | flops 1024 | bytes 1024 | tf_op jit(solution)/shard_map/stage/pallas_call | solution.py:381
  12.1 1.5 %local.8 = (f32[384,512]{1,0:T(8,128)S(1)}, f32[384,512]{1,0:T(8,128)S(1)}, f32[256,512]{1,0:T(8,128)S(1)}, f32[8,512]{1,0:T(8,128)S(1)}, bf16[384,1024]{1,0:T(8,128)(2,1)S(1)}, /*index=5*/bf16[384,1024]{1,0:T(8,128)(2,1)S(1)}) custom-call(bf16[384,1024]{1,0:T(8,128)(2,1)S(1)} %get-tuple-element.76.x_ref, ...), custom_call_target="tpu_custom_call" | custom-call | flops 1024 | bytes 1024 | tf_op jit(solution)/shard_map/local/pallas_call | solution.py:412
  15.8 1.5 %local.9 = (f32[384,512]{1,0:T(8,128)S(1)}, f32[384,512]{1,0:T(8,128)S(1)}, f32[256,512]{1,0:T(8,128)S(1)}, f32[8,512]{1,0:T(8,128)S(1)}, bf16[384,1024]{1,0:T(8,128)(2,1)S(1)}, /*index=5*/bf16[384,1024]{1,0:T(8,128)(2,1)S(1)}) custom-call(bf16[384,1024]{1,0:T(8,128)(2,1)S(1)} %get-tuple-element.76.x_ref, ...), custom_call_target="tpu_custom_call" | custom-call | flops 1024 | bytes 1024 | tf_op jit(solution)/shard_map/local/pallas_call | solution.py:412
  18.3 1.5 %local.10 = (f32[384,512]{1,0:T(8,128)S(1)}, f32[384,512]{1,0:T(8,128)S(1)}, f32[256,512]{1,0:T(8,128)S(1)}, f32[8,512]{1,0:T(8,128)S(1)}) custom-call(bf16[384,1024]{1,0:T(8,128)(2,1)S(1)} %get-tuple-element.89.x_ref, bf16[3,5120]{1,0:T(4,128)(2,1)S(1)} %collective-permute-done.early_ref, f32[4,4096]{1,0:T(4,128)S(1)} %get-tuple-element.77.taps_ref, ...), custom_call_target="tpu_custom_call" | custom-call | flops 1024 | bytes 1024 | tf_op jit(solution)/shard_map/local/pallas_call | solution.py:412
  20.0 1.3 %collective-permute-start.8 = (bf16[256,512]{1,0:T(8,128)(2,1)S(1)}, bf16[256,512]{1,0:T(8,128)(2,1)S(1)}, u32[]{:S(2)}, u32[]{:S(2)}) collective-permute-start(bf16[256,512]{1,0:T(8,128)(2,1)S(1)} %combine.12.gate_ref), channel_id=1, source_target_pairs={{4,8},{8,12},{5,9},{9,13},{6,10},{10,14},{7,11},{11,15},{20,24},{2... | collective-permute-start | bytes 786440 | tf_op jit(solution)/shard_map/ppermute | solution.py:509
  22.0 1.5 %local.11 = (f32[384,512]{1,0:T(8,128)S(1)}, f32[384,512]{1,0:T(8,128)S(1)}, f32[256,512]{1,0:T(8,128)S(1)}, f32[8,512]{1,0:T(8,128)S(1)}) custom-call(bf16[384,1024]{1,0:T(8,128)(2,1)S(1)} %get-tuple-element.89.x_ref, bf16[3,5120]{1,0:T(4,128)(2,1)S(1)} %collective-permute-done.early_ref, f32[4,4096]{1,0:T(4,128)S(1)} %get-tuple-element.77.taps_ref, ...), custom_call_target="tpu_custom_call" | custom-call | flops 1024 | bytes 1024 | tf_op jit(solution)/shard_map/local/pallas_call | solution.py:412
  23.6 1.3 %collective-permute-start.11 = (bf16[256,512]{1,0:T(8,128)(2,1)S(1)}, bf16[256,512]{1,0:T(8,128)(2,1)S(1)}, u32[]{:S(2)}, u32[]{:S(2)}) collective-permute-start(bf16[256,512]{1,0:T(8,128)(2,1)S(1)} %combine.13.gate_ref), channel_id=1, source_target_pairs={{4,8},{8,12},{5,9},{9,13},{6,10},{10,14},{7,11},{11,15},{20,24},{2... | collective-permute-start | bytes 786440 | tf_op jit(solution)/shard_map/ppermute | solution.py:509
  25.6 1.5 %local.12 = (f32[384,512]{1,0:T(8,128)S(1)}, f32[384,512]{1,0:T(8,128)S(1)}, f32[256,512]{1,0:T(8,128)S(1)}, f32[8,512]{1,0:T(8,128)S(1)}) custom-call(bf16[384,1024]{1,0:T(8,128)(2,1)S(1)} %get-tuple-element.87.x_ref, bf16[3,5120]{1,0:T(4,128)(2,1)S(1)} %collective-permute-done.early_ref, f32[4,4096]{1,0:T(4,128)S(1)} %get-tuple-element.77.taps_ref, ...), custom_call_target="tpu_custom_call" | custom-call | flops 1024 | bytes 1024 | tf_op jit(solution)/shard_map/local/pallas_call | solution.py:412
  27.1 3.3 %collective-permute-done.8.refs_2_.refs_5_.refs_1_ = bf16[256,512]{1,0:T(8,128)(2,1)S(1)} collective-permute-done((bf16[256,512]{1,0:T(8,128)(2,1)S(1)}, bf16[256,512]{1,0:T(8,128)(2,1)S(1)}, u32[]{:S(2)}, u32[]{:S(2)}) %collective-permute-start.8) | collective-permute-done | bytes 262176 | tf_op jit(solution)/shard_map/ppermute | solution.py:509
  31.7 1.5 %collective-permute-start.9 = (bf16[256,512]{1,0:T(8,128)(2,1)S(1)}, bf16[256,512]{1,0:T(8,128)(2,1)S(1)}, u32[]{:S(2)}, u32[]{:S(2)}) collective-permute-start(bf16[256,512]{1,0:T(8,128)(2,1)S(1)} %combine.14.gate_ref), channel_id=1, source_target_pairs={{4,8},{8,12},{5,9},{9,13},{6,10},{10,14},{7,11},{11,15},{20,24},{2... | collective-permute-start | bytes 786440 | tf_op jit(solution)/shard_map/ppermute | solution.py:509
  33.2 1.5 %local.13 = (f32[384,512]{1,0:T(8,128)S(1)}, f32[384,512]{1,0:T(8,128)S(1)}, f32[256,512]{1,0:T(8,128)S(1)}, f32[8,512]{1,0:T(8,128)S(1)}) custom-call(bf16[384,1024]{1,0:T(8,128)(2,1)S(1)} %get-tuple-element.87.x_ref, bf16[3,5120]{1,0:T(4,128)(2,1)S(1)} %collective-permute-done.early_ref, f32[4,4096]{1,0:T(4,128)S(1)} %get-tuple-element.77.taps_ref, ...), custom_call_target="tpu_custom_call" | custom-call | flops 1024 | bytes 1024 | tf_op jit(solution)/shard_map/local/pallas_call | solution.py:412
  34.7 1.3 %collective-permute-done.11.refs_2_.refs_5_.refs_1_ = bf16[256,512]{1,0:T(8,128)(2,1)S(1)} collective-permute-done((bf16[256,512]{1,0:T(8,128)(2,1)S(1)}, bf16[256,512]{1,0:T(8,128)(2,1)S(1)}, u32[]{:S(2)}, u32[]{:S(2)}) %collective-permute-start.11) | collective-permute-done | bytes 262176 | tf_op jit(solution)/shard_map/ppermute | solution.py:509
  36.5 1.3 %collective-permute-start.15 = (bf16[256,512]{1,0:T(8,128)(2,1)S(1)}, bf16[256,512]{1,0:T(8,128)(2,1)S(1)}, u32[]{:S(2)}, u32[]{:S(2)}) collective-permute-start(bf16[256,512]{1,0:T(8,128)(2,1)S(1)} %combine.15.gate_ref), channel_id=1, source_target_pairs={{4,8},{8,12},{5,9},{9,13},{6,10},{10,14},{7,11},{11,15},{20,24},{2... | collective-permute-start | bytes 786440 | tf_op jit(solution)/shard_map/ppermute | solution.py:509
  38.5 1.5 %local.14 = (f32[384,512]{1,0:T(8,128)S(1)}, f32[384,512]{1,0:T(8,128)S(1)}, f32[256,512]{1,0:T(8,128)S(1)}, f32[8,512]{1,0:T(8,128)S(1)}) custom-call(bf16[384,1024]{1,0:T(8,128)(2,1)S(1)} %get-tuple-element.92.x_ref, bf16[3,5120]{1,0:T(4,128)(2,1)S(1)} %collective-permute-done.early_ref, f32[4,4096]{1,0:T(4,128)S(1)} %get-tuple-element.77.taps_ref, ...), custom_call_target="tpu_custom_call" | custom-call | flops 1024 | bytes 1024 | tf_op jit(solution)/shard_map/local/pallas_call | solution.py:412
  40.0 2.7 %collective-permute-done.9.refs_2_.refs_5_.refs_1_ = bf16[256,512]{1,0:T(8,128)(2,1)S(1)} collective-permute-done((bf16[256,512]{1,0:T(8,128)(2,1)S(1)}, bf16[256,512]{1,0:T(8,128)(2,1)S(1)}, u32[]{:S(2)}, u32[]{:S(2)}) %collective-permute-start.9) | collective-permute-done | bytes 262176 | tf_op jit(solution)/shard_map/ppermute | solution.py:509
  43.1 1.3 %collective-permute-start.13 = (bf16[256,512]{1,0:T(8,128)(2,1)S(1)}, bf16[256,512]{1,0:T(8,128)(2,1)S(1)}, u32[]{:S(2)}, u32[]{:S(2)}) collective-permute-start(bf16[256,512]{1,0:T(8,128)(2,1)S(1)} %combine.16.gate_ref), channel_id=1, source_target_pairs={{4,8},{8,12},{5,9},{9,13},{6,10},{10,14},{7,11},{11,15},{20,24},{2... | collective-permute-start | bytes 786440 | tf_op jit(solution)/shard_map/ppermute | solution.py:509
  44.4 1.5 %local.15 = (f32[384,512]{1,0:T(8,128)S(1)}, f32[384,512]{1,0:T(8,128)S(1)}, f32[256,512]{1,0:T(8,128)S(1)}, f32[8,512]{1,0:T(8,128)S(1)}) custom-call(bf16[384,1024]{1,0:T(8,128)(2,1)S(1)} %get-tuple-element.92.x_ref, bf16[3,5120]{1,0:T(4,128)(2,1)S(1)} %collective-permute-done.early_ref, f32[4,4096]{1,0:T(4,128)S(1)} %get-tuple-element.77.taps_ref, ...), custom_call_target="tpu_custom_call" | custom-call | flops 1024 | bytes 1024 | tf_op jit(solution)/shard_map/local/pallas_call | solution.py:412
  45.9 3.3 %collective-permute-done.15.refs_2_.refs_5_.refs_1_ = bf16[256,512]{1,0:T(8,128)(2,1)S(1)} collective-permute-done((bf16[256,512]{1,0:T(8,128)(2,1)S(1)}, bf16[256,512]{1,0:T(8,128)(2,1)S(1)}, u32[]{:S(2)}, u32[]{:S(2)}) %collective-permute-start.15) | collective-permute-done | bytes 262176 | tf_op jit(solution)/shard_map/ppermute | solution.py:509
  49.7 1.3 %collective-permute-start.16 = (bf16[256,512]{1,0:T(8,128)(2,1)S(1)}, bf16[256,512]{1,0:T(8,128)(2,1)S(1)}, u32[]{:S(2)}, u32[]{:S(2)}) collective-permute-start(bf16[256,512]{1,0:T(8,128)(2,1)S(1)} %combine.17.refs_3_), channel_id=1, source_target_pairs={{4,8},{8,12},{5,9},{9,13},{6,10},{10,14},{7,11},{11,15},{20,24},{2... | collective-permute-start | bytes 786440 | tf_op jit(solution)/shard_map/ppermute | solution.py:509
  51.0 3.7 %collective-permute-done.13.refs_2_.refs_1_ = bf16[256,512]{1,0:T(8,128)(2,1)S(1)} collective-permute-done((bf16[256,512]{1,0:T(8,128)(2,1)S(1)}, bf16[256,512]{1,0:T(8,128)(2,1)S(1)}, u32[]{:S(2)}, u32[]{:S(2)}) %collective-permute-start.13) | collective-permute-done | bytes 262176 | tf_op jit(solution)/shard_map/ppermute | solution.py:509
  55.2 1.3 %collective-permute-start.17 = (bf16[256,512]{1,0:T(8,128)(2,1)S(1)}, bf16[256,512]{1,0:T(8,128)(2,1)S(1)}, u32[]{:S(2)}, u32[]{:S(2)}) collective-permute-start(bf16[256,512]{1,0:T(8,128)(2,1)S(1)} %combine.18.refs_3_), channel_id=1, source_target_pairs={{8,12},{9,13},{10,14},{11,15},{24,28},{25,29},{26,30},{27,31}} | collective-permute-start | bytes 786440 | tf_op jit(solution)/shard_map/ppermute | solution.py:509
  56.5 4.1 %collective-permute-done.16.refs_2_.refs_1_ = bf16[256,512]{1,0:T(8,128)(2,1)S(1)} collective-permute-done((bf16[256,512]{1,0:T(8,128)(2,1)S(1)}, bf16[256,512]{1,0:T(8,128)(2,1)S(1)}, u32[]{:S(2)}, u32[]{:S(2)}) %collective-permute-start.16) | collective-permute-done | bytes 262176 | tf_op jit(solution)/shard_map/ppermute | solution.py:509
  61.0 1.3 %collective-permute-start.18 = (bf16[256,512]{1,0:T(8,128)(2,1)S(1)}, bf16[256,512]{1,0:T(8,128)(2,1)S(1)}, u32[]{:S(2)}, u32[]{:S(2)}) collective-permute-start(bf16[256,512]{1,0:T(8,128)(2,1)S(1)} %combine.19.refs_3_), channel_id=1, source_target_pairs={{8,12},{9,13},{10,14},{11,15},{24,28},{25,29},{26,30},{27,31}} | collective-permute-start | bytes 786440 | tf_op jit(solution)/shard_map/ppermute | solution.py:509
  62.3 2.0 %finish.2.refs_9_ = bf16[384,4096]{1,0:T(8,128)(2,1)} custom-call(f32[1,4096]{1,0:T(1,128)S(1)} %get-tuple-element.73.gain_ref, f32[384,512]{1,0:T(8,128)S(1)} %get-tuple-element.137.refs_0_, f32[384,512]{1,0:T(8,128)S(1)} %get-tuple-element.138.refs_1_, f32[384,512]{1,0:T(8,128)S(1)} %get-tuple-element.139.refs_2_, ...), custom_call_target="tpu_custom_call" | custom-call | flops 1024 | bytes 1024 | tf_op jit(solution)/shard_map/finish/pallas_call | solution.py:471
  64.3 1.9 %collective-permute-done.17.refs_2_ = bf16[256,512]{1,0:T(8,128)(2,1)S(1)} collective-permute-done((bf16[256,512]{1,0:T(8,128)(2,1)S(1)}, bf16[256,512]{1,0:T(8,128)(2,1)S(1)}, u32[]{:S(2)}, u32[]{:S(2)}) %collective-permute-start.17) | collective-permute-done | bytes 262176 | tf_op jit(solution)/shard_map/ppermute | solution.py:509
  66.5 4.8 %collective-permute-done.18.refs_2_ = bf16[256,512]{1,0:T(8,128)(2,1)S(1)} collective-permute-done((bf16[256,512]{1,0:T(8,128)(2,1)S(1)}, bf16[256,512]{1,0:T(8,128)(2,1)S(1)}, u32[]{:S(2)}, u32[]{:S(2)}) %collective-permute-start.18) | collective-permute-done | bytes 262176 | tf_op jit(solution)/shard_map/ppermute | solution.py:509
  71.7 2.0 %finish.3 = bf16[384,4096]{1,0:T(8,128)(2,1)} custom-call(f32[1,4096]{1,0:T(1,128)S(1)} %get-tuple-element.73.gain_ref, f32[384,512]{1,0:T(8,128)S(1)} %get-tuple-element.123.refs_0_, f32[384,512]{1,0:T(8,128)S(1)} %get-tuple-element.127.refs_1_, f32[384,512]{1,0:T(8,128)S(1)} %get-tuple-element.131.refs_2_, ...), custom_call_target="tpu_custom_call", output_to_operand_aliasing={{}: (10, {})} | custom-call | flops 1024 | bytes 1024 | tf_op jit(solution)/shard_map/finish/pallas_call | solution.py:471
  (50 shorter events, 10.4 us)
Async XLA Ops:
  2.2 5.9 %collective-permute-start = (bf16[3,5120]{1,0:T(4,128)(2,1)S(1)}, bf16[3,5120]{1,0:T(4,128)(2,1)S(1)}, u32[]{:S(2)}, u32[]{:S(2)}) collective-permute-start(bf16[3,5120]{1,0:T(4,128)(2,1)S(1)} %pad_maximum_fusion), channel_id=1, source_target_pairs={{0,4},{4,8},{8,12},{1,5},{5,9},{9,13},{2,6},{6,10},{10,14},{3,7},{... | collective-permute-start | bytes 92168 | tf_op jit(solution)/shard_map/ppermute | solution.py:377
  3.5 10.8 %collective-permute-start.1 = (bf16[256,512]{1,0:T(8,128)(2,1)S(1)}, bf16[256,512]{1,0:T(8,128)(2,1)S(1)}, u32[]{:S(2)}, u32[]{:S(2)}) collective-permute-start(bf16[256,512]{1,0:T(8,128)(2,1)S(1)} %first.8.gate_ref), channel_id=1, source_target_pairs={{0,4},{1,5},{2,6},{3,7},{16,20},{17,21},{18,22},{19,23}} | collective-permute-start | bytes 786440 | tf_op jit(solution)/shard_map/ppermute | solution.py:344
  10.1 7.3 %collective-permute-start.2 = (bf16[256,512]{1,0:T(8,128)(2,1)S(1)}, bf16[256,512]{1,0:T(8,128)(2,1)S(1)}, u32[]{:S(2)}, u32[]{:S(2)}) collective-permute-start(bf16[256,512]{1,0:T(8,128)(2,1)S(1)} %first.9.gate_ref), channel_id=1, source_target_pairs={{0,4},{1,5},{2,6},{3,7},{16,20},{17,21},{18,22},{19,23}} | collective-permute-start | bytes 786440 | tf_op jit(solution)/shard_map/ppermute | solution.py:344
  13.7 6.2 %collective-permute-start.3 = (bf16[256,512]{1,0:T(8,128)(2,1)S(1)}, bf16[256,512]{1,0:T(8,128)(2,1)S(1)}, u32[]{:S(2)}, u32[]{:S(2)}) collective-permute-start(bf16[256,512]{1,0:T(8,128)(2,1)S(1)} %first.10.refs_3_), channel_id=1, source_target_pairs={{0,4},{1,5},{2,6},{3,7},{16,20},{17,21},{18,22},{19,23}} | collective-permute-start | bytes 786440 | tf_op jit(solution)/shard_map/ppermute | solution.py:344
  14.4 5.4 %collective-permute-start.4 = (bf16[256,512]{1,0:T(8,128)(2,1)S(1)}, bf16[256,512]{1,0:T(8,128)(2,1)S(1)}, u32[]{:S(2)}, u32[]{:S(2)}) collective-permute-start(bf16[256,512]{1,0:T(8,128)(2,1)S(1)} %combine.10.gate_ref), channel_id=1, source_target_pairs={{4,8},{5,9},{6,10},{7,11},{20,24},{21,25},{22,26},{23,27}} | collective-permute-start | bytes 786440 | tf_op jit(solution)/shard_map/ppermute | solution.py:509
  15.2 8.3 %collective-permute-start.5 = (bf16[256,512]{1,0:T(8,128)(2,1)S(1)}, bf16[256,512]{1,0:T(8,128)(2,1)S(1)}, u32[]{:S(2)}, u32[]{:S(2)}) collective-permute-start(bf16[256,512]{1,0:T(8,128)(2,1)S(1)} %first.11.gate_ref), channel_id=1, source_target_pairs={{0,4},{1,5},{2,6},{3,7},{16,20},{17,21},{18,22},{19,23}} | collective-permute-start | bytes 786440 | tf_op jit(solution)/shard_map/ppermute | solution.py:344
  17.4 6.0 %collective-permute-start.6 = (bf16[256,512]{1,0:T(8,128)(2,1)S(1)}, bf16[256,512]{1,0:T(8,128)(2,1)S(1)}, u32[]{:S(2)}, u32[]{:S(2)}) collective-permute-start(bf16[256,512]{1,0:T(8,128)(2,1)S(1)} %combine.11.gate_ref), channel_id=1, source_target_pairs={{4,8},{5,9},{6,10},{7,11},{20,24},{21,25},{22,26},{23,27}} | collective-permute-start | bytes 786440 | tf_op jit(solution)/shard_map/ppermute | solution.py:509
  20.0 10.5 %collective-permute-start.8 = (bf16[256,512]{1,0:T(8,128)(2,1)S(1)}, bf16[256,512]{1,0:T(8,128)(2,1)S(1)}, u32[]{:S(2)}, u32[]{:S(2)}) collective-permute-start(bf16[256,512]{1,0:T(8,128)(2,1)S(1)} %combine.12.gate_ref), channel_id=1, source_target_pairs={{4,8},{8,12},{5,9},{9,13},{6,10},{10,14},{7,11},{11,15},{20,24},{2... | collective-permute-start | bytes 786440 | tf_op jit(solution)/shard_map/ppermute | solution.py:509
  21.3 9.5 %collective-permute-start.7 = (bf16[256,512]{1,0:T(8,128)(2,1)S(1)}, bf16[256,512]{1,0:T(8,128)(2,1)S(1)}, u32[]{:S(2)}, u32[]{:S(2)}) collective-permute-start(bf16[256,512]{1,0:T(8,128)(2,1)S(1)} %first.12.gate_ref), channel_id=1, source_target_pairs={{0,4},{1,5},{2,6},{3,7},{16,20},{17,21},{18,22},{19,23}} | collective-permute-start | bytes 786440 | tf_op jit(solution)/shard_map/ppermute | solution.py:344
  23.6 12.4 %collective-permute-start.11 = (bf16[256,512]{1,0:T(8,128)(2,1)S(1)}, bf16[256,512]{1,0:T(8,128)(2,1)S(1)}, u32[]{:S(2)}, u32[]{:S(2)}) collective-permute-start(bf16[256,512]{1,0:T(8,128)(2,1)S(1)} %combine.13.gate_ref), channel_id=1, source_target_pairs={{4,8},{8,12},{5,9},{9,13},{6,10},{10,14},{7,11},{11,15},{20,24},{2... | collective-permute-start | bytes 786440 | tf_op jit(solution)/shard_map/ppermute | solution.py:509
  24.9 11.4 %collective-permute-start.10 = (bf16[256,512]{1,0:T(8,128)(2,1)S(1)}, bf16[256,512]{1,0:T(8,128)(2,1)S(1)}, u32[]{:S(2)}, u32[]{:S(2)}) collective-permute-start(bf16[256,512]{1,0:T(8,128)(2,1)S(1)} %first.13.gate_ref), channel_id=1, source_target_pairs={{0,4},{1,5},{2,6},{3,7},{16,20},{17,21},{18,22},{19,23}} | collective-permute-start | bytes 786440 | tf_op jit(solution)/shard_map/ppermute | solution.py:344
  31.0 12.0 %collective-permute-start.12 = (bf16[256,512]{1,0:T(8,128)(2,1)S(1)}, bf16[256,512]{1,0:T(8,128)(2,1)S(1)}, u32[]{:S(2)}, u32[]{:S(2)}) collective-permute-start(bf16[256,512]{1,0:T(8,128)(2,1)S(1)} %first.14.gate_ref), channel_id=1, source_target_pairs={{0,4},{1,5},{2,6},{3,7},{16,20},{17,21},{18,22},{19,23}} | collective-permute-start | bytes 786440 | tf_op jit(solution)/shard_map/ppermute | solution.py:344
  31.7 11.0 %collective-permute-start.9 = (bf16[256,512]{1,0:T(8,128)(2,1)S(1)}, bf16[256,512]{1,0:T(8,128)(2,1)S(1)}, u32[]{:S(2)}, u32[]{:S(2)}) collective-permute-start(bf16[256,512]{1,0:T(8,128)(2,1)S(1)} %combine.14.gate_ref), channel_id=1, source_target_pairs={{4,8},{8,12},{5,9},{9,13},{6,10},{10,14},{7,11},{11,15},{20,24},{2... | collective-permute-start | bytes 786440 | tf_op jit(solution)/shard_map/ppermute | solution.py:509
  36.5 12.7 %collective-permute-start.15 = (bf16[256,512]{1,0:T(8,128)(2,1)S(1)}, bf16[256,512]{1,0:T(8,128)(2,1)S(1)}, u32[]{:S(2)}, u32[]{:S(2)}) collective-permute-start(bf16[256,512]{1,0:T(8,128)(2,1)S(1)} %combine.15.gate_ref), channel_id=1, source_target_pairs={{4,8},{8,12},{5,9},{9,13},{6,10},{10,14},{7,11},{11,15},{20,24},{2... | collective-permute-start | bytes 786440 | tf_op jit(solution)/shard_map/ppermute | solution.py:509
  37.8 11.8 %collective-permute-start.14 = (bf16[256,512]{1,0:T(8,128)(2,1)S(1)}, bf16[256,512]{1,0:T(8,128)(2,1)S(1)}, u32[]{:S(2)}, u32[]{:S(2)}) collective-permute-start(bf16[256,512]{1,0:T(8,128)(2,1)S(1)} %first.15.gate_ref), channel_id=1, source_target_pairs={{0,4},{1,5},{2,6},{3,7},{16,20},{17,21},{18,22},{19,23}} | collective-permute-start | bytes 786440 | tf_op jit(solution)/shard_map/ppermute | solution.py:344
  43.1 11.6 %collective-permute-start.13 = (bf16[256,512]{1,0:T(8,128)(2,1)S(1)}, bf16[256,512]{1,0:T(8,128)(2,1)S(1)}, u32[]{:S(2)}, u32[]{:S(2)}) collective-permute-start(bf16[256,512]{1,0:T(8,128)(2,1)S(1)} %combine.16.gate_ref), channel_id=1, source_target_pairs={{4,8},{8,12},{5,9},{9,13},{6,10},{10,14},{7,11},{11,15},{20,24},{2... | collective-permute-start | bytes 786440 | tf_op jit(solution)/shard_map/ppermute | solution.py:509
  49.7 10.9 %collective-permute-start.16 = (bf16[256,512]{1,0:T(8,128)(2,1)S(1)}, bf16[256,512]{1,0:T(8,128)(2,1)S(1)}, u32[]{:S(2)}, u32[]{:S(2)}) collective-permute-start(bf16[256,512]{1,0:T(8,128)(2,1)S(1)} %combine.17.refs_3_), channel_id=1, source_target_pairs={{4,8},{8,12},{5,9},{9,13},{6,10},{10,14},{7,11},{11,15},{20,24},{2... | collective-permute-start | bytes 786440 | tf_op jit(solution)/shard_map/ppermute | solution.py:509
  55.2 11.0 %collective-permute-start.17 = (bf16[256,512]{1,0:T(8,128)(2,1)S(1)}, bf16[256,512]{1,0:T(8,128)(2,1)S(1)}, u32[]{:S(2)}, u32[]{:S(2)}) collective-permute-start(bf16[256,512]{1,0:T(8,128)(2,1)S(1)} %combine.18.refs_3_), channel_id=1, source_target_pairs={{8,12},{9,13},{10,14},{11,15},{24,28},{25,29},{26,30},{27,31}} | collective-permute-start | bytes 786440 | tf_op jit(solution)/shard_map/ppermute | solution.py:509
  61.0 10.4 %collective-permute-start.18 = (bf16[256,512]{1,0:T(8,128)(2,1)S(1)}, bf16[256,512]{1,0:T(8,128)(2,1)S(1)}, u32[]{:S(2)}, u32[]{:S(2)}) collective-permute-start(bf16[256,512]{1,0:T(8,128)(2,1)S(1)} %combine.19.refs_3_), channel_id=1, source_target_pairs={{8,12},{9,13},{10,14},{11,15},{24,28},{25,29},{26,30},{27,31}} | collective-permute-start | bytes 786440 | tf_op jit(solution)/shard_map/ppermute | solution.py:509

commit v4 on v3

--- a/solution.py
+++ b/solution.py
@@ -253,18 +253,22 @@
     sent_ref[...] = (total * value + state).astype(sent_ref.dtype)
 
 
-def absorb_kernel(group, owners, left_ref, part_ref, reach_ref, place_ref, *refs):
-    length, width = part_ref.shape
-    gated_ref, square_ref = refs[-2:]
-    place = place_ref[0]
+def arrived_state(place, owners, refs):
     incoming = refs[0][...].astype(F32)
     for owner, other in zip(owners[1:], refs[1:]):
         incoming = jnp.where(place >= owner, other[...].astype(F32), incoming)
-    incoming = incoming.astype(BF16)
+    return incoming.astype(BF16)
+
+
+def absorb_kernel(group, chunk, owners, place_ref, left_ref, gain_ref, part_ref, reach_ref, *refs):
+    length, width = part_ref.shape
+    gated_ref, square_ref = refs[-2:]
+    incoming = arrived_state(place_ref[0], owners, refs[: len(owners)])
+    gain = gain_ref[:, chunk * CHUNK : (chunk + 1) * CHUNK]
     for start in range(0, length, SUB):
         rows = slice(start, start + SUB)
         value = part_ref[rows] + reach_ref[rows] * dot(left_ref[group, rows, SUB:], incoming)
-        gated_ref[rows, :] = value
+        gated_ref[rows, :] = value * gain
         power = value * value
         total = power[:, :128]
         for lane in range(128, width, 128):
@@ -272,21 +276,39 @@
         square_ref[rows, :] = total
 
 
-def finish_kernel(group, chunks, gain_ref, *refs):
-    gated = refs[:chunks]
-    squares = refs[chunks : 2 * chunks]
-    out_ref = refs[-1]
-    height = out_ref.shape[0]
-    rows = pl.ds(pl.multiple_of(pl.program_id(0) * height, height), height)
-    total = squares[0][rows, :]
-    for square in squares[1:]:
-        total = total + square[rows, :]
-    mean = jnp.sum(total, axis=1, keepdims=True) * (1.0 / (CHUNK * chunks))
-    scale = lax.rsqrt(mean + 1e-05)
-    for index in range(chunks):
-        lanes = slice(index * CHUNK, (index + 1) * CHUNK)
-        start = (group * chunks + index) * CHUNK
-        out_ref[:, lanes] = (gated[index][rows, :] * scale * gain_ref[:, start : start + CHUNK]).astype(BF16)
+def finish_kernel(group, chunks, owners, place_ref, left_ref, gain_ref, part_ref, reach_ref, *refs):
+    length, width = part_ref.shape
+    came, refs = refs[: len(owners)], refs[len(owners) :]
+    gated, squares = refs[: chunks - 1], refs[chunks - 1 : 2 * chunks - 2]
+    out_hbm, out_ref, sems = refs[-3:]
+    incoming = arrived_state(place_ref[0], owners, came)
+    first_lane = group * chunks * width
+    last = slice(first_lane + (chunks - 1) * width, first_lane + chunks * width)
+    copies = []
+    for start in range(0, length, SUB):
+        rows = slice(start, start + SUB)
+        value = part_ref[rows] + reach_ref[rows] * dot(left_ref[group, rows, SUB:], incoming)
+        square = jnp.sum(value * value, axis=1, keepdims=True)
+        if chunks > 1:
+            total = squares[0][rows]
+            for other in squares[1:]:
+                total = total + other[rows]
+            square = square + jnp.sum(total, axis=1, keepdims=True)
+        scale = lax.rsqrt(square * (1.0 / (width * chunks)) + 1e-05)
+        for index in range(chunks):
+            scaled = value * gain_ref[:, last] if index == chunks - 1 else gated[index][rows]
+            lanes = slice(index * width, (index + 1) * width)
+            out_ref[rows, lanes] = (scaled * scale).astype(BF16)
+            copies.append(
+                pltpu.make_async_copy(
+                    out_ref.at[rows, lanes],
+                    out_hbm.at[rows, first_lane + index * width : first_lane + (index + 1) * width],
+                    sems.at[len(copies)],
+                )
+            )
+            copies[-1].start()
+    for copy in copies:
+        copy.wait()
 
 
 def shards(x_in, bc_in, z_in, dt_in, conv_x, conv_bc, dt_bias, a_log, d_skip, norm_gain):
@@ -444,11 +466,10 @@
         )(place, *lanes, *states, *came, gate)
 
     def absorb(chunk, owners, came, gate):
-        group = chunk // in_group
         part, reach = pieces[chunk][:2]
         return pl.pallas_call(
-            functools.partial(absorb_kernel, group, owners),
-            in_specs=[near] * 3 + [scalar] + [near] * (1 + len(came)),
+            functools.partial(absorb_kernel, chunk // in_group, chunk, owners),
+            in_specs=[scalar] + [near] * (5 + len(came)),
             out_specs=(near, near),
             out_shape=(
                 jax.ShapeDtypeStruct((length, CHUNK), F32),
@@ -457,24 +478,28 @@
             compiler_params=pltpu.CompilerParams(vmem_limit_bytes=8 << 20),
             cost_estimate=COST,
             name="absorb",
-        )(left, part, reach, place, *came, gate)
-
-    def finish(group, done, out, gate):
-        rows = SUB
-        operands = [gain] + [pair[0] for pair in done] + [pair[1] for pair in done] + [gate]
-        specs = [near] * len(operands)
+        )(place, left, gain, part, reach, *came, gate)
+
+    def finish(chunk, owners, came, done, out, gate):
+        part, reach = pieces[chunk][:2]
+        operands = [place, left, gain, part, reach, *came]
+        operands += [pair[0] for pair in done] + [pair[1] for pair in done] + [gate]
+        specs = [scalar] + [near] * (len(operands) - 1)
         aliases = {}
         if out is not None:
             aliases = {len(operands): 0}
-            operands.append(out)
-            specs.append(pl.BlockSpec(memory_space=pl.ANY))
+            operands.append(far(out))
+            specs.append(afar)
         return pl.pallas_call(
-            functools.partial(finish_kernel, group, in_group),
-            grid=(length // rows,),
+            functools.partial(finish_kernel, chunk // in_group, in_group, owners),
             in_specs=specs,
-            out_specs=pl.BlockSpec((rows, per_group), lambda i: (i, group)),
+            out_specs=afar,
             out_shape=jax.ShapeDtypeStruct((length, channels), BF16),
             input_output_aliases=aliases,
+            scratch_shapes=[
+                pltpu.VMEM((length, per_group), BF16),
+                pltpu.SemaphoreType.DMA((length // SUB * in_group,)),
+            ],
             compiler_params=pltpu.CompilerParams(vmem_limit_bytes=12 << 20),
             cost_estimate=COST,
             name="finish",
@@ -517,11 +542,12 @@
         if 0 <= chunk < count:
             owners = [0] + list(range(2, contexts))
             came = [from_first[chunk]] + [from_later[chunk + 2 * (i - 2)] for i in owners[1:]]
-            done.append(absorb(chunk, owners, came, gate))
-            gate = done[-1][1]
-            if (chunk + 1) % in_group == 0:
-                group = chunk // in_group
-                out = finish(group, done[group * in_group :], out, gate)
+            if (chunk + 1) % in_group:
+                done.append(absorb(chunk, owners, came, gate))
+                gate = done[-1][1]
+            else:
+                out = finish(chunk, owners, came, done, out, gate)
+                done = []
     return out
 
 

time: 74.2 us -> 73.4 us (0.989)
  Pallas kernels: 25.3 us -> 24.3 us
    pallas_call x10 -> x8, Pallas kernels: 6.73 us -> 5.67 us  [the longest x2 3.47 us: finish(): pl.pallas_call(functools.partial(finish_kernel, chunk // in_group, in_gro...]
where the time goes in v4:
time: 73.4 us; the launch traced here: 72.9 us
  waiting for transfers between devices  29.2 us (40%)
  Pallas kernels  24.3 us (33%)
  starting transfers between devices  18.6 us (25%)
    ppermute x10, waiting for transfers between devices, shards(): lax.ppermute(gate, 'ctx', [(owner, owner + 1) for owner in senders])  25.2 us
    pallas_call x8, Pallas kernels, local(): pl.pallas_call(functools.partial(local_kernel, group, chunk, which), in_s...  12 us
    ppermute x10, starting transfers between devices, shards(): lax.ppermute(gate, 'ctx', [(owner, owner + 1) for owner in senders])  11.7 us
    ppermute x8, starting transfers between devices, send(): from_first.append(lax.ppermute(value, 'ctx', [(0, 1)]))  5.64 us
    ppermute x1, waiting for transfers between devices, shards(): early = lax.ppermute(early, 'ctx', ahead)  3.91 us
    pallas_call x2, Pallas kernels, finish(): pl.pallas_call(functools.partial(finish_kernel, chunk // in_group, in_gro...  3.47 us
    pallas_call x6, Pallas kernels, absorb(): pl.pallas_call(functools.partial(absorb_kernel, chunk // in_group, chunk,...  2.19 us
    pallas_call x1, Pallas kernels, shards(): pl.pallas_call(steps_kernel, in_specs=[pl.BlockSpec(memory_space=pltpu.HB...  2 us
  transfers between devices with their start and end apart: 19, of which 9 were waited for; matrix products, arithmetic and copies ran while one was open for 0% of the time, Pallas kernels for 28%

profile of v4, /device:TPU:28, one launch (start us, length us, event | category | flops | bytes accessed | tf_op | source)
XLA Modules:
  0.0 72.9 jit_solution(16221976645406553244)
XLA Ops:
  0.0 2.0 %steps.1 = (bf16[384,1024]{1,0:T(8,128)(2,1)S(1)}, bf16[8,4096]{1,0:T(8,128)(2,1)S(1)}, f32[4,4096]{1,0:T(4,128)S(1)}, f32[4,2,512]{2,1,0:T(2,128)S(1)}, bf16[38...) custom-call(bf16[384,4096]{1,0:T(8,128)(2,1)} %refs_0_.7, ...), custom_call_target="tpu_custom_call" | custom-call | flops 1024 | bytes 1024 | tf_op jit(solution)/shard_map/steps/pallas_call | solution.py:331
  2.2 1.3 %collective-permute-start = (bf16[3,5120]{1,0:T(4,128)(2,1)S(1)}, bf16[3,5120]{1,0:T(4,128)(2,1)S(1)}, u32[]{:S(2)}, u32[]{:S(2)}) collective-permute-start(bf16[3,5120]{1,0:T(4,128)(2,1)S(1)} %pad_maximum_fusion), channel_id=1, source_target_pairs={{0,4},{4,8},{8,12},{1,5},{5,9},{9,13},{2,6},{6,10},{10,14},{3,7},{... | collective-permute-start | bytes 92168 | tf_op jit(solution)/shard_map/ppermute | solution.py:399
  4.2 3.9 %collective-permute-done.early_ref = bf16[3,5120]{1,0:T(4,128)(2,1)S(1)} collective-permute-done((bf16[3,5120]{1,0:T(4,128)(2,1)S(1)}, bf16[3,5120]{1,0:T(4,128)(2,1)S(1)}, u32[]{:S(2)}, u32[]{:S(2)}) %collective-permute-start) | collective-permute-done | bytes 30752 | tf_op jit(solution)/shard_map/ppermute | solution.py:399
  8.1 1.9 %groups.1 = (bf16[2,384,384]{2,1,0:T(8,128)(2,1)S(1)}, bf16[2,256,384]{2,1,0:T(8,128)(2,1)S(1)}, bf16[384,1024]{1,0:T(8,128)(2,1)S(1)}) custom-call(bf16[384,1024]{1,0:T(8,128)(2,1)S(1)} %bitcast.12, bf16[3,5120]{1,0:T(4,128)(2,1)S(1)} %collective-permute-done.early_ref, f32[4,2,512]{2,1,0:T(2,128)S(1)} %get-tuple-element.75.bc_taps_ref.taps_ref, ...), custom_call_target="tpu_custom_call" | custom-call | flops 1024 | bytes 1024 | tf_op jit(solution)/shard_map/groups/pallas_call | solution.py:416
  10.7 1.4 %stage.1 = (bf16[384,1024]{1,0:T(8,128)(2,1)S(1)}, bf16[384,1024]{1,0:T(8,128)(2,1)S(1)}) custom-call(bf16[256,512]{1,0:T(8,128)(2,1)S(1)} %first.8.gate_ref, bf16[384,4096]{1,0:T(8,128)(2,1)} %refs_1_.5, bf16[384,4096]{1,0:T(8,128)(2,1)} %refs_0_.7), custom_call_target="tpu_custom_call" | custom-call | flops 1024 | bytes 1024 | tf_op jit(solution)/shard_map/stage/pallas_call | solution.py:403
  12.1 1.5 %local.8 = (f32[384,512]{1,0:T(8,128)S(1)}, f32[384,512]{1,0:T(8,128)S(1)}, f32[256,512]{1,0:T(8,128)S(1)}, f32[8,512]{1,0:T(8,128)S(1)}, bf16[384,1024]{1,0:T(8,128)(2,1)S(1)}, /*index=5*/bf16[384,1024]{1,0:T(8,128)(2,1)S(1)}) custom-call(bf16[384,1024]{1,0:T(8,128)(2,1)S(1)} %get-tuple-element.71.x_ref, ...), custom_call_target="tpu_custom_call" | custom-call | flops 1024 | bytes 1024 | tf_op jit(solution)/shard_map/local/pallas_call | solution.py:434
  13.7 0.7 collective-permute-start.3
  15.8 1.5 %local.9 = (f32[384,512]{1,0:T(8,128)S(1)}, f32[384,512]{1,0:T(8,128)S(1)}, f32[256,512]{1,0:T(8,128)S(1)}, f32[8,512]{1,0:T(8,128)S(1)}, bf16[384,1024]{1,0:T(8,128)(2,1)S(1)}, /*index=5*/bf16[384,1024]{1,0:T(8,128)(2,1)S(1)}) custom-call(bf16[384,1024]{1,0:T(8,128)(2,1)S(1)} %get-tuple-element.71.x_ref, ...), custom_call_target="tpu_custom_call" | custom-call | flops 1024 | bytes 1024 | tf_op jit(solution)/shard_map/local/pallas_call | solution.py:434
  18.3 1.5 %local.10 = (f32[384,512]{1,0:T(8,128)S(1)}, f32[384,512]{1,0:T(8,128)S(1)}, f32[256,512]{1,0:T(8,128)S(1)}, f32[8,512]{1,0:T(8,128)S(1)}) custom-call(bf16[384,1024]{1,0:T(8,128)(2,1)S(1)} %get-tuple-element.83.x_ref, bf16[3,5120]{1,0:T(4,128)(2,1)S(1)} %collective-permute-done.early_ref, f32[4,4096]{1,0:T(4,128)S(1)} %get-tuple-element.72.taps_ref, ...), custom_call_target="tpu_custom_call" | custom-call | flops 1024 | bytes 1024 | tf_op jit(solution)/shard_map/local/pallas_call | solution.py:434
  20.0 1.3 %collective-permute-start.8 = (bf16[256,512]{1,0:T(8,128)(2,1)S(1)}, bf16[256,512]{1,0:T(8,128)(2,1)S(1)}, u32[]{:S(2)}, u32[]{:S(2)}) collective-permute-start(bf16[256,512]{1,0:T(8,128)(2,1)S(1)} %combine.12.gate_ref), channel_id=1, source_target_pairs={{4,8},{8,12},{5,9},{9,13},{6,10},{10,14},{7,11},{11,15},{20,24},{2... | collective-permute-start | bytes 786440 | tf_op jit(solution)/shard_map/ppermute | solution.py:534
  21.3 0.7 collective-permute-start.7
  22.0 1.5 %local.11 = (f32[384,512]{1,0:T(8,128)S(1)}, f32[384,512]{1,0:T(8,128)S(1)}, f32[256,512]{1,0:T(8,128)S(1)}, f32[8,512]{1,0:T(8,128)S(1)}) custom-call(bf16[384,1024]{1,0:T(8,128)(2,1)S(1)} %get-tuple-element.83.x_ref, bf16[3,5120]{1,0:T(4,128)(2,1)S(1)} %collective-permute-done.early_ref, f32[4,4096]{1,0:T(4,128)S(1)} %get-tuple-element.72.taps_ref, ...), custom_call_target="tpu_custom_call" | custom-call | flops 1024 | bytes 1024 | tf_op jit(solution)/shard_map/local/pallas_call | solution.py:434
  23.6 1.3 %collective-permute-start.10 = (bf16[256,512]{1,0:T(8,128)(2,1)S(1)}, bf16[256,512]{1,0:T(8,128)(2,1)S(1)}, u32[]{:S(2)}, u32[]{:S(2)}) collective-permute-start(bf16[256,512]{1,0:T(8,128)(2,1)S(1)} %combine.13.gate_ref), channel_id=1, source_target_pairs={{4,8},{8,12},{5,9},{9,13},{6,10},{10,14},{7,11},{11,15},{20,24},{2... | collective-permute-start | bytes 786440 | tf_op jit(solution)/shard_map/ppermute | solution.py:534
  25.6 1.5 %local.12 = (f32[384,512]{1,0:T(8,128)S(1)}, f32[384,512]{1,0:T(8,128)S(1)}, f32[256,512]{1,0:T(8,128)S(1)}, f32[8,512]{1,0:T(8,128)S(1)}) custom-call(bf16[384,1024]{1,0:T(8,128)(2,1)S(1)} %get-tuple-element.88.x_ref, bf16[3,5120]{1,0:T(4,128)(2,1)S(1)} %collective-permute-done.early_ref, f32[4,4096]{1,0:T(4,128)S(1)} %get-tuple-element.72.taps_ref, ...), custom_call_target="tpu_custom_call" | custom-call | flops 1024 | bytes 1024 | tf_op jit(solution)/shard_map/local/pallas_call | solution.py:434
  27.1 3.3 %collective-permute-done.8.refs_2_.refs_5_.refs_1_ = bf16[256,512]{1,0:T(8,128)(2,1)S(1)} collective-permute-done((bf16[256,512]{1,0:T(8,128)(2,1)S(1)}, bf16[256,512]{1,0:T(8,128)(2,1)S(1)}, u32[]{:S(2)}, u32[]{:S(2)}) %collective-permute-start.8) | collective-permute-done | bytes 262176 | tf_op jit(solution)/shard_map/ppermute | solution.py:534
  31.0 1.3 %collective-permute-start.12 = (bf16[256,512]{1,0:T(8,128)(2,1)S(1)}, bf16[256,512]{1,0:T(8,128)(2,1)S(1)}, u32[]{:S(2)}, u32[]{:S(2)}) collective-permute-start(bf16[256,512]{1,0:T(8,128)(2,1)S(1)} %combine.14.gate_ref), channel_id=1, source_target_pairs={{4,8},{8,12},{5,9},{9,13},{6,10},{10,14},{7,11},{11,15},{20,24},{2... | collective-permute-start | bytes 786440 | tf_op jit(solution)/shard_map/ppermute | solution.py:534
  33.0 0.9 %collective-permute-start.13 = (bf16[256,512]{1,0:T(8,128)(2,1)S(1)}, bf16[256,512]{1,0:T(8,128)(2,1)S(1)}, u32[]{:S(2)}, u32[]{:S(2)}) collective-permute-start(bf16[256,512]{1,0:T(8,128)(2,1)S(1)} %first.15.gate_ref), channel_id=1, source_target_pairs={{0,4},{1,5},{2,6},{3,7},{16,20},{17,21},{18,22},{19,23}} | collective-permute-start | bytes 786440 | tf_op jit(solution)/shard_map/ppermute | solution.py:366
  33.9 1.5 %local.13 = (f32[384,512]{1,0:T(8,128)S(1)}, f32[384,512]{1,0:T(8,128)S(1)}, f32[256,512]{1,0:T(8,128)S(1)}, f32[8,512]{1,0:T(8,128)S(1)}) custom-call(bf16[384,1024]{1,0:T(8,128)(2,1)S(1)} %get-tuple-element.88.x_ref, bf16[3,5120]{1,0:T(4,128)(2,1)S(1)} %collective-permute-done.early_ref, f32[4,4096]{1,0:T(4,128)S(1)} %get-tuple-element.72.taps_ref, ...), custom_call_target="tpu_custom_call" | custom-call | flops 1024 | bytes 1024 | tf_op jit(solution)/shard_map/local/pallas_call | solution.py:434
  36.5 1.3 %collective-permute-start.14 = (bf16[256,512]{1,0:T(8,128)(2,1)S(1)}, bf16[256,512]{1,0:T(8,128)(2,1)S(1)}, u32[]{:S(2)}, u32[]{:S(2)}) collective-permute-start(bf16[256,512]{1,0:T(8,128)(2,1)S(1)} %combine.15.gate_ref), channel_id=1, source_target_pairs={{4,8},{8,12},{5,9},{9,13},{6,10},{10,14},{7,11},{11,15},{20,24},{2... | collective-permute-start | bytes 786440 | tf_op jit(solution)/shard_map/ppermute | solution.py:534
  37.8 1.5 %local.14 = (f32[384,512]{1,0:T(8,128)S(1)}, f32[384,512]{1,0:T(8,128)S(1)}, f32[256,512]{1,0:T(8,128)S(1)}, f32[8,512]{1,0:T(8,128)S(1)}) custom-call(bf16[384,1024]{1,0:T(8,128)(2,1)S(1)} %get-tuple-element.86.x_ref, bf16[3,5120]{1,0:T(4,128)(2,1)S(1)} %collective-permute-done.early_ref, f32[4,4096]{1,0:T(4,128)S(1)} %get-tuple-element.72.taps_ref, ...), custom_call_target="tpu_custom_call" | custom-call | flops 1024 | bytes 1024 | tf_op jit(solution)/shard_map/local/pallas_call | solution.py:434
  39.3 2.6 %collective-permute-done.12.refs_2_.refs_5_.refs_1_ = bf16[256,512]{1,0:T(8,128)(2,1)S(1)} collective-permute-done((bf16[256,512]{1,0:T(8,128)(2,1)S(1)}, bf16[256,512]{1,0:T(8,128)(2,1)S(1)}, u32[]{:S(2)}, u32[]{:S(2)}) %collective-permute-start.12) | collective-permute-done | bytes 262176 | tf_op jit(solution)/shard_map/ppermute | solution.py:534
  42.5 1.3 %collective-permute-start.16 = (bf16[256,512]{1,0:T(8,128)(2,1)S(1)}, bf16[256,512]{1,0:T(8,128)(2,1)S(1)}, u32[]{:S(2)}, u32[]{:S(2)}) collective-permute-start(bf16[256,512]{1,0:T(8,128)(2,1)S(1)} %combine.16.gate_ref), channel_id=1, source_target_pairs={{4,8},{8,12},{5,9},{9,13},{6,10},{10,14},{7,11},{11,15},{20,24},{2... | collective-permute-start | bytes 786440 | tf_op jit(solution)/shard_map/ppermute | solution.py:534
  43.8 1.5 %local.15 = (f32[384,512]{1,0:T(8,128)S(1)}, f32[384,512]{1,0:T(8,128)S(1)}, f32[256,512]{1,0:T(8,128)S(1)}, f32[8,512]{1,0:T(8,128)S(1)}) custom-call(bf16[384,1024]{1,0:T(8,128)(2,1)S(1)} %get-tuple-element.86.x_ref, bf16[3,5120]{1,0:T(4,128)(2,1)S(1)} %collective-permute-done.early_ref, f32[4,4096]{1,0:T(4,128)S(1)} %get-tuple-element.72.taps_ref, ...), custom_call_target="tpu_custom_call" | custom-call | flops 1024 | bytes 1024 | tf_op jit(solution)/shard_map/local/pallas_call | solution.py:434
  45.3 3.8 %collective-permute-done.14.refs_5_.refs_1_.refs_2_ = bf16[256,512]{1,0:T(8,128)(2,1)S(1)} collective-permute-done((bf16[256,512]{1,0:T(8,128)(2,1)S(1)}, bf16[256,512]{1,0:T(8,128)(2,1)S(1)}, u32[]{:S(2)}, u32[]{:S(2)}) %collective-permute-start.14) | collective-permute-done | bytes 262176 | tf_op jit(solution)/shard_map/ppermute | solution.py:534
  49.2 1.3 %collective-permute-start.15 = (bf16[256,512]{1,0:T(8,128)(2,1)S(1)}, bf16[256,512]{1,0:T(8,128)(2,1)S(1)}, u32[]{:S(2)}, u32[]{:S(2)}) collective-permute-start(bf16[256,512]{1,0:T(8,128)(2,1)S(1)} %combine.17.refs_3_), channel_id=1, source_target_pairs={{4,8},{8,12},{5,9},{9,13},{6,10},{10,14},{7,11},{11,15},{20,24},{2... | collective-permute-start | bytes 786440 | tf_op jit(solution)/shard_map/ppermute | solution.py:534
  50.5 5.2 %collective-permute-done.16.refs_2_.refs_1_ = bf16[256,512]{1,0:T(8,128)(2,1)S(1)} collective-permute-done((bf16[256,512]{1,0:T(8,128)(2,1)S(1)}, bf16[256,512]{1,0:T(8,128)(2,1)S(1)}, u32[]{:S(2)}, u32[]{:S(2)}) %collective-permute-start.16) | collective-permute-done | bytes 262176 | tf_op jit(solution)/shard_map/ppermute | solution.py:534
  56.1 1.3 %collective-permute-start.18 = (bf16[256,512]{1,0:T(8,128)(2,1)S(1)}, bf16[256,512]{1,0:T(8,128)(2,1)S(1)}, u32[]{:S(2)}, u32[]{:S(2)}) collective-permute-start(bf16[256,512]{1,0:T(8,128)(2,1)S(1)} %combine.18.refs_3_), channel_id=1, source_target_pairs={{8,12},{9,13},{10,14},{11,15},{24,28},{25,29},{26,30},{27,31}} | collective-permute-start | bytes 786440 | tf_op jit(solution)/shard_map/ppermute | solution.py:534
  57.4 4.7 %collective-permute-done.15.refs_2_.refs_1_ = bf16[256,512]{1,0:T(8,128)(2,1)S(1)} collective-permute-done((bf16[256,512]{1,0:T(8,128)(2,1)S(1)}, bf16[256,512]{1,0:T(8,128)(2,1)S(1)}, u32[]{:S(2)}, u32[]{:S(2)}) %collective-permute-start.15) | collective-permute-done | bytes 262176 | tf_op jit(solution)/shard_map/ppermute | solution.py:534
  62.6 1.3 %collective-permute-start.17 = (bf16[256,512]{1,0:T(8,128)(2,1)S(1)}, bf16[256,512]{1,0:T(8,128)(2,1)S(1)}, u32[]{:S(2)}, u32[]{:S(2)}) collective-permute-start(bf16[256,512]{1,0:T(8,128)(2,1)S(1)} %combine.19.refs_3_), channel_id=1, source_target_pairs={{8,12},{9,13},{10,14},{11,15},{24,28},{25,29},{26,30},{27,31}} | collective-permute-start | bytes 786440 | tf_op jit(solution)/shard_map/ppermute | solution.py:534
  63.9 1.7 %finish.2.refs_10_ = bf16[384,4096]{1,0:T(8,128)(2,1)} custom-call(s32[1]{0:T(128)} %bitcast.place_ref, bf16[2,384,384]{2,1,0:T(8,128)(2,1)S(1)} %get-tuple-element.77.left_ref, f32[1,4096]{1,0:T(1,128)S(1)} %get-tuple-element.78.gain_ref, f32[384,512]{1,0:T(8,128)S(1)} %get-tuple-element.128.part_ref, f32[384,512]{1,0:T(8,128)S(1)} %get-tuple-element.129.reach_ref, ...), custom_call_target="tpu_custom_call" | custom-call | flops 1024 | bytes 1024 | tf_op jit(solution)/shard_map/finish/pallas_call | solution.py:493
  66.5 4.5 %collective-permute-done.17.refs_2_ = bf16[256,512]{1,0:T(8,128)(2,1)S(1)} collective-permute-done((bf16[256,512]{1,0:T(8,128)(2,1)S(1)}, bf16[256,512]{1,0:T(8,128)(2,1)S(1)}, u32[]{:S(2)}, u32[]{:S(2)}) %collective-permute-start.17) | collective-permute-done | bytes 262176 | tf_op jit(solution)/shard_map/ppermute | solution.py:534
  71.0 1.7 %finish.3 = bf16[384,4096]{1,0:T(8,128)(2,1)} custom-call(s32[1]{0:T(128)} %bitcast.place_ref, bf16[2,384,384]{2,1,0:T(8,128)(2,1)S(1)} %get-tuple-element.77.left_ref, f32[1,4096]{1,0:T(1,128)S(1)} %get-tuple-element.78.gain_ref, f32[384,512]{1,0:T(8,128)S(1)} %get-tuple-element.112.part_ref, ...), custom_call_target="tpu_custom_call", output_to_operand_aliasing={{}: (15, {})} | custom-call | flops 1024 | bytes 1024 | tf_op jit(solution)/shard_map/finish/pallas_call | solution.py:493
  (48 shorter events, 9.5 us)
Async XLA Ops:
  2.2 5.9 %collective-permute-start = (bf16[3,5120]{1,0:T(4,128)(2,1)S(1)}, bf16[3,5120]{1,0:T(4,128)(2,1)S(1)}, u32[]{:S(2)}, u32[]{:S(2)}) collective-permute-start(bf16[3,5120]{1,0:T(4,128)(2,1)S(1)} %pad_maximum_fusion), channel_id=1, source_target_pairs={{0,4},{4,8},{8,12},{1,5},{5,9},{9,13},{2,6},{6,10},{10,14},{3,7},{... | collective-permute-start | bytes 92168 | tf_op jit(solution)/shard_map/ppermute | solution.py:399
  3.5 10.8 %collective-permute-start.1 = (bf16[256,512]{1,0:T(8,128)(2,1)S(1)}, bf16[256,512]{1,0:T(8,128)(2,1)S(1)}, u32[]{:S(2)}, u32[]{:S(2)}) collective-permute-start(bf16[256,512]{1,0:T(8,128)(2,1)S(1)} %first.8.gate_ref), channel_id=1, source_target_pairs={{0,4},{1,5},{2,6},{3,7},{16,20},{17,21},{18,22},{19,23}} | collective-permute-start | bytes 786440 | tf_op jit(solution)/shard_map/ppermute | solution.py:366
  10.1 7.3 %collective-permute-start.2 = (bf16[256,512]{1,0:T(8,128)(2,1)S(1)}, bf16[256,512]{1,0:T(8,128)(2,1)S(1)}, u32[]{:S(2)}, u32[]{:S(2)}) collective-permute-start(bf16[256,512]{1,0:T(8,128)(2,1)S(1)} %first.9.gate_ref), channel_id=1, source_target_pairs={{0,4},{1,5},{2,6},{3,7},{16,20},{17,21},{18,22},{19,23}} | collective-permute-start | bytes 786440 | tf_op jit(solution)/shard_map/ppermute | solution.py:366
  13.7 6.2 %collective-permute-start.3 = (bf16[256,512]{1,0:T(8,128)(2,1)S(1)}, bf16[256,512]{1,0:T(8,128)(2,1)S(1)}, u32[]{:S(2)}, u32[]{:S(2)}) collective-permute-start(bf16[256,512]{1,0:T(8,128)(2,1)S(1)} %first.10.refs_3_), channel_id=1, source_target_pairs={{0,4},{1,5},{2,6},{3,7},{16,20},{17,21},{18,22},{19,23}} | collective-permute-start | bytes 786440 | tf_op jit(solution)/shard_map/ppermute | solution.py:366
  14.4 5.4 %collective-permute-start.4 = (bf16[256,512]{1,0:T(8,128)(2,1)S(1)}, bf16[256,512]{1,0:T(8,128)(2,1)S(1)}, u32[]{:S(2)}, u32[]{:S(2)}) collective-permute-start(bf16[256,512]{1,0:T(8,128)(2,1)S(1)} %combine.10.gate_ref), channel_id=1, source_target_pairs={{4,8},{5,9},{6,10},{7,11},{20,24},{21,25},{22,26},{23,27}} | collective-permute-start | bytes 786440 | tf_op jit(solution)/shard_map/ppermute | solution.py:534
  15.2 8.3 %collective-permute-start.5 = (bf16[256,512]{1,0:T(8,128)(2,1)S(1)}, bf16[256,512]{1,0:T(8,128)(2,1)S(1)}, u32[]{:S(2)}, u32[]{:S(2)}) collective-permute-start(bf16[256,512]{1,0:T(8,128)(2,1)S(1)} %first.11.gate_ref), channel_id=1, source_target_pairs={{0,4},{1,5},{2,6},{3,7},{16,20},{17,21},{18,22},{19,23}} | collective-permute-start | bytes 786440 | tf_op jit(solution)/shard_map/ppermute | solution.py:366
  17.4 6.0 %collective-permute-start.6 = (bf16[256,512]{1,0:T(8,128)(2,1)S(1)}, bf16[256,512]{1,0:T(8,128)(2,1)S(1)}, u32[]{:S(2)}, u32[]{:S(2)}) collective-permute-start(bf16[256,512]{1,0:T(8,128)(2,1)S(1)} %combine.11.gate_ref), channel_id=1, source_target_pairs={{4,8},{5,9},{6,10},{7,11},{20,24},{21,25},{22,26},{23,27}} | collective-permute-start | bytes 786440 | tf_op jit(solution)/shard_map/ppermute | solution.py:534
  20.0 10.5 %collective-permute-start.8 = (bf16[256,512]{1,0:T(8,128)(2,1)S(1)}, bf16[256,512]{1,0:T(8,128)(2,1)S(1)}, u32[]{:S(2)}, u32[]{:S(2)}) collective-permute-start(bf16[256,512]{1,0:T(8,128)(2,1)S(1)} %combine.12.gate_ref), channel_id=1, source_target_pairs={{4,8},{8,12},{5,9},{9,13},{6,10},{10,14},{7,11},{11,15},{20,24},{2... | collective-permute-start | bytes 786440 | tf_op jit(solution)/shard_map/ppermute | solution.py:534
  21.3 9.6 %collective-permute-start.7 = (bf16[256,512]{1,0:T(8,128)(2,1)S(1)}, bf16[256,512]{1,0:T(8,128)(2,1)S(1)}, u32[]{:S(2)}, u32[]{:S(2)}) collective-permute-start(bf16[256,512]{1,0:T(8,128)(2,1)S(1)} %first.12.gate_ref), channel_id=1, source_target_pairs={{0,4},{1,5},{2,6},{3,7},{16,20},{17,21},{18,22},{19,23}} | collective-permute-start | bytes 786440 | tf_op jit(solution)/shard_map/ppermute | solution.py:366
  23.6 12.4 %collective-permute-start.10 = (bf16[256,512]{1,0:T(8,128)(2,1)S(1)}, bf16[256,512]{1,0:T(8,128)(2,1)S(1)}, u32[]{:S(2)}, u32[]{:S(2)}) collective-permute-start(bf16[256,512]{1,0:T(8,128)(2,1)S(1)} %combine.13.gate_ref), channel_id=1, source_target_pairs={{4,8},{8,12},{5,9},{9,13},{6,10},{10,14},{7,11},{11,15},{20,24},{2... | collective-permute-start | bytes 786440 | tf_op jit(solution)/shard_map/ppermute | solution.py:534
  24.9 11.4 %collective-permute-start.9 = (bf16[256,512]{1,0:T(8,128)(2,1)S(1)}, bf16[256,512]{1,0:T(8,128)(2,1)S(1)}, u32[]{:S(2)}, u32[]{:S(2)}) collective-permute-start(bf16[256,512]{1,0:T(8,128)(2,1)S(1)} %first.13.gate_ref), channel_id=1, source_target_pairs={{0,4},{1,5},{2,6},{3,7},{16,20},{17,21},{18,22},{19,23}} | collective-permute-start | bytes 786440 | tf_op jit(solution)/shard_map/ppermute | solution.py:366
  31.0 11.0 %collective-permute-start.12 = (bf16[256,512]{1,0:T(8,128)(2,1)S(1)}, bf16[256,512]{1,0:T(8,128)(2,1)S(1)}, u32[]{:S(2)}, u32[]{:S(2)}) collective-permute-start(bf16[256,512]{1,0:T(8,128)(2,1)S(1)} %combine.14.gate_ref), channel_id=1, source_target_pairs={{4,8},{8,12},{5,9},{9,13},{6,10},{10,14},{7,11},{11,15},{20,24},{2... | collective-permute-start | bytes 786440 | tf_op jit(solution)/shard_map/ppermute | solution.py:534
  32.3 10.0 %collective-permute-start.11 = (bf16[256,512]{1,0:T(8,128)(2,1)S(1)}, bf16[256,512]{1,0:T(8,128)(2,1)S(1)}, u32[]{:S(2)}, u32[]{:S(2)}) collective-permute-start(bf16[256,512]{1,0:T(8,128)(2,1)S(1)} %first.14.gate_ref), channel_id=1, source_target_pairs={{0,4},{1,5},{2,6},{3,7},{16,20},{17,21},{18,22},{19,23}} | collective-permute-start | bytes 786440 | tf_op jit(solution)/shard_map/ppermute | solution.py:366
  33.0 12.3 %collective-permute-start.13 = (bf16[256,512]{1,0:T(8,128)(2,1)S(1)}, bf16[256,512]{1,0:T(8,128)(2,1)S(1)}, u32[]{:S(2)}, u32[]{:S(2)}) collective-permute-start(bf16[256,512]{1,0:T(8,128)(2,1)S(1)} %first.15.gate_ref), channel_id=1, source_target_pairs={{0,4},{1,5},{2,6},{3,7},{16,20},{17,21},{18,22},{19,23}} | collective-permute-start | bytes 786440 | tf_op jit(solution)/shard_map/ppermute | solution.py:366
  36.5 12.6 %collective-permute-start.14 = (bf16[256,512]{1,0:T(8,128)(2,1)S(1)}, bf16[256,512]{1,0:T(8,128)(2,1)S(1)}, u32[]{:S(2)}, u32[]{:S(2)}) collective-permute-start(bf16[256,512]{1,0:T(8,128)(2,1)S(1)} %combine.15.gate_ref), channel_id=1, source_target_pairs={{4,8},{8,12},{5,9},{9,13},{6,10},{10,14},{7,11},{11,15},{20,24},{2... | collective-permute-start | bytes 786440 | tf_op jit(solution)/shard_map/ppermute | solution.py:534
  42.5 13.2 %collective-permute-start.16 = (bf16[256,512]{1,0:T(8,128)(2,1)S(1)}, bf16[256,512]{1,0:T(8,128)(2,1)S(1)}, u32[]{:S(2)}, u32[]{:S(2)}) collective-permute-start(bf16[256,512]{1,0:T(8,128)(2,1)S(1)} %combine.16.gate_ref), channel_id=1, source_target_pairs={{4,8},{8,12},{5,9},{9,13},{6,10},{10,14},{7,11},{11,15},{20,24},{2... | collective-permute-start | bytes 786440 | tf_op jit(solution)/shard_map/ppermute | solution.py:534
  49.2 12.9 %collective-permute-start.15 = (bf16[256,512]{1,0:T(8,128)(2,1)S(1)}, bf16[256,512]{1,0:T(8,128)(2,1)S(1)}, u32[]{:S(2)}, u32[]{:S(2)}) collective-permute-start(bf16[256,512]{1,0:T(8,128)(2,1)S(1)} %combine.17.refs_3_), channel_id=1, source_target_pairs={{4,8},{8,12},{5,9},{9,13},{6,10},{10,14},{7,11},{11,15},{20,24},{2... | collective-permute-start | bytes 786440 | tf_op jit(solution)/shard_map/ppermute | solution.py:534
  56.1 10.0 %collective-permute-start.18 = (bf16[256,512]{1,0:T(8,128)(2,1)S(1)}, bf16[256,512]{1,0:T(8,128)(2,1)S(1)}, u32[]{:S(2)}, u32[]{:S(2)}) collective-permute-start(bf16[256,512]{1,0:T(8,128)(2,1)S(1)} %combine.18.refs_3_), channel_id=1, source_target_pairs={{8,12},{9,13},{10,14},{11,15},{24,28},{25,29},{26,30},{27,31}} | collective-permute-start | bytes 786440 | tf_op jit(solution)/shard_map/ppermute | solution.py:534
  62.6 8.4 %collective-permute-start.17 = (bf16[256,512]{1,0:T(8,128)(2,1)S(1)}, bf16[256,512]{1,0:T(8,128)(2,1)S(1)}, u32[]{:S(2)}, u32[]{:S(2)}) collective-permute-start(bf16[256,512]{1,0:T(8,128)(2,1)S(1)} %combine.19.refs_3_), channel_id=1, source_target_pairs={{8,12},{9,13},{10,14},{11,15},{24,28},{25,29},{26,30},{27,31}} | collective-permute-start | bytes 786440 | tf_op jit(solution)/shard_map/ppermute | solution.py:534

commit v5 on v4

--- a/solution.py
+++ b/solution.py
@@ -533,11 +533,11 @@
             from_later.append(
                 lax.ppermute(gate, "ctx", [(owner, owner + 1) for owner in senders])
             )
+        if step + 1 < count:
+            gate = work(step + 1)
         if step + 3 < count:
             gate = first(step + 3, gate, [])
             send(gate)
-        if step + 1 < count:
-            gate = work(step + 1)
         chunk = step - 1 - 2 * max(hops - 2, 0)
         if 0 <= chunk < count:
             owners = [0] + list(range(2, contexts))

time: 73.4 us -> 73.1 us (level)
  no operation moved by 1% of the time
where the time goes in v5:
time: 73.1 us; the launch traced here: 72.6 us
  waiting for transfers between devices  29 us (40%)
  Pallas kernels  24 us (33%)
  starting transfers between devices  18.8 us (26%)
    ppermute x10, waiting for transfers between devices, shards(): lax.ppermute(gate, 'ctx', [(owner, owner + 1) for owner in senders])  25 us
    pallas_call x8, Pallas kernels, local(): pl.pallas_call(functools.partial(local_kernel, group, chunk, which), in_s...  12 us
    ppermute x10, starting transfers between devices, shards(): lax.ppermute(gate, 'ctx', [(owner, owner + 1) for owner in senders])  11.9 us
    ppermute x8, starting transfers between devices, send(): from_first.append(lax.ppermute(value, 'ctx', [(0, 1)]))  5.64 us
    ppermute x1, waiting for transfers between devices, shards(): early = lax.ppermute(early, 'ctx', ahead)  3.91 us
    pallas_call x2, Pallas kernels, finish(): pl.pallas_call(functools.partial(finish_kernel, chunk // in_group, in_gro...  3.45 us
    pallas_call x6, Pallas kernels, absorb(): pl.pallas_call(functools.partial(absorb_kernel, chunk // in_group, chunk,...  2.19 us
    pallas_call x1, Pallas kernels, shards(): pl.pallas_call(steps_kernel, in_specs=[pl.BlockSpec(memory_space=pltpu.HB...  2 us
  transfers between devices with their start and end apart: 19, of which 9 were waited for; matrix products, arithmetic and copies ran while one was open for 0% of the time, Pallas kernels for 28%

profile of v5, /device:TPU:28, one launch (start us, length us, event | category | flops | bytes accessed | tf_op | source)
XLA Modules:
  0.0 72.6 jit_solution(3901079346613014539)
XLA Ops:
  0.0 2.0 %steps.1 = (bf16[384,1024]{1,0:T(8,128)(2,1)S(1)}, bf16[8,4096]{1,0:T(8,128)(2,1)S(1)}, f32[4,4096]{1,0:T(4,128)S(1)}, f32[4,2,512]{2,1,0:T(2,128)S(1)}, bf16[38...) custom-call(bf16[384,4096]{1,0:T(8,128)(2,1)} %refs_0_.7, ...), custom_call_target="tpu_custom_call" | custom-call | flops 1024 | bytes 1024 | tf_op jit(solution)/shard_map/steps/pallas_call | solution.py:331
  2.2 1.3 %collective-permute-start = (bf16[3,5120]{1,0:T(4,128)(2,1)S(1)}, bf16[3,5120]{1,0:T(4,128)(2,1)S(1)}, u32[]{:S(2)}, u32[]{:S(2)}) collective-permute-start(bf16[3,5120]{1,0:T(4,128)(2,1)S(1)} %pad_maximum_fusion), channel_id=1, source_target_pairs={{0,4},{4,8},{8,12},{1,5},{5,9},{9,13},{2,6},{6,10},{10,14},{3,7},{... | collective-permute-start | bytes 92168 | tf_op jit(solution)/shard_map/ppermute | solution.py:399
  4.2 3.9 %collective-permute-done.early_ref = bf16[3,5120]{1,0:T(4,128)(2,1)S(1)} collective-permute-done((bf16[3,5120]{1,0:T(4,128)(2,1)S(1)}, bf16[3,5120]{1,0:T(4,128)(2,1)S(1)}, u32[]{:S(2)}, u32[]{:S(2)}) %collective-permute-start) | collective-permute-done | bytes 30752 | tf_op jit(solution)/shard_map/ppermute | solution.py:399
  8.1 1.9 %groups.1 = (bf16[2,384,384]{2,1,0:T(8,128)(2,1)S(1)}, bf16[2,256,384]{2,1,0:T(8,128)(2,1)S(1)}, bf16[384,1024]{1,0:T(8,128)(2,1)S(1)}) custom-call(bf16[384,1024]{1,0:T(8,128)(2,1)S(1)} %bitcast.12, bf16[3,5120]{1,0:T(4,128)(2,1)S(1)} %collective-permute-done.early_ref, f32[4,2,512]{2,1,0:T(2,128)S(1)} %get-tuple-element.75.bc_taps_ref.taps_ref, ...), custom_call_target="tpu_custom_call" | custom-call | flops 1024 | bytes 1024 | tf_op jit(solution)/shard_map/groups/pallas_call | solution.py:416
  10.7 1.4 %stage.1 = (bf16[384,1024]{1,0:T(8,128)(2,1)S(1)}, bf16[384,1024]{1,0:T(8,128)(2,1)S(1)}) custom-call(bf16[256,512]{1,0:T(8,128)(2,1)S(1)} %first.8.gate_ref, bf16[384,4096]{1,0:T(8,128)(2,1)} %refs_1_.5, bf16[384,4096]{1,0:T(8,128)(2,1)} %refs_0_.7), custom_call_target="tpu_custom_call" | custom-call | flops 1024 | bytes 1024 | tf_op jit(solution)/shard_map/stage/pallas_call | solution.py:403
  12.1 1.5 %local.8 = (f32[384,512]{1,0:T(8,128)S(1)}, f32[384,512]{1,0:T(8,128)S(1)}, f32[256,512]{1,0:T(8,128)S(1)}, f32[8,512]{1,0:T(8,128)S(1)}, bf16[384,1024]{1,0:T(8,128)(2,1)S(1)}, /*index=5*/bf16[384,1024]{1,0:T(8,128)(2,1)S(1)}) custom-call(bf16[384,1024]{1,0:T(8,128)(2,1)S(1)} %get-tuple-element.71.x_ref, ...), custom_call_target="tpu_custom_call" | custom-call | flops 1024 | bytes 1024 | tf_op jit(solution)/shard_map/local/pallas_call | solution.py:434
  15.1 1.5 %local.9 = (f32[384,512]{1,0:T(8,128)S(1)}, f32[384,512]{1,0:T(8,128)S(1)}, f32[256,512]{1,0:T(8,128)S(1)}, f32[8,512]{1,0:T(8,128)S(1)}, bf16[384,1024]{1,0:T(8,128)(2,1)S(1)}, /*index=5*/bf16[384,1024]{1,0:T(8,128)(2,1)S(1)}) custom-call(bf16[384,1024]{1,0:T(8,128)(2,1)S(1)} %get-tuple-element.71.x_ref, ...), custom_call_target="tpu_custom_call" | custom-call | flops 1024 | bytes 1024 | tf_op jit(solution)/shard_map/local/pallas_call | solution.py:434
  17.4 0.9 %collective-permute-start.6 = (bf16[256,512]{1,0:T(8,128)(2,1)S(1)}, bf16[256,512]{1,0:T(8,128)(2,1)S(1)}, u32[]{:S(2)}, u32[]{:S(2)}) collective-permute-start(bf16[256,512]{1,0:T(8,128)(2,1)S(1)} %combine.11.gate_ref), channel_id=1, source_target_pairs={{4,8},{5,9},{6,10},{7,11},{20,24},{21,25},{22,26},{23,27}} | collective-permute-start | bytes 786440 | tf_op jit(solution)/shard_map/ppermute | solution.py:534
  18.3 1.5 %local.10 = (f32[384,512]{1,0:T(8,128)S(1)}, f32[384,512]{1,0:T(8,128)S(1)}, f32[256,512]{1,0:T(8,128)S(1)}, f32[8,512]{1,0:T(8,128)S(1)}) custom-call(bf16[384,1024]{1,0:T(8,128)(2,1)S(1)} %get-tuple-element.85.x_ref, bf16[3,5120]{1,0:T(4,128)(2,1)S(1)} %collective-permute-done.early_ref, f32[4,4096]{1,0:T(4,128)S(1)} %get-tuple-element.72.taps_ref, ...), custom_call_target="tpu_custom_call" | custom-call | flops 1024 | bytes 1024 | tf_op jit(solution)/shard_map/local/pallas_call | solution.py:434
  20.0 1.3 %collective-permute-start.8 = (bf16[256,512]{1,0:T(8,128)(2,1)S(1)}, bf16[256,512]{1,0:T(8,128)(2,1)S(1)}, u32[]{:S(2)}, u32[]{:S(2)}) collective-permute-start(bf16[256,512]{1,0:T(8,128)(2,1)S(1)} %combine.12.gate_ref), channel_id=1, source_target_pairs={{4,8},{8,12},{5,9},{9,13},{6,10},{10,14},{7,11},{11,15},{20,24},{2... | collective-permute-start | bytes 786440 | tf_op jit(solution)/shard_map/ppermute | solution.py:534
  22.0 1.5 %local.11 = (f32[384,512]{1,0:T(8,128)S(1)}, f32[384,512]{1,0:T(8,128)S(1)}, f32[256,512]{1,0:T(8,128)S(1)}, f32[8,512]{1,0:T(8,128)S(1)}) custom-call(bf16[384,1024]{1,0:T(8,128)(2,1)S(1)} %get-tuple-element.85.x_ref, bf16[3,5120]{1,0:T(4,128)(2,1)S(1)} %collective-permute-done.early_ref, f32[4,4096]{1,0:T(4,128)S(1)} %get-tuple-element.72.taps_ref, ...), custom_call_target="tpu_custom_call" | custom-call | flops 1024 | bytes 1024 | tf_op jit(solution)/shard_map/local/pallas_call | solution.py:434
  23.6 1.3 %collective-permute-start.10 = (bf16[256,512]{1,0:T(8,128)(2,1)S(1)}, bf16[256,512]{1,0:T(8,128)(2,1)S(1)}, u32[]{:S(2)}, u32[]{:S(2)}) collective-permute-start(bf16[256,512]{1,0:T(8,128)(2,1)S(1)} %combine.13.gate_ref), channel_id=1, source_target_pairs={{4,8},{8,12},{5,9},{9,13},{6,10},{10,14},{7,11},{11,15},{20,24},{2... | collective-permute-start | bytes 786440 | tf_op jit(solution)/shard_map/ppermute | solution.py:534
  25.6 1.5 %local.12 = (f32[384,512]{1,0:T(8,128)S(1)}, f32[384,512]{1,0:T(8,128)S(1)}, f32[256,512]{1,0:T(8,128)S(1)}, f32[8,512]{1,0:T(8,128)S(1)}) custom-call(bf16[384,1024]{1,0:T(8,128)(2,1)S(1)} %get-tuple-element.88.x_ref, bf16[3,5120]{1,0:T(4,128)(2,1)S(1)} %collective-permute-done.early_ref, f32[4,4096]{1,0:T(4,128)S(1)} %get-tuple-element.72.taps_ref, ...), custom_call_target="tpu_custom_call" | custom-call | flops 1024 | bytes 1024 | tf_op jit(solution)/shard_map/local/pallas_call | solution.py:434
  27.8 2.6 %collective-permute-done.8.refs_2_.refs_5_.refs_1_ = bf16[256,512]{1,0:T(8,128)(2,1)S(1)} collective-permute-done((bf16[256,512]{1,0:T(8,128)(2,1)S(1)}, bf16[256,512]{1,0:T(8,128)(2,1)S(1)}, u32[]{:S(2)}, u32[]{:S(2)}) %collective-permute-start.8) | collective-permute-done | bytes 262176 | tf_op jit(solution)/shard_map/ppermute | solution.py:534
  31.0 1.3 %collective-permute-start.12 = (bf16[256,512]{1,0:T(8,128)(2,1)S(1)}, bf16[256,512]{1,0:T(8,128)(2,1)S(1)}, u32[]{:S(2)}, u32[]{:S(2)}) collective-permute-start(bf16[256,512]{1,0:T(8,128)(2,1)S(1)} %combine.14.gate_ref), channel_id=1, source_target_pairs={{4,8},{8,12},{5,9},{9,13},{6,10},{10,14},{7,11},{11,15},{20,24},{2... | collective-permute-start | bytes 786440 | tf_op jit(solution)/shard_map/ppermute | solution.py:534
  32.3 1.5 %local.13 = (f32[384,512]{1,0:T(8,128)S(1)}, f32[384,512]{1,0:T(8,128)S(1)}, f32[256,512]{1,0:T(8,128)S(1)}, f32[8,512]{1,0:T(8,128)S(1)}) custom-call(bf16[384,1024]{1,0:T(8,128)(2,1)S(1)} %get-tuple-element.88.x_ref, bf16[3,5120]{1,0:T(4,128)(2,1)S(1)} %collective-permute-done.early_ref, f32[4,4096]{1,0:T(4,128)S(1)} %get-tuple-element.72.taps_ref, ...), custom_call_target="tpu_custom_call" | custom-call | flops 1024 | bytes 1024 | tf_op jit(solution)/shard_map/local/pallas_call | solution.py:434
  33.8 0.9 %collective-permute-start.13 = (bf16[256,512]{1,0:T(8,128)(2,1)S(1)}, bf16[256,512]{1,0:T(8,128)(2,1)S(1)}, u32[]{:S(2)}, u32[]{:S(2)}) collective-permute-start(bf16[256,512]{1,0:T(8,128)(2,1)S(1)} %first.15.refs_3_), channel_id=1, source_target_pairs={{0,4},{1,5},{2,6},{3,7},{16,20},{17,21},{18,22},{19,23}} | collective-permute-start | bytes 786440 | tf_op jit(solution)/shard_map/ppermute | solution.py:366
  34.7 1.3 %collective-permute-done.10.refs_2_.refs_5_.refs_1_ = bf16[256,512]{1,0:T(8,128)(2,1)S(1)} collective-permute-done((bf16[256,512]{1,0:T(8,128)(2,1)S(1)}, bf16[256,512]{1,0:T(8,128)(2,1)S(1)}, u32[]{:S(2)}, u32[]{:S(2)}) %collective-permute-start.10) | collective-permute-done | bytes 262176 | tf_op jit(solution)/shard_map/ppermute | solution.py:534
  36.5 1.3 %collective-permute-start.14 = (bf16[256,512]{1,0:T(8,128)(2,1)S(1)}, bf16[256,512]{1,0:T(8,128)(2,1)S(1)}, u32[]{:S(2)}, u32[]{:S(2)}) collective-permute-start(bf16[256,512]{1,0:T(8,128)(2,1)S(1)} %combine.15.gate_ref), channel_id=1, source_target_pairs={{4,8},{8,12},{5,9},{9,13},{6,10},{10,14},{7,11},{11,15},{20,24},{2... | collective-permute-start | bytes 786440 | tf_op jit(solution)/shard_map/ppermute | solution.py:534
  37.8 1.5 %local.14 = (f32[384,512]{1,0:T(8,128)S(1)}, f32[384,512]{1,0:T(8,128)S(1)}, f32[256,512]{1,0:T(8,128)S(1)}, f32[8,512]{1,0:T(8,128)S(1)}) custom-call(bf16[384,1024]{1,0:T(8,128)(2,1)S(1)} %get-tuple-element.86.x_ref, bf16[3,5120]{1,0:T(4,128)(2,1)S(1)} %collective-permute-done.early_ref, f32[4,4096]{1,0:T(4,128)S(1)} %get-tuple-element.72.taps_ref, ...), custom_call_target="tpu_custom_call" | custom-call | flops 1024 | bytes 1024 | tf_op jit(solution)/shard_map/local/pallas_call | solution.py:434
  39.3 2.6 %collective-permute-done.12.refs_2_.refs_5_.refs_1_ = bf16[256,512]{1,0:T(8,128)(2,1)S(1)} collective-permute-done((bf16[256,512]{1,0:T(8,128)(2,1)S(1)}, bf16[256,512]{1,0:T(8,128)(2,1)S(1)}, u32[]{:S(2)}, u32[]{:S(2)}) %collective-permute-start.12) | collective-permute-done | bytes 262176 | tf_op jit(solution)/shard_map/ppermute | solution.py:534
  42.5 1.3 %collective-permute-start.16 = (bf16[256,512]{1,0:T(8,128)(2,1)S(1)}, bf16[256,512]{1,0:T(8,128)(2,1)S(1)}, u32[]{:S(2)}, u32[]{:S(2)}) collective-permute-start(bf16[256,512]{1,0:T(8,128)(2,1)S(1)} %combine.16.gate_ref), channel_id=1, source_target_pairs={{4,8},{8,12},{5,9},{9,13},{6,10},{10,14},{7,11},{11,15},{20,24},{2... | collective-permute-start | bytes 786440 | tf_op jit(solution)/shard_map/ppermute | solution.py:534
  43.8 1.5 %local.15 = (f32[384,512]{1,0:T(8,128)S(1)}, f32[384,512]{1,0:T(8,128)S(1)}, f32[256,512]{1,0:T(8,128)S(1)}, f32[8,512]{1,0:T(8,128)S(1)}) custom-call(bf16[384,1024]{1,0:T(8,128)(2,1)S(1)} %get-tuple-element.86.x_ref, bf16[3,5120]{1,0:T(4,128)(2,1)S(1)} %collective-permute-done.early_ref, f32[4,4096]{1,0:T(4,128)S(1)} %get-tuple-element.72.taps_ref, ...), custom_call_target="tpu_custom_call" | custom-call | flops 1024 | bytes 1024 | tf_op jit(solution)/shard_map/local/pallas_call | solution.py:434
  45.3 2.8 %collective-permute-done.14.refs_5_.refs_1_.refs_2_ = bf16[256,512]{1,0:T(8,128)(2,1)S(1)} collective-permute-done((bf16[256,512]{1,0:T(8,128)(2,1)S(1)}, bf16[256,512]{1,0:T(8,128)(2,1)S(1)}, u32[]{:S(2)}, u32[]{:S(2)}) %collective-permute-start.14) | collective-permute-done | bytes 262176 | tf_op jit(solution)/shard_map/ppermute | solution.py:534
  48.2 1.3 %collective-permute-start.15 = (bf16[256,512]{1,0:T(8,128)(2,1)S(1)}, bf16[256,512]{1,0:T(8,128)(2,1)S(1)}, u32[]{:S(2)}, u32[]{:S(2)}) collective-permute-start(bf16[256,512]{1,0:T(8,128)(2,1)S(1)} %combine.17.refs_3_), channel_id=1, source_target_pairs={{4,8},{8,12},{5,9},{9,13},{6,10},{10,14},{7,11},{11,15},{20,24},{2... | collective-permute-start | bytes 786440 | tf_op jit(solution)/shard_map/ppermute | solution.py:534
  49.5 6.1 %collective-permute-done.16.refs_2_.refs_1_ = bf16[256,512]{1,0:T(8,128)(2,1)S(1)} collective-permute-done((bf16[256,512]{1,0:T(8,128)(2,1)S(1)}, bf16[256,512]{1,0:T(8,128)(2,1)S(1)}, u32[]{:S(2)}, u32[]{:S(2)}) %collective-permute-start.16) | collective-permute-done | bytes 262176 | tf_op jit(solution)/shard_map/ppermute | solution.py:534
  56.0 1.3 %collective-permute-start.18 = (bf16[256,512]{1,0:T(8,128)(2,1)S(1)}, bf16[256,512]{1,0:T(8,128)(2,1)S(1)}, u32[]{:S(2)}, u32[]{:S(2)}) collective-permute-start(bf16[256,512]{1,0:T(8,128)(2,1)S(1)} %combine.18.refs_3_), channel_id=1, source_target_pairs={{8,12},{9,13},{10,14},{11,15},{24,28},{25,29},{26,30},{27,31}} | collective-permute-start | bytes 786440 | tf_op jit(solution)/shard_map/ppermute | solution.py:534
  57.3 4.6 %collective-permute-done.15.refs_2_.refs_1_ = bf16[256,512]{1,0:T(8,128)(2,1)S(1)} collective-permute-done((bf16[256,512]{1,0:T(8,128)(2,1)S(1)}, bf16[256,512]{1,0:T(8,128)(2,1)S(1)}, u32[]{:S(2)}, u32[]{:S(2)}) %collective-permute-start.15) | collective-permute-done | bytes 262176 | tf_op jit(solution)/shard_map/ppermute | solution.py:534
  62.4 1.3 %collective-permute-start.17 = (bf16[256,512]{1,0:T(8,128)(2,1)S(1)}, bf16[256,512]{1,0:T(8,128)(2,1)S(1)}, u32[]{:S(2)}, u32[]{:S(2)}) collective-permute-start(bf16[256,512]{1,0:T(8,128)(2,1)S(1)} %combine.19.refs_3_), channel_id=1, source_target_pairs={{8,12},{9,13},{10,14},{11,15},{24,28},{25,29},{26,30},{27,31}} | collective-permute-start | bytes 786440 | tf_op jit(solution)/shard_map/ppermute | solution.py:534
  63.7 1.7 %finish.2.refs_10_ = bf16[384,4096]{1,0:T(8,128)(2,1)} custom-call(s32[1]{0:T(128)} %bitcast.place_ref, bf16[2,384,384]{2,1,0:T(8,128)(2,1)S(1)} %get-tuple-element.77.left_ref, f32[1,4096]{1,0:T(1,128)S(1)} %get-tuple-element.78.gain_ref, f32[384,512]{1,0:T(8,128)S(1)} %get-tuple-element.128.part_ref, f32[384,512]{1,0:T(8,128)S(1)} %get-tuple-element.129.reach_ref, ...), custom_call_target="tpu_custom_call" | custom-call | flops 1024 | bytes 1024 | tf_op jit(solution)/shard_map/finish/pallas_call | solution.py:493
  66.0 4.8 %collective-permute-done.17.refs_2_ = bf16[256,512]{1,0:T(8,128)(2,1)S(1)} collective-permute-done((bf16[256,512]{1,0:T(8,128)(2,1)S(1)}, bf16[256,512]{1,0:T(8,128)(2,1)S(1)}, u32[]{:S(2)}, u32[]{:S(2)}) %collective-permute-start.17) | collective-permute-done | bytes 262176 | tf_op jit(solution)/shard_map/ppermute | solution.py:534
  70.7 1.7 %finish.3 = bf16[384,4096]{1,0:T(8,128)(2,1)} custom-call(s32[1]{0:T(128)} %bitcast.place_ref, bf16[2,384,384]{2,1,0:T(8,128)(2,1)S(1)} %get-tuple-element.77.left_ref, f32[1,4096]{1,0:T(1,128)S(1)} %get-tuple-element.78.gain_ref, f32[384,512]{1,0:T(8,128)S(1)} %get-tuple-element.112.part_ref, ...), custom_call_target="tpu_custom_call", output_to_operand_aliasing={{}: (15, {})} | custom-call | flops 1024 | bytes 1024 | tf_op jit(solution)/shard_map/finish/pallas_call | solution.py:493
  (48 shorter events, 9.1 us)
Async XLA Ops:
  2.2 5.9 %collective-permute-start = (bf16[3,5120]{1,0:T(4,128)(2,1)S(1)}, bf16[3,5120]{1,0:T(4,128)(2,1)S(1)}, u32[]{:S(2)}, u32[]{:S(2)}) collective-permute-start(bf16[3,5120]{1,0:T(4,128)(2,1)S(1)} %pad_maximum_fusion), channel_id=1, source_target_pairs={{0,4},{4,8},{8,12},{1,5},{5,9},{9,13},{2,6},{6,10},{10,14},{3,7},{... | collective-permute-start | bytes 92168 | tf_op jit(solution)/shard_map/ppermute | solution.py:399
  3.5 10.8 %collective-permute-start.1 = (bf16[256,512]{1,0:T(8,128)(2,1)S(1)}, bf16[256,512]{1,0:T(8,128)(2,1)S(1)}, u32[]{:S(2)}, u32[]{:S(2)}) collective-permute-start(bf16[256,512]{1,0:T(8,128)(2,1)S(1)} %first.8.gate_ref), channel_id=1, source_target_pairs={{0,4},{1,5},{2,6},{3,7},{16,20},{17,21},{18,22},{19,23}} | collective-permute-start | bytes 786440 | tf_op jit(solution)/shard_map/ppermute | solution.py:366
  10.1 7.3 %collective-permute-start.2 = (bf16[256,512]{1,0:T(8,128)(2,1)S(1)}, bf16[256,512]{1,0:T(8,128)(2,1)S(1)}, u32[]{:S(2)}, u32[]{:S(2)}) collective-permute-start(bf16[256,512]{1,0:T(8,128)(2,1)S(1)} %first.9.gate_ref), channel_id=1, source_target_pairs={{0,4},{1,5},{2,6},{3,7},{16,20},{17,21},{18,22},{19,23}} | collective-permute-start | bytes 786440 | tf_op jit(solution)/shard_map/ppermute | solution.py:366
  13.7 6.2 %collective-permute-start.3 = (bf16[256,512]{1,0:T(8,128)(2,1)S(1)}, bf16[256,512]{1,0:T(8,128)(2,1)S(1)}, u32[]{:S(2)}, u32[]{:S(2)}) collective-permute-start(bf16[256,512]{1,0:T(8,128)(2,1)S(1)} %first.10.refs_3_), channel_id=1, source_target_pairs={{0,4},{1,5},{2,6},{3,7},{16,20},{17,21},{18,22},{19,23}} | collective-permute-start | bytes 786440 | tf_op jit(solution)/shard_map/ppermute | solution.py:366
  14.4 5.4 %collective-permute-start.4 = (bf16[256,512]{1,0:T(8,128)(2,1)S(1)}, bf16[256,512]{1,0:T(8,128)(2,1)S(1)}, u32[]{:S(2)}, u32[]{:S(2)}) collective-permute-start(bf16[256,512]{1,0:T(8,128)(2,1)S(1)} %combine.10.gate_ref), channel_id=1, source_target_pairs={{4,8},{5,9},{6,10},{7,11},{20,24},{21,25},{22,26},{23,27}} | collective-permute-start | bytes 786440 | tf_op jit(solution)/shard_map/ppermute | solution.py:534
  16.7 6.8 %collective-permute-start.5 = (bf16[256,512]{1,0:T(8,128)(2,1)S(1)}, bf16[256,512]{1,0:T(8,128)(2,1)S(1)}, u32[]{:S(2)}, u32[]{:S(2)}) collective-permute-start(bf16[256,512]{1,0:T(8,128)(2,1)S(1)} %first.11.refs_3_), channel_id=1, source_target_pairs={{0,4},{1,5},{2,6},{3,7},{16,20},{17,21},{18,22},{19,23}} | collective-permute-start | bytes 786440 | tf_op jit(solution)/shard_map/ppermute | solution.py:366
  17.4 6.0 %collective-permute-start.6 = (bf16[256,512]{1,0:T(8,128)(2,1)S(1)}, bf16[256,512]{1,0:T(8,128)(2,1)S(1)}, u32[]{:S(2)}, u32[]{:S(2)}) collective-permute-start(bf16[256,512]{1,0:T(8,128)(2,1)S(1)} %combine.11.gate_ref), channel_id=1, source_target_pairs={{4,8},{5,9},{6,10},{7,11},{20,24},{21,25},{22,26},{23,27}} | collective-permute-start | bytes 786440 | tf_op jit(solution)/shard_map/ppermute | solution.py:534
  20.0 10.5 %collective-permute-start.8 = (bf16[256,512]{1,0:T(8,128)(2,1)S(1)}, bf16[256,512]{1,0:T(8,128)(2,1)S(1)}, u32[]{:S(2)}, u32[]{:S(2)}) collective-permute-start(bf16[256,512]{1,0:T(8,128)(2,1)S(1)} %combine.12.gate_ref), channel_id=1, source_target_pairs={{4,8},{8,12},{5,9},{9,13},{6,10},{10,14},{7,11},{11,15},{20,24},{2... | collective-permute-start | bytes 786440 | tf_op jit(solution)/shard_map/ppermute | solution.py:534
  21.3 9.5 %collective-permute-start.7 = (bf16[256,512]{1,0:T(8,128)(2,1)S(1)}, bf16[256,512]{1,0:T(8,128)(2,1)S(1)}, u32[]{:S(2)}, u32[]{:S(2)}) collective-permute-start(bf16[256,512]{1,0:T(8,128)(2,1)S(1)} %first.12.refs_6_), channel_id=1, source_target_pairs={{0,4},{1,5},{2,6},{3,7},{16,20},{17,21},{18,22},{19,23}} | collective-permute-start | bytes 786440 | tf_op jit(solution)/shard_map/ppermute | solution.py:366
  23.6 12.4 %collective-permute-start.10 = (bf16[256,512]{1,0:T(8,128)(2,1)S(1)}, bf16[256,512]{1,0:T(8,128)(2,1)S(1)}, u32[]{:S(2)}, u32[]{:S(2)}) collective-permute-start(bf16[256,512]{1,0:T(8,128)(2,1)S(1)} %combine.13.gate_ref), channel_id=1, source_target_pairs={{4,8},{8,12},{5,9},{9,13},{6,10},{10,14},{7,11},{11,15},{20,24},{2... | collective-permute-start | bytes 786440 | tf_op jit(solution)/shard_map/ppermute | solution.py:534
  24.9 11.4 %collective-permute-start.9 = (bf16[256,512]{1,0:T(8,128)(2,1)S(1)}, bf16[256,512]{1,0:T(8,128)(2,1)S(1)}, u32[]{:S(2)}, u32[]{:S(2)}) collective-permute-start(bf16[256,512]{1,0:T(8,128)(2,1)S(1)} %first.13.refs_6_), channel_id=1, source_target_pairs={{0,4},{1,5},{2,6},{3,7},{16,20},{17,21},{18,22},{19,23}} | collective-permute-start | bytes 786440 | tf_op jit(solution)/shard_map/ppermute | solution.py:366
  27.1 15.2 %collective-permute-start.11 = (bf16[256,512]{1,0:T(8,128)(2,1)S(1)}, bf16[256,512]{1,0:T(8,128)(2,1)S(1)}, u32[]{:S(2)}, u32[]{:S(2)}) collective-permute-start(bf16[256,512]{1,0:T(8,128)(2,1)S(1)} %first.14.refs_3_), channel_id=1, source_target_pairs={{0,4},{1,5},{2,6},{3,7},{16,20},{17,21},{18,22},{19,23}} | collective-permute-start | bytes 786440 | tf_op jit(solution)/shard_map/ppermute | solution.py:366
  31.0 11.0 %collective-permute-start.12 = (bf16[256,512]{1,0:T(8,128)(2,1)S(1)}, bf16[256,512]{1,0:T(8,128)(2,1)S(1)}, u32[]{:S(2)}, u32[]{:S(2)}) collective-permute-start(bf16[256,512]{1,0:T(8,128)(2,1)S(1)} %combine.14.gate_ref), channel_id=1, source_target_pairs={{4,8},{8,12},{5,9},{9,13},{6,10},{10,14},{7,11},{11,15},{20,24},{2... | collective-permute-start | bytes 786440 | tf_op jit(solution)/shard_map/ppermute | solution.py:534
  33.8 11.5 %collective-permute-start.13 = (bf16[256,512]{1,0:T(8,128)(2,1)S(1)}, bf16[256,512]{1,0:T(8,128)(2,1)S(1)}, u32[]{:S(2)}, u32[]{:S(2)}) collective-permute-start(bf16[256,512]{1,0:T(8,128)(2,1)S(1)} %first.15.refs_3_), channel_id=1, source_target_pairs={{0,4},{1,5},{2,6},{3,7},{16,20},{17,21},{18,22},{19,23}} | collective-permute-start | bytes 786440 | tf_op jit(solution)/shard_map/ppermute | solution.py:366
  36.5 11.6 %collective-permute-start.14 = (bf16[256,512]{1,0:T(8,128)(2,1)S(1)}, bf16[256,512]{1,0:T(8,128)(2,1)S(1)}, u32[]{:S(2)}, u32[]{:S(2)}) collective-permute-start(bf16[256,512]{1,0:T(8,128)(2,1)S(1)} %combine.15.gate_ref), channel_id=1, source_target_pairs={{4,8},{8,12},{5,9},{9,13},{6,10},{10,14},{7,11},{11,15},{20,24},{2... | collective-permute-start | bytes 786440 | tf_op jit(solution)/shard_map/ppermute | solution.py:534
  42.5 13.1 %collective-permute-start.16 = (bf16[256,512]{1,0:T(8,128)(2,1)S(1)}, bf16[256,512]{1,0:T(8,128)(2,1)S(1)}, u32[]{:S(2)}, u32[]{:S(2)}) collective-permute-start(bf16[256,512]{1,0:T(8,128)(2,1)S(1)} %combine.16.gate_ref), channel_id=1, source_target_pairs={{4,8},{8,12},{5,9},{9,13},{6,10},{10,14},{7,11},{11,15},{20,24},{2... | collective-permute-start | bytes 786440 | tf_op jit(solution)/shard_map/ppermute | solution.py:534
  48.2 13.8 %collective-permute-start.15 = (bf16[256,512]{1,0:T(8,128)(2,1)S(1)}, bf16[256,512]{1,0:T(8,128)(2,1)S(1)}, u32[]{:S(2)}, u32[]{:S(2)}) collective-permute-start(bf16[256,512]{1,0:T(8,128)(2,1)S(1)} %combine.17.refs_3_), channel_id=1, source_target_pairs={{4,8},{8,12},{5,9},{9,13},{6,10},{10,14},{7,11},{11,15},{20,24},{2... | collective-permute-start | bytes 786440 | tf_op jit(solution)/shard_map/ppermute | solution.py:534
  56.0 9.5 %collective-permute-start.18 = (bf16[256,512]{1,0:T(8,128)(2,1)S(1)}, bf16[256,512]{1,0:T(8,128)(2,1)S(1)}, u32[]{:S(2)}, u32[]{:S(2)}) collective-permute-start(bf16[256,512]{1,0:T(8,128)(2,1)S(1)} %combine.18.refs_3_), channel_id=1, source_target_pairs={{8,12},{9,13},{10,14},{11,15},{24,28},{25,29},{26,30},{27,31}} | collective-permute-start | bytes 786440 | tf_op jit(solution)/shard_map/ppermute | solution.py:534
  62.4 8.3 %collective-permute-start.17 = (bf16[256,512]{1,0:T(8,128)(2,1)S(1)}, bf16[256,512]{1,0:T(8,128)(2,1)S(1)}, u32[]{:S(2)}, u32[]{:S(2)}) collective-permute-start(bf16[256,512]{1,0:T(8,128)(2,1)S(1)} %combine.19.refs_3_), channel_id=1, source_target_pairs={{8,12},{9,13},{10,14},{11,15},{24,28},{25,29},{26,30},{27,31}} | collective-permute-start | bytes 786440 | tf_op jit(solution)/shard_map/ppermute | solution.py:534

commit v6 on v5

--- a/solution.py
+++ b/solution.py
@@ -398,7 +398,7 @@
     early, ready = lax.optimization_barrier((early, ready))
     early = lax.ppermute(early, "ctx", ahead)
     send(ready)
-    stages = [("z", 0), ("x", 1)] if last_piece > 0 else [("z", 0)]
+    stages = [("z", 0)]
     which, inputs, shapes, scratch = staged_of(stages)
     arrays = pl.pallas_call(
         functools.partial(stage_kernel, which),
@@ -411,7 +411,7 @@
         name="stage",
     )(ready, *inputs)
     keep(stages, arrays)
-    stages = [("z", 1)] if last_piece > 0 else []
+    stages = [("x", 1)] if last_piece > 0 else []
     which, inputs, shapes, scratch = staged_of(stages)
     left, b_turned, *arrays = pl.pallas_call(
         functools.partial(groups_kernel, groups, which),
@@ -509,9 +509,8 @@
     gate, out = b_turned, None
 
     def work(chunk):
-        stages = []
-        if len(pieces) < last_piece - 1:
-            stages = [("x", len(pieces) + 2), ("z", len(pieces) + 2)]
+        stages = [("z", len(pieces) + 1), ("x", len(pieces) + 2)]
+        stages = [(name, piece) for name, piece in stages if piece <= last_piece]
         pieces[chunk] = local(chunk, gate, stages)
         return pieces[chunk][3]
 

time: 73.1 us -> 73.2 us (level)
    pallas_call x8, Pallas kernels: 12 us -> 12.8 us  [local(): pl.pallas_call(functools.partial(local_kernel, group, chunk, which), in_s...]
  transfers between devices with their start and end apart: 19 -> 19, of which waited for: 9 -> 9; matrix products, arithmetic and copies ran while one was open for 0% -> 0% of each run, Pallas kernels for 28% -> 29%
where the time goes in v6:
time: 73.2 us; the launch traced here: 72.6 us
  waiting for transfers between devices  28.4 us (39%)
  Pallas kernels  24.5 us (33%)
  starting transfers between devices  18.8 us (26%)
    ppermute x10, waiting for transfers between devices, shards(): lax.ppermute(gate, 'ctx', [(owner, owner + 1) for owner in senders])  24.5 us
    pallas_call x8, Pallas kernels, local(): pl.pallas_call(functools.partial(local_kernel, group, chunk, which), in_s...  12.8 us
    ppermute x10, starting transfers between devices, shards(): lax.ppermute(gate, 'ctx', [(owner, owner + 1) for owner in senders])  11.9 us
    ppermute x8, starting transfers between devices, send(): from_first.append(lax.ppermute(value, 'ctx', [(0, 1)]))  5.64 us
    ppermute x1, waiting for transfers between devices, shards(): early = lax.ppermute(early, 'ctx', ahead)  3.91 us
    pallas_call x2, Pallas kernels, finish(): pl.pallas_call(functools.partial(finish_kernel, chunk // in_group, in_gro...  3.45 us
    pallas_call x6, Pallas kernels, absorb(): pl.pallas_call(functools.partial(absorb_kernel, chunk // in_group, chunk,...  2.2 us
    pallas_call x1, Pallas kernels, shards(): pl.pallas_call(steps_kernel, in_specs=[pl.BlockSpec(memory_space=pltpu.HB...  2 us
  transfers between devices with their start and end apart: 19, of which 9 were waited for; matrix products, arithmetic and copies ran while one was open for 0% of the time, Pallas kernels for 29%

profile of v6, /device:TPU:28, one launch (start us, length us, event | category | flops | bytes accessed | tf_op | source)
XLA Modules:
  0.0 72.6 jit_solution(17666325354053544306)
XLA Ops:
  0.0 2.0 %steps.1 = (bf16[384,1024]{1,0:T(8,128)(2,1)S(1)}, bf16[8,4096]{1,0:T(8,128)(2,1)S(1)}, f32[4,4096]{1,0:T(4,128)S(1)}, f32[4,2,512]{2,1,0:T(2,128)S(1)}, bf16[38...) custom-call(bf16[384,4096]{1,0:T(8,128)(2,1)} %refs_1_.3, ...), custom_call_target="tpu_custom_call" | custom-call | flops 1024 | bytes 1024 | tf_op jit(solution)/shard_map/steps/pallas_call | solution.py:331
  2.2 1.3 %collective-permute-start = (bf16[3,5120]{1,0:T(4,128)(2,1)S(1)}, bf16[3,5120]{1,0:T(4,128)(2,1)S(1)}, u32[]{:S(2)}, u32[]{:S(2)}) collective-permute-start(bf16[3,5120]{1,0:T(4,128)(2,1)S(1)} %pad_maximum_fusion), channel_id=1, source_target_pairs={{0,4},{4,8},{8,12},{1,5},{5,9},{9,13},{2,6},{6,10},{10,14},{3,7},{... | collective-permute-start | bytes 92168 | tf_op jit(solution)/shard_map/ppermute | solution.py:399
  4.2 3.9 %collective-permute-done.early_ref = bf16[3,5120]{1,0:T(4,128)(2,1)S(1)} collective-permute-done((bf16[3,5120]{1,0:T(4,128)(2,1)S(1)}, bf16[3,5120]{1,0:T(4,128)(2,1)S(1)}, u32[]{:S(2)}, u32[]{:S(2)}) %collective-permute-start) | collective-permute-done | bytes 30752 | tf_op jit(solution)/shard_map/ppermute | solution.py:399
  8.1 1.9 %groups.1 = (bf16[2,384,384]{2,1,0:T(8,128)(2,1)S(1)}, bf16[2,256,384]{2,1,0:T(8,128)(2,1)S(1)}, bf16[384,1024]{1,0:T(8,128)(2,1)S(1)}) custom-call(bf16[384,1024]{1,0:T(8,128)(2,1)S(1)} %bitcast.12, bf16[3,5120]{1,0:T(4,128)(2,1)S(1)} %collective-permute-done.early_ref, f32[4,2,512]{2,1,0:T(2,128)S(1)} %get-tuple-element.74.bc_taps_ref.taps_ref, ...), custom_call_target="tpu_custom_call" | custom-call | flops 1024 | bytes 1024 | tf_op jit(solution)/shard_map/groups/pallas_call | solution.py:416
  10.7 1.1 %stage.1.z_ref = bf16[384,1024]{1,0:T(8,128)(2,1)S(1)} custom-call(bf16[256,512]{1,0:T(8,128)(2,1)S(1)} %first.8.gate_ref, bf16[384,4096]{1,0:T(8,128)(2,1)} %refs_0_.9), custom_call_target="tpu_custom_call" | custom-call | flops 1024 | bytes 1024 | tf_op jit(solution)/shard_map/stage/pallas_call | solution.py:403
  11.9 1.5 %local.8 = (f32[384,512]{1,0:T(8,128)S(1)}, f32[384,512]{1,0:T(8,128)S(1)}, f32[256,512]{1,0:T(8,128)S(1)}, f32[8,512]{1,0:T(8,128)S(1)}, bf16[384,1024]{1,0:T(8,128)(2,1)S(1)}, /*index=5*/bf16[384,1024]{1,0:T(8,128)(2,1)S(1)}) custom-call(bf16[384,1024]{1,0:T(8,128)(2,1)S(1)} %get-tuple-element.70.x_ref, ...), custom_call_target="tpu_custom_call" | custom-call | flops 1024 | bytes 1024 | tf_op jit(solution)/shard_map/local/pallas_call | solution.py:434
  14.9 1.5 %local.9 = (f32[384,512]{1,0:T(8,128)S(1)}, f32[384,512]{1,0:T(8,128)S(1)}, f32[256,512]{1,0:T(8,128)S(1)}, f32[8,512]{1,0:T(8,128)S(1)}, bf16[384,1024]{1,0:T(8,128)(2,1)S(1)}, /*index=5*/bf16[384,1024]{1,0:T(8,128)(2,1)S(1)}) custom-call(bf16[384,1024]{1,0:T(8,128)(2,1)S(1)} %get-tuple-element.70.x_ref, ...), custom_call_target="tpu_custom_call" | custom-call | flops 1024 | bytes 1024 | tf_op jit(solution)/shard_map/local/pallas_call | solution.py:434
  17.2 0.9 %collective-permute-start.6 = (bf16[256,512]{1,0:T(8,128)(2,1)S(1)}, bf16[256,512]{1,0:T(8,128)(2,1)S(1)}, u32[]{:S(2)}, u32[]{:S(2)}) collective-permute-start(bf16[256,512]{1,0:T(8,128)(2,1)S(1)} %combine.11.gate_ref), channel_id=1, source_target_pairs={{4,8},{5,9},{6,10},{7,11},{20,24},{21,25},{22,26},{23,27}} | collective-permute-start | bytes 786440 | tf_op jit(solution)/shard_map/ppermute | solution.py:533
  18.0 2.3 %local.10 = (f32[384,512]{1,0:T(8,128)S(1)}, f32[384,512]{1,0:T(8,128)S(1)}, f32[256,512]{1,0:T(8,128)S(1)}, f32[8,512]{1,0:T(8,128)S(1)}, bf16[384,1024]{1,0:T(8,128)(2,1)S(1)}) custom-call(bf16[384,1024]{1,0:T(8,128)(2,1)S(1)} %get-tuple-element.83.x_ref, bf16[3,5120]{1,0:T(4,128)(2,1)S(1)} %collective-permute-done.early_ref, ...), custom_call_target="tpu_custom_call" | custom-call | flops 1024 | bytes 1024 | tf_op jit(solution)/shard_map/local/pallas_call | solution.py:434
  20.5 1.3 %collective-permute-start.8 = (bf16[256,512]{1,0:T(8,128)(2,1)S(1)}, bf16[256,512]{1,0:T(8,128)(2,1)S(1)}, u32[]{:S(2)}, u32[]{:S(2)}) collective-permute-start(bf16[256,512]{1,0:T(8,128)(2,1)S(1)} %combine.12.gate_ref), channel_id=1, source_target_pairs={{4,8},{8,12},{5,9},{9,13},{6,10},{10,14},{7,11},{11,15},{20,24},{2... | collective-permute-start | bytes 786440 | tf_op jit(solution)/shard_map/ppermute | solution.py:533
  22.5 1.5 %local.11 = (f32[384,512]{1,0:T(8,128)S(1)}, f32[384,512]{1,0:T(8,128)S(1)}, f32[256,512]{1,0:T(8,128)S(1)}, f32[8,512]{1,0:T(8,128)S(1)}) custom-call(bf16[384,1024]{1,0:T(8,128)(2,1)S(1)} %get-tuple-element.83.x_ref, bf16[3,5120]{1,0:T(4,128)(2,1)S(1)} %collective-permute-done.early_ref, f32[4,4096]{1,0:T(4,128)S(1)} %get-tuple-element.71.taps_ref, ...), custom_call_target="tpu_custom_call" | custom-call | flops 1024 | bytes 1024 | tf_op jit(solution)/shard_map/local/pallas_call | solution.py:434
  24.1 1.3 %collective-permute-start.10 = (bf16[256,512]{1,0:T(8,128)(2,1)S(1)}, bf16[256,512]{1,0:T(8,128)(2,1)S(1)}, u32[]{:S(2)}, u32[]{:S(2)}) collective-permute-start(bf16[256,512]{1,0:T(8,128)(2,1)S(1)} %combine.13.gate_ref), channel_id=1, source_target_pairs={{4,8},{8,12},{5,9},{9,13},{6,10},{10,14},{7,11},{11,15},{20,24},{2... | collective-permute-start | bytes 786440 | tf_op jit(solution)/shard_map/ppermute | solution.py:533
  26.1 1.5 %local.12 = (f32[384,512]{1,0:T(8,128)S(1)}, f32[384,512]{1,0:T(8,128)S(1)}, f32[256,512]{1,0:T(8,128)S(1)}, f32[8,512]{1,0:T(8,128)S(1)}) custom-call(bf16[384,1024]{1,0:T(8,128)(2,1)S(1)} %get-tuple-element.89.x_ref, bf16[3,5120]{1,0:T(4,128)(2,1)S(1)} %collective-permute-done.early_ref, f32[4,4096]{1,0:T(4,128)S(1)} %get-tuple-element.71.taps_ref, ...), custom_call_target="tpu_custom_call" | custom-call | flops 1024 | bytes 1024 | tf_op jit(solution)/shard_map/local/pallas_call | solution.py:434
  28.3 1.6 %collective-permute-done.8.refs_2_.refs_5_.refs_1_ = bf16[256,512]{1,0:T(8,128)(2,1)S(1)} collective-permute-done((bf16[256,512]{1,0:T(8,128)(2,1)S(1)}, bf16[256,512]{1,0:T(8,128)(2,1)S(1)}, u32[]{:S(2)}, u32[]{:S(2)}) %collective-permute-start.8) | collective-permute-done | bytes 262176 | tf_op jit(solution)/shard_map/ppermute | solution.py:533
  30.5 1.3 %collective-permute-start.12 = (bf16[256,512]{1,0:T(8,128)(2,1)S(1)}, bf16[256,512]{1,0:T(8,128)(2,1)S(1)}, u32[]{:S(2)}, u32[]{:S(2)}) collective-permute-start(bf16[256,512]{1,0:T(8,128)(2,1)S(1)} %combine.14.gate_ref), channel_id=1, source_target_pairs={{4,8},{8,12},{5,9},{9,13},{6,10},{10,14},{7,11},{11,15},{20,24},{2... | collective-permute-start | bytes 786440 | tf_op jit(solution)/shard_map/ppermute | solution.py:533
  31.8 1.5 %local.13 = (f32[384,512]{1,0:T(8,128)S(1)}, f32[384,512]{1,0:T(8,128)S(1)}, f32[256,512]{1,0:T(8,128)S(1)}, f32[8,512]{1,0:T(8,128)S(1)}) custom-call(bf16[384,1024]{1,0:T(8,128)(2,1)S(1)} %get-tuple-element.89.x_ref, bf16[3,5120]{1,0:T(4,128)(2,1)S(1)} %collective-permute-done.early_ref, f32[4,4096]{1,0:T(4,128)S(1)} %get-tuple-element.71.taps_ref, ...), custom_call_target="tpu_custom_call" | custom-call | flops 1024 | bytes 1024 | tf_op jit(solution)/shard_map/local/pallas_call | solution.py:434
  33.3 0.9 %collective-permute-start.13 = (bf16[256,512]{1,0:T(8,128)(2,1)S(1)}, bf16[256,512]{1,0:T(8,128)(2,1)S(1)}, u32[]{:S(2)}, u32[]{:S(2)}) collective-permute-start(bf16[256,512]{1,0:T(8,128)(2,1)S(1)} %first.15.refs_3_), channel_id=1, source_target_pairs={{0,4},{1,5},{2,6},{3,7},{16,20},{17,21},{18,22},{19,23}} | collective-permute-start | bytes 786440 | tf_op jit(solution)/shard_map/ppermute | solution.py:366
  34.2 1.3 %collective-permute-done.10.refs_2_.refs_5_.refs_1_ = bf16[256,512]{1,0:T(8,128)(2,1)S(1)} collective-permute-done((bf16[256,512]{1,0:T(8,128)(2,1)S(1)}, bf16[256,512]{1,0:T(8,128)(2,1)S(1)}, u32[]{:S(2)}, u32[]{:S(2)}) %collective-permute-start.10) | collective-permute-done | bytes 262176 | tf_op jit(solution)/shard_map/ppermute | solution.py:533
  36.0 1.3 %collective-permute-start.14 = (bf16[256,512]{1,0:T(8,128)(2,1)S(1)}, bf16[256,512]{1,0:T(8,128)(2,1)S(1)}, u32[]{:S(2)}, u32[]{:S(2)}) collective-permute-start(bf16[256,512]{1,0:T(8,128)(2,1)S(1)} %combine.15.gate_ref), channel_id=1, source_target_pairs={{4,8},{8,12},{5,9},{9,13},{6,10},{10,14},{7,11},{11,15},{20,24},{2... | collective-permute-start | bytes 786440 | tf_op jit(solution)/shard_map/ppermute | solution.py:533
  37.3 1.5 %local.14 = (f32[384,512]{1,0:T(8,128)S(1)}, f32[384,512]{1,0:T(8,128)S(1)}, f32[256,512]{1,0:T(8,128)S(1)}, f32[8,512]{1,0:T(8,128)S(1)}) custom-call(bf16[384,1024]{1,0:T(8,128)(2,1)S(1)} %get-tuple-element.84.x_ref, bf16[3,5120]{1,0:T(4,128)(2,1)S(1)} %collective-permute-done.early_ref, f32[4,4096]{1,0:T(4,128)S(1)} %get-tuple-element.71.taps_ref, ...), custom_call_target="tpu_custom_call" | custom-call | flops 1024 | bytes 1024 | tf_op jit(solution)/shard_map/local/pallas_call | solution.py:434
  38.8 2.7 %collective-permute-done.12.refs_2_.refs_5_.refs_1_ = bf16[256,512]{1,0:T(8,128)(2,1)S(1)} collective-permute-done((bf16[256,512]{1,0:T(8,128)(2,1)S(1)}, bf16[256,512]{1,0:T(8,128)(2,1)S(1)}, u32[]{:S(2)}, u32[]{:S(2)}) %collective-permute-start.12) | collective-permute-done | bytes 262176 | tf_op jit(solution)/shard_map/ppermute | solution.py:533
  42.0 1.3 %collective-permute-start.16 = (bf16[256,512]{1,0:T(8,128)(2,1)S(1)}, bf16[256,512]{1,0:T(8,128)(2,1)S(1)}, u32[]{:S(2)}, u32[]{:S(2)}) collective-permute-start(bf16[256,512]{1,0:T(8,128)(2,1)S(1)} %combine.16.gate_ref), channel_id=1, source_target_pairs={{4,8},{8,12},{5,9},{9,13},{6,10},{10,14},{7,11},{11,15},{20,24},{2... | collective-permute-start | bytes 786440 | tf_op jit(solution)/shard_map/ppermute | solution.py:533
  43.3 1.5 %local.15 = (f32[384,512]{1,0:T(8,128)S(1)}, f32[384,512]{1,0:T(8,128)S(1)}, f32[256,512]{1,0:T(8,128)S(1)}, f32[8,512]{1,0:T(8,128)S(1)}) custom-call(bf16[384,1024]{1,0:T(8,128)(2,1)S(1)} %get-tuple-element.84.x_ref, bf16[3,5120]{1,0:T(4,128)(2,1)S(1)} %collective-permute-done.early_ref, f32[4,4096]{1,0:T(4,128)S(1)} %get-tuple-element.71.taps_ref, ...), custom_call_target="tpu_custom_call" | custom-call | flops 1024 | bytes 1024 | tf_op jit(solution)/shard_map/local/pallas_call | solution.py:434
  44.8 2.6 %collective-permute-done.14.refs_5_.refs_1_.refs_2_ = bf16[256,512]{1,0:T(8,128)(2,1)S(1)} collective-permute-done((bf16[256,512]{1,0:T(8,128)(2,1)S(1)}, bf16[256,512]{1,0:T(8,128)(2,1)S(1)}, u32[]{:S(2)}, u32[]{:S(2)}) %collective-permute-start.14) | collective-permute-done | bytes 262176 | tf_op jit(solution)/shard_map/ppermute | solution.py:533
  47.5 1.3 %collective-permute-start.15 = (bf16[256,512]{1,0:T(8,128)(2,1)S(1)}, bf16[256,512]{1,0:T(8,128)(2,1)S(1)}, u32[]{:S(2)}, u32[]{:S(2)}) collective-permute-start(bf16[256,512]{1,0:T(8,128)(2,1)S(1)} %combine.17.refs_3_), channel_id=1, source_target_pairs={{4,8},{8,12},{5,9},{9,13},{6,10},{10,14},{7,11},{11,15},{20,24},{2... | collective-permute-start | bytes 786440 | tf_op jit(solution)/shard_map/ppermute | solution.py:533
  48.8 6.8 %collective-permute-done.16.refs_2_.refs_1_ = bf16[256,512]{1,0:T(8,128)(2,1)S(1)} collective-permute-done((bf16[256,512]{1,0:T(8,128)(2,1)S(1)}, bf16[256,512]{1,0:T(8,128)(2,1)S(1)}, u32[]{:S(2)}, u32[]{:S(2)}) %collective-permute-start.16) | collective-permute-done | bytes 262176 | tf_op jit(solution)/shard_map/ppermute | solution.py:533
  56.1 1.3 %collective-permute-start.18 = (bf16[256,512]{1,0:T(8,128)(2,1)S(1)}, bf16[256,512]{1,0:T(8,128)(2,1)S(1)}, u32[]{:S(2)}, u32[]{:S(2)}) collective-permute-start(bf16[256,512]{1,0:T(8,128)(2,1)S(1)} %combine.18.refs_3_), channel_id=1, source_target_pairs={{8,12},{9,13},{10,14},{11,15},{24,28},{25,29},{26,30},{27,31}} | collective-permute-start | bytes 786440 | tf_op jit(solution)/shard_map/ppermute | solution.py:533
  57.4 4.6 %collective-permute-done.15.refs_2_.refs_1_ = bf16[256,512]{1,0:T(8,128)(2,1)S(1)} collective-permute-done((bf16[256,512]{1,0:T(8,128)(2,1)S(1)}, bf16[256,512]{1,0:T(8,128)(2,1)S(1)}, u32[]{:S(2)}, u32[]{:S(2)}) %collective-permute-start.15) | collective-permute-done | bytes 262176 | tf_op jit(solution)/shard_map/ppermute | solution.py:533
  62.4 1.3 %collective-permute-start.17 = (bf16[256,512]{1,0:T(8,128)(2,1)S(1)}, bf16[256,512]{1,0:T(8,128)(2,1)S(1)}, u32[]{:S(2)}, u32[]{:S(2)}) collective-permute-start(bf16[256,512]{1,0:T(8,128)(2,1)S(1)} %combine.19.refs_3_), channel_id=1, source_target_pairs={{8,12},{9,13},{10,14},{11,15},{24,28},{25,29},{26,30},{27,31}} | collective-permute-start | bytes 786440 | tf_op jit(solution)/shard_map/ppermute | solution.py:533
  63.7 1.7 %finish.2.refs_10_ = bf16[384,4096]{1,0:T(8,128)(2,1)} custom-call(s32[1]{0:T(128)} %bitcast.place_ref, bf16[2,384,384]{2,1,0:T(8,128)(2,1)S(1)} %get-tuple-element.76.left_ref, f32[1,4096]{1,0:T(1,128)S(1)} %get-tuple-element.77.gain_ref, f32[384,512]{1,0:T(8,128)S(1)} %get-tuple-element.126.part_ref, f32[384,512]{1,0:T(8,128)S(1)} %get-tuple-element.127.reach_ref, ...), custom_call_target="tpu_custom_call" | custom-call | flops 1024 | bytes 1024 | tf_op jit(solution)/shard_map/finish/pallas_call | solution.py:493
  65.9 4.8 %collective-permute-done.17.refs_2_ = bf16[256,512]{1,0:T(8,128)(2,1)S(1)} collective-permute-done((bf16[256,512]{1,0:T(8,128)(2,1)S(1)}, bf16[256,512]{1,0:T(8,128)(2,1)S(1)}, u32[]{:S(2)}, u32[]{:S(2)}) %collective-permute-start.17) | collective-permute-done | bytes 262176 | tf_op jit(solution)/shard_map/ppermute | solution.py:533
  70.7 1.7 %finish.3 = bf16[384,4096]{1,0:T(8,128)(2,1)} custom-call(s32[1]{0:T(128)} %bitcast.place_ref, bf16[2,384,384]{2,1,0:T(8,128)(2,1)S(1)} %get-tuple-element.76.left_ref, f32[1,4096]{1,0:T(1,128)S(1)} %get-tuple-element.77.gain_ref, f32[384,512]{1,0:T(8,128)S(1)} %get-tuple-element.110.part_ref, ...), custom_call_target="tpu_custom_call", output_to_operand_aliasing={{}: (15, {})} | custom-call | flops 1024 | bytes 1024 | tf_op jit(solution)/shard_map/finish/pallas_call | solution.py:493
  (48 shorter events, 9.0 us)
Async XLA Ops:
  2.2 5.9 %collective-permute-start = (bf16[3,5120]{1,0:T(4,128)(2,1)S(1)}, bf16[3,5120]{1,0:T(4,128)(2,1)S(1)}, u32[]{:S(2)}, u32[]{:S(2)}) collective-permute-start(bf16[3,5120]{1,0:T(4,128)(2,1)S(1)} %pad_maximum_fusion), channel_id=1, source_target_pairs={{0,4},{4,8},{8,12},{1,5},{5,9},{9,13},{2,6},{6,10},{10,14},{3,7},{... | collective-permute-start | bytes 92168 | tf_op jit(solution)/shard_map/ppermute | solution.py:399
  3.5 10.6 %collective-permute-start.1 = (bf16[256,512]{1,0:T(8,128)(2,1)S(1)}, bf16[256,512]{1,0:T(8,128)(2,1)S(1)}, u32[]{:S(2)}, u32[]{:S(2)}) collective-permute-start(bf16[256,512]{1,0:T(8,128)(2,1)S(1)} %first.8.gate_ref), channel_id=1, source_target_pairs={{0,4},{1,5},{2,6},{3,7},{16,20},{17,21},{18,22},{19,23}} | collective-permute-start | bytes 786440 | tf_op jit(solution)/shard_map/ppermute | solution.py:366
  10.1 7.0 %collective-permute-start.2 = (bf16[256,512]{1,0:T(8,128)(2,1)S(1)}, bf16[256,512]{1,0:T(8,128)(2,1)S(1)}, u32[]{:S(2)}, u32[]{:S(2)}) collective-permute-start(bf16[256,512]{1,0:T(8,128)(2,1)S(1)} %first.9.gate_ref), channel_id=1, source_target_pairs={{0,4},{1,5},{2,6},{3,7},{16,20},{17,21},{18,22},{19,23}} | collective-permute-start | bytes 786440 | tf_op jit(solution)/shard_map/ppermute | solution.py:366
  13.4 6.9 %collective-permute-start.3 = (bf16[256,512]{1,0:T(8,128)(2,1)S(1)}, bf16[256,512]{1,0:T(8,128)(2,1)S(1)}, u32[]{:S(2)}, u32[]{:S(2)}) collective-permute-start(bf16[256,512]{1,0:T(8,128)(2,1)S(1)} %first.10.refs_3_), channel_id=1, source_target_pairs={{0,4},{1,5},{2,6},{3,7},{16,20},{17,21},{18,22},{19,23}} | collective-permute-start | bytes 786440 | tf_op jit(solution)/shard_map/ppermute | solution.py:366
  14.2 6.2 %collective-permute-start.4 = (bf16[256,512]{1,0:T(8,128)(2,1)S(1)}, bf16[256,512]{1,0:T(8,128)(2,1)S(1)}, u32[]{:S(2)}, u32[]{:S(2)}) collective-permute-start(bf16[256,512]{1,0:T(8,128)(2,1)S(1)} %combine.10.gate_ref), channel_id=1, source_target_pairs={{4,8},{5,9},{6,10},{7,11},{20,24},{21,25},{22,26},{23,27}} | collective-permute-start | bytes 786440 | tf_op jit(solution)/shard_map/ppermute | solution.py:533
  16.4 7.6 %collective-permute-start.5 = (bf16[256,512]{1,0:T(8,128)(2,1)S(1)}, bf16[256,512]{1,0:T(8,128)(2,1)S(1)}, u32[]{:S(2)}, u32[]{:S(2)}) collective-permute-start(bf16[256,512]{1,0:T(8,128)(2,1)S(1)} %first.11.refs_3_), channel_id=1, source_target_pairs={{0,4},{1,5},{2,6},{3,7},{16,20},{17,21},{18,22},{19,23}} | collective-permute-start | bytes 786440 | tf_op jit(solution)/shard_map/ppermute | solution.py:366
  17.2 6.8 %collective-permute-start.6 = (bf16[256,512]{1,0:T(8,128)(2,1)S(1)}, bf16[256,512]{1,0:T(8,128)(2,1)S(1)}, u32[]{:S(2)}, u32[]{:S(2)}) collective-permute-start(bf16[256,512]{1,0:T(8,128)(2,1)S(1)} %combine.11.gate_ref), channel_id=1, source_target_pairs={{4,8},{5,9},{6,10},{7,11},{20,24},{21,25},{22,26},{23,27}} | collective-permute-start | bytes 786440 | tf_op jit(solution)/shard_map/ppermute | solution.py:533
  20.5 9.4 %collective-permute-start.8 = (bf16[256,512]{1,0:T(8,128)(2,1)S(1)}, bf16[256,512]{1,0:T(8,128)(2,1)S(1)}, u32[]{:S(2)}, u32[]{:S(2)}) collective-permute-start(bf16[256,512]{1,0:T(8,128)(2,1)S(1)} %combine.12.gate_ref), channel_id=1, source_target_pairs={{4,8},{8,12},{5,9},{9,13},{6,10},{10,14},{7,11},{11,15},{20,24},{2... | collective-permute-start | bytes 786440 | tf_op jit(solution)/shard_map/ppermute | solution.py:533
  21.8 8.5 %collective-permute-start.7 = (bf16[256,512]{1,0:T(8,128)(2,1)S(1)}, bf16[256,512]{1,0:T(8,128)(2,1)S(1)}, u32[]{:S(2)}, u32[]{:S(2)}) collective-permute-start(bf16[256,512]{1,0:T(8,128)(2,1)S(1)} %first.12.refs_6_), channel_id=1, source_target_pairs={{0,4},{1,5},{2,6},{3,7},{16,20},{17,21},{18,22},{19,23}} | collective-permute-start | bytes 786440 | tf_op jit(solution)/shard_map/ppermute | solution.py:366
  24.1 11.3 %collective-permute-start.10 = (bf16[256,512]{1,0:T(8,128)(2,1)S(1)}, bf16[256,512]{1,0:T(8,128)(2,1)S(1)}, u32[]{:S(2)}, u32[]{:S(2)}) collective-permute-start(bf16[256,512]{1,0:T(8,128)(2,1)S(1)} %combine.13.gate_ref), channel_id=1, source_target_pairs={{4,8},{8,12},{5,9},{9,13},{6,10},{10,14},{7,11},{11,15},{20,24},{2... | collective-permute-start | bytes 786440 | tf_op jit(solution)/shard_map/ppermute | solution.py:533
  25.4 10.4 %collective-permute-start.9 = (bf16[256,512]{1,0:T(8,128)(2,1)S(1)}, bf16[256,512]{1,0:T(8,128)(2,1)S(1)}, u32[]{:S(2)}, u32[]{:S(2)}) collective-permute-start(bf16[256,512]{1,0:T(8,128)(2,1)S(1)} %first.13.refs_6_), channel_id=1, source_target_pairs={{0,4},{1,5},{2,6},{3,7},{16,20},{17,21},{18,22},{19,23}} | collective-permute-start | bytes 786440 | tf_op jit(solution)/shard_map/ppermute | solution.py:366
  27.6 14.2 %collective-permute-start.11 = (bf16[256,512]{1,0:T(8,128)(2,1)S(1)}, bf16[256,512]{1,0:T(8,128)(2,1)S(1)}, u32[]{:S(2)}, u32[]{:S(2)}) collective-permute-start(bf16[256,512]{1,0:T(8,128)(2,1)S(1)} %first.14.refs_3_), channel_id=1, source_target_pairs={{0,4},{1,5},{2,6},{3,7},{16,20},{17,21},{18,22},{19,23}} | collective-permute-start | bytes 786440 | tf_op jit(solution)/shard_map/ppermute | solution.py:366
  30.5 11.0 %collective-permute-start.12 = (bf16[256,512]{1,0:T(8,128)(2,1)S(1)}, bf16[256,512]{1,0:T(8,128)(2,1)S(1)}, u32[]{:S(2)}, u32[]{:S(2)}) collective-permute-start(bf16[256,512]{1,0:T(8,128)(2,1)S(1)} %combine.14.gate_ref), channel_id=1, source_target_pairs={{4,8},{8,12},{5,9},{9,13},{6,10},{10,14},{7,11},{11,15},{20,24},{2... | collective-permute-start | bytes 786440 | tf_op jit(solution)/shard_map/ppermute | solution.py:533
  33.3 11.5 %collective-permute-start.13 = (bf16[256,512]{1,0:T(8,128)(2,1)S(1)}, bf16[256,512]{1,0:T(8,128)(2,1)S(1)}, u32[]{:S(2)}, u32[]{:S(2)}) collective-permute-start(bf16[256,512]{1,0:T(8,128)(2,1)S(1)} %first.15.refs_3_), channel_id=1, source_target_pairs={{0,4},{1,5},{2,6},{3,7},{16,20},{17,21},{18,22},{19,23}} | collective-permute-start | bytes 786440 | tf_op jit(solution)/shard_map/ppermute | solution.py:366
  36.0 11.4 %collective-permute-start.14 = (bf16[256,512]{1,0:T(8,128)(2,1)S(1)}, bf16[256,512]{1,0:T(8,128)(2,1)S(1)}, u32[]{:S(2)}, u32[]{:S(2)}) collective-permute-start(bf16[256,512]{1,0:T(8,128)(2,1)S(1)} %combine.15.gate_ref), channel_id=1, source_target_pairs={{4,8},{8,12},{5,9},{9,13},{6,10},{10,14},{7,11},{11,15},{20,24},{2... | collective-permute-start | bytes 786440 | tf_op jit(solution)/shard_map/ppermute | solution.py:533
  42.0 13.7 %collective-permute-start.16 = (bf16[256,512]{1,0:T(8,128)(2,1)S(1)}, bf16[256,512]{1,0:T(8,128)(2,1)S(1)}, u32[]{:S(2)}, u32[]{:S(2)}) collective-permute-start(bf16[256,512]{1,0:T(8,128)(2,1)S(1)} %combine.16.gate_ref), channel_id=1, source_target_pairs={{4,8},{8,12},{5,9},{9,13},{6,10},{10,14},{7,11},{11,15},{20,24},{2... | collective-permute-start | bytes 786440 | tf_op jit(solution)/shard_map/ppermute | solution.py:533
  47.5 14.5 %collective-permute-start.15 = (bf16[256,512]{1,0:T(8,128)(2,1)S(1)}, bf16[256,512]{1,0:T(8,128)(2,1)S(1)}, u32[]{:S(2)}, u32[]{:S(2)}) collective-permute-start(bf16[256,512]{1,0:T(8,128)(2,1)S(1)} %combine.17.refs_3_), channel_id=1, source_target_pairs={{4,8},{8,12},{5,9},{9,13},{6,10},{10,14},{7,11},{11,15},{20,24},{2... | collective-permute-start | bytes 786440 | tf_op jit(solution)/shard_map/ppermute | solution.py:533
  56.1 9.5 %collective-permute-start.18 = (bf16[256,512]{1,0:T(8,128)(2,1)S(1)}, bf16[256,512]{1,0:T(8,128)(2,1)S(1)}, u32[]{:S(2)}, u32[]{:S(2)}) collective-permute-start(bf16[256,512]{1,0:T(8,128)(2,1)S(1)} %combine.18.refs_3_), channel_id=1, source_target_pairs={{8,12},{9,13},{10,14},{11,15},{24,28},{25,29},{26,30},{27,31}} | collective-permute-start | bytes 786440 | tf_op jit(solution)/shard_map/ppermute | solution.py:533
  62.4 8.3 %collective-permute-start.17 = (bf16[256,512]{1,0:T(8,128)(2,1)S(1)}, bf16[256,512]{1,0:T(8,128)(2,1)S(1)}, u32[]{:S(2)}, u32[]{:S(2)}) collective-permute-start(bf16[256,512]{1,0:T(8,128)(2,1)S(1)} %combine.19.refs_3_), channel_id=1, source_target_pairs={{8,12},{9,13},{10,14},{11,15},{24,28},{25,29},{26,30},{27,31}} | collective-permute-start | bytes 786440 | tf_op jit(solution)/shard_map/ppermute | solution.py:533
